TPU v7x, 32 devices: a whole 2x2x4 slice. The times are simulated.
32 devices in a mesh: seq: 8 (over y, x, core), wa: 4 (over z).
Axes of the slice: x: 2, y: 2, z: 4, core: 2. Of those that a mesh axis runs over, the one named last changes fastest.
Arguments:
- tokens: bfloat16 [8, 2048, 1792], P(None, ('seq', 'wa')), may hold values from -6 to 6
- cotangent: bfloat16 [8, 2048, 1792], P(None, ('seq', 'wa')), may hold values from -6 to 6
- lengths: int32 [8], replicated, may hold values from 1 to 2048, 10240 in all
- adapter_ids: int32 [8], replicated, may hold values from 0 to 7
- gain_first: float32 [1792], replicated, may hold values from 0.5 to 1.5
- gain_second: float32 [1792], replicated, may hold values from 0.5 to 1.5
- conv_kernel: bfloat16 [3, 1792], replicated, may hold values from -0.625 to 0.625
- mixer_in: bfloat16 [1792, 4096], P(None, 'wa'), may hold values from -0.125 to 0.125
- mixer_out: bfloat16 [1792, 1792], P('wa'), may hold values from -3 to 3
- gate_up: bfloat16 [2, 1792, 4864], P(None, None, 'wa'), may hold values from -0.125 to 0.125
- down_weight: bfloat16 [4864, 1792], P('wa'), may hold values from -0.078125 to 0.078125
- inward_down: bfloat16 [8, 16, 1792], replicated, may hold values from -0.125 to 0.125
- inward_up: bfloat16 [8, 16, 4096], P(None, None, 'wa'), may hold values from -1.5 to 1.5
- outward_down: bfloat16 [8, 16, 1792], P(None, None, 'wa'), may hold values from -3 to 3
- outward_up: bfloat16 [8, 16, 1792], replicated, may hold values from -1.5 to 1.5
- expand_down: bfloat16 [8, 16, 1792], replicated, may hold values from -0.125 to 0.125
- expand_up: bfloat16 [8, 16, 2, 4864], P(None, None, None, 'wa'), may hold values from -1.5 to 1.5
- reduce_down: bfloat16 [8, 16, 4864], P(None, None, 'wa'), may hold values from -0.078125 to 0.078125
- reduce_up: bfloat16 [8, 16, 1792], replicated, may hold values from -1.5 to 1.5
Outputs:
- output: float32 [8, 2048, 1792], P(None, ('seq', 'wa'))
- input_grad: float32 [8, 2048, 1792], P(None, ('seq', 'wa'))
- grad_inward_down: float32 [8, 16, 1792], P(None, None, 'wa')
- grad_inward_up: float32 [8, 16, 4096], P(None, None, 'wa')
- grad_outward_down: float32 [8, 16, 1792], P(None, None, 'wa')
- grad_outward_up: float32 [8, 16, 1792], P(None, None, 'wa')
- grad_expand_down: float32 [8, 16, 1792], P(None, None, 'wa')
- grad_expand_up: float32 [8, 16, 2, 4864], P(None, None, None, 'wa')
- grad_reduce_down: float32 [8, 16, 4864], P(None, None, 'wa')
- grad_reduce_up: float32 [8, 16, 1792], P(None, None, 'wa')
Inputs may be any that keep to these rules, and one draw needn't show every extreme that they name: Sequence s holds lengths[s] valid tokens from its start; together the lengths fill 5 * 2048 slots, and one sequence fills all 2048.
All inputs are finite; a program needn't handle non-finite values.
Results may differ from a plain program's by a relative error of at most 0.023.
Values may be sent and summed in bfloat16 or wider, within the bound.
No kernel may reach another device: no remote copies, remote signals or barrier semaphores. Data moves between devices by JAX's collectives and lax.ppermute only.
A program may use at most 256 MiB of HBM per device.

v0:
```python
import math

import jax
import jax.numpy as jnp
from jax import lax
from jax.sharding import PartitionSpec as P

HEADS = 16
HEAD = 112
FEAT = 16
ADAPT = 8
PACK = 256


EPSILON = 1e-05
HIGHEST = lax.Precision.HIGHEST


def rms_norm(values, scale_gain):
    return (
        values * lax.rsqrt(jnp.mean(values * values, axis=-1, keepdims=True) + EPSILON) * scale_gain
    )


def rms_back(values, scale_gain, upstream):
    _, pull = jax.vjp(lambda inner_values: rms_norm(inner_values, scale_gain), values)
    return pull(upstream)[0]


def project(operand_one, operand_two, pattern):
    return jnp.einsum(pattern, operand_one, operand_two, preferred_element_type=jnp.float32)


def precise(operand_one, operand_two, pattern):
    return jnp.einsum(pattern, operand_one, operand_two, precision=HIGHEST)


def feature_map(values):
    row_count = values.shape[0]
    products = (values[:, :, None] * values[:, None, :]).reshape(row_count, -1) * (
        1.0 / math.sqrt(2.0)
    )
    return jnp.concatenate([jnp.ones((row_count, 1), jnp.float32), values, products], axis=1)


def taylor_head(query_part, key_part, value_part, keep_mask):
    length = query_part.shape[0]
    block_rows = math.gcd(512, length)
    block_count = length // block_rows
    causal = jnp.tril(jnp.ones((block_rows, block_rows), jnp.float32))
    feature_width = 1 + query_part.shape[1] + query_part.shape[1] * query_part.shape[1]

    def advance(running, pieces):
        memory, normalizer = running
        query_block, key_block, value_block, keep_block = pieces
        scores = jnp.dot(query_block, key_block.T, precision=HIGHEST)
        weight = (1.0 + scores + 0.5 * scores * scores) * causal * keep_block[None, :]
        query_feat = feature_map(query_block)
        key_feat = feature_map(key_block) * keep_block[:, None]
        numerator = jnp.dot(weight, value_block, precision=HIGHEST) + jnp.dot(
            query_feat, memory, precision=HIGHEST
        )
        denominator = jnp.sum(weight, axis=1) + jnp.dot(query_feat, normalizer, precision=HIGHEST)
        memory = memory + jnp.dot(key_feat.T, value_block, precision=HIGHEST)
        normalizer = normalizer + jnp.sum(key_feat, axis=0)
        return ((memory, normalizer), numerator / denominator[:, None])

    pieces = (
        0.5 * query_part.reshape(block_count, block_rows, -1),
        0.5 * key_part.reshape(block_count, block_rows, -1),
        value_part.reshape(block_count, block_rows, -1),
        keep_mask.reshape(block_count, block_rows),
    )
    start = (
        jnp.zeros((feature_width, value_part.shape[1]), jnp.float32),
        jnp.zeros((feature_width,), jnp.float32),
    )
    _, result = lax.scan(jax.checkpoint(advance), start, pieces)
    return result.reshape(length, -1)


def mixer_head(packed, kernel, keep_mask):
    query_part = packed[:, :FEAT]
    key_part = packed[:, FEAT : 2 * FEAT]
    value_part = packed[:, 2 * FEAT : 2 * FEAT + HEAD]
    gate_part = packed[:, 2 * FEAT + HEAD :]
    attended = taylor_head(query_part, key_part, value_part, keep_mask)
    shifted_one = jnp.pad(value_part, ((1, 0), (0, 0)))[:-1]
    shifted_two = jnp.pad(value_part, ((2, 0), (0, 0)))[:-2]
    convolved = kernel[0] * value_part + kernel[1] * shifted_one + kernel[2] * shifted_two
    return attended + convolved * jax.nn.silu(gate_part)


def on_device(
    tokens,
    cotangent,
    lengths,
    adapter_ids,
    gain_first,
    gain_second,
    conv_kernel,
    mixer_in,
    mixer_out,
    gate_up,
    down_weight,
    inward_down,
    inward_up,
    outward_down,
    outward_up,
    expand_down,
    expand_up,
    reduce_down,
    reduce_up,
):
    sequences, slot_rows, model_width = tokens.shape
    shard_ways = lax.axis_size("wa")
    seq_place = lax.axis_index("seq")
    shard_place = lax.axis_index("wa")
    rank_width = inward_down.shape[1]
    positions = (seq_place * shard_ways + shard_place) * slot_rows + jnp.arange(
        slot_rows, dtype=jnp.int32
    )
    keep_mask = (positions[None, :] < lengths[:, None]).astype(jnp.float32)
    adapter_hot = (adapter_ids[:, None] == jnp.arange(ADAPT, dtype=jnp.int32)[None, :]).astype(
        jnp.float32
    )

    def choose_table(table):
        return jnp.tensordot(adapter_hot, table.astype(jnp.float32), axes=1, precision=HIGHEST)

    def spread(part):
        return jnp.tensordot(adapter_hot.T, part, axes=1, precision=HIGHEST)

    inward_first = choose_table(inward_down)
    outward_second = choose_table(outward_up).astype(jnp.bfloat16)
    expand_first = choose_table(expand_down)
    reduce_second = choose_table(reduce_up).astype(jnp.bfloat16)
    inputs = tokens.astype(jnp.float32)
    normed = rms_norm(inputs, gain_first).astype(jnp.bfloat16)
    enter_rank = project(normed, inward_first.astype(jnp.bfloat16), "std,srd->str").astype(
        jnp.bfloat16
    )
    used_in, used_inward, used_out, used_outward = (mixer_in, inward_up, mixer_out, outward_down)
    normed_all, enter_all = (
        lax.all_gather(normed, "wa", axis=1, tiled=True),
        lax.all_gather(enter_rank, "wa", axis=1, tiled=True),
    )
    heads_here = mixer_in.shape[1] // PACK
    head_offset = shard_place * heads_here
    rows_here = normed_all.shape[1]
    inward_second = choose_table(used_inward).astype(jnp.bfloat16)
    outward_first = choose_table(used_outward).astype(jnp.bfloat16)
    enter_weights = used_in.reshape(model_width, heads_here, PACK)
    enter_adapt = inward_second.reshape(sequences, rank_width, heads_here, PACK)
    packed = (
        project(normed_all, enter_weights, "std,dhc->shtc")
        + project(enter_all, enter_adapt, "str,srhc->shtc")
    ).astype(jnp.bfloat16)
    packed_items = packed.reshape(sequences * heads_here, rows_here, PACK)
    head_items = lax.all_to_all(packed_items, "seq", split_axis=0, concat_axis=1, tiled=True)
    item_count = head_items.shape[0]
    seq_slots = head_items.shape[1]
    item_index = seq_place * item_count + jnp.arange(item_count, dtype=jnp.int32)
    item_sequence = item_index // heads_here
    item_head = head_offset + item_index % heads_here
    sequence_match = item_sequence[:, None] == jnp.arange(sequences, dtype=jnp.int32)[None, :]
    item_length = jnp.sum(jnp.where(sequence_match, lengths[None, :], 0), axis=1)
    item_keep = (jnp.arange(seq_slots, dtype=jnp.int32)[None, :] < item_length[:, None]).astype(
        jnp.float32
    )
    head_match = (item_head[:, None] == jnp.arange(HEADS, dtype=jnp.int32)[None, :]).astype(
        jnp.float32
    )
    item_kernel = jnp.einsum(
        "ih,khc->ikc",
        head_match,
        conv_kernel.astype(jnp.float32).reshape(3, HEADS, HEAD),
        precision=HIGHEST,
    )

    def run_mixer(item_values):
        return jax.vmap(mixer_head)(item_values, item_kernel, item_keep)

    mixed_items, mixer_pull = jax.vjp(run_mixer, head_items.astype(jnp.float32))
    mixed_back = lax.all_to_all(
        mixed_items.astype(jnp.bfloat16), "seq", split_axis=1, concat_axis=0, tiled=True
    )
    mixed_back = mixed_back.reshape(sequences, heads_here, rows_here, HEAD)
    leave_weights = used_out.reshape(heads_here, HEAD, model_width)
    leave_adapt = outward_first.reshape(sequences, rank_width, heads_here, HEAD)
    branch_part = project(mixed_back, leave_weights, "shtc,hcd->std")
    leave_part = project(mixed_back, leave_adapt, "shtc,srhc->str")
    branch_main, leave_sum = (
        lax.psum_scatter(branch_part, "wa", scatter_dimension=1, tiled=True),
        lax.psum_scatter(leave_part, "wa", scatter_dimension=1, tiled=True),
    )
    leave_rank = leave_sum.astype(jnp.bfloat16)
    residual = inputs + branch_main + project(leave_rank, outward_second, "str,srd->std")
    normed_two = rms_norm(residual, gain_second).astype(jnp.bfloat16)
    expand_rank = project(normed_two, expand_first.astype(jnp.bfloat16), "std,srd->str").astype(
        jnp.bfloat16
    )
    ffn_normed, ffn_rank = (
        lax.all_gather(normed_two, "wa", axis=1, tiled=True),
        lax.all_gather(expand_rank, "wa", axis=1, tiled=True),
    )
    ffn_expand = choose_table(expand_up).astype(jnp.bfloat16)
    ffn_reduce = choose_table(reduce_down).astype(jnp.bfloat16)
    gate_up_out = project(ffn_normed, gate_up, "std,gdf->gstf") + project(
        ffn_rank, ffn_expand, "str,srgf->gstf"
    )
    gating = gate_up_out[0]
    upward = gate_up_out[1]
    hidden = (jax.nn.silu(gating) * upward).astype(jnp.bfloat16)
    feed_part = project(hidden, down_weight, "stf,fd->std")
    reduce_part = project(hidden, ffn_reduce, "stf,srf->str")
    feed_main, reduce_sum = (
        lax.psum_scatter(
            feed_part.astype(jnp.bfloat16), "wa", scatter_dimension=1, tiled=True
        ).astype(jnp.float32),
        lax.psum_scatter(
            reduce_part.astype(jnp.bfloat16), "wa", scatter_dimension=1, tiled=True
        ).astype(jnp.float32),
    )
    reduce_rank = reduce_sum.astype(jnp.bfloat16)
    feed_out = feed_main + project(reduce_rank, reduce_second, "str,srd->std")
    output = keep_mask[:, :, None] * (residual + feed_out)
    top_grad = keep_mask[:, :, None] * cotangent.astype(jnp.float32)
    top_low = top_grad.astype(jnp.bfloat16)
    reduce_grad = project(top_low, reduce_second, "std,srd->str").astype(jnp.bfloat16)
    reduce_up_part = project(reduce_rank, top_low, "str,std->srd")
    top_all, reduce_grad_all = (
        lax.all_gather(top_low, "wa", axis=1, tiled=True),
        lax.all_gather(reduce_grad, "wa", axis=1, tiled=True),
    )
    hidden_grad = project(top_all, down_weight, "std,fd->stf") + project(
        reduce_grad_all, ffn_reduce, "str,srf->stf"
    )
    reduce_down_part = project(reduce_grad_all, hidden, "str,stf->srf")
    _, silu_pull = jax.vjp(
        lambda gate_value, up_value: jax.nn.silu(gate_value) * up_value, gating, upward
    )
    gate_grad, up_grad = silu_pull(hidden_grad)
    gate_up_grad = jnp.stack([gate_grad, up_grad]).astype(jnp.bfloat16)
    expand_up_part = project(ffn_rank, gate_up_grad, "str,gstf->srgf")
    expand_grad = project(gate_up_grad, ffn_expand, "gstf,srgf->str")
    normed_two_part = project(gate_up_grad, gate_up, "gstf,gdf->std") + precise(
        expand_grad, expand_first, "str,srd->std"
    )
    expand_down_part = precise(expand_grad, ffn_normed.astype(jnp.float32), "str,std->srd")
    normed_two_grad = lax.psum_scatter(
        normed_two_part.astype(jnp.bfloat16), "wa", scatter_dimension=1, tiled=True
    ).astype(jnp.float32)
    expand_up_total = spread(expand_up_part)
    reduce_down_total = spread(reduce_down_part)
    residual_grad = top_grad + rms_back(residual, gain_second, normed_two_grad)
    branch_grad = residual_grad.astype(jnp.bfloat16)
    leave_grad = project(branch_grad, outward_second, "std,srd->str").astype(jnp.bfloat16)
    outward_up_part = project(leave_rank, branch_grad, "str,std->srd")
    branch_all, leave_all = (
        lax.all_gather(branch_grad, "wa", axis=1, tiled=True),
        lax.all_gather(leave_grad, "wa", axis=1, tiled=True),
    )
    mixed_grad = (
        project(branch_all, leave_weights, "std,hcd->shtc")
        + project(leave_all, leave_adapt, "str,srhc->shtc")
    ).astype(jnp.bfloat16)
    outward_down_part = project(leave_all, mixed_back, "str,shtc->srhc").reshape(
        sequences, rank_width, heads_here * HEAD
    )
    grad_items = mixed_grad.reshape(sequences * heads_here, rows_here, HEAD)
    items_grad = lax.all_to_all(grad_items, "seq", split_axis=0, concat_axis=1, tiled=True)
    packed_grad = mixer_pull(items_grad.astype(jnp.float32))[0].astype(jnp.bfloat16)
    packed_back = lax.all_to_all(packed_grad, "seq", split_axis=1, concat_axis=0, tiled=True)
    packed_back = packed_back.reshape(sequences, heads_here, rows_here, PACK)
    enter_grad = project(packed_back, enter_adapt, "shtc,srhc->str")
    normed_part = project(packed_back, enter_weights, "shtc,dhc->std") + precise(
        enter_grad, inward_first, "str,srd->std"
    )
    inward_up_part = project(enter_all, packed_back, "str,shtc->srhc").reshape(
        sequences, rank_width, heads_here * PACK
    )
    inward_down_part = precise(enter_grad, normed_all.astype(jnp.float32), "str,std->srd")
    shared = jnp.stack(
        [
            spread(inward_down_part),
            spread(outward_up_part),
            spread(expand_down_part),
            spread(reduce_up_part),
        ]
    )
    normed_grad, shared_sum = (
        lax.psum_scatter(
            normed_part.astype(jnp.bfloat16), "wa", scatter_dimension=1, tiled=True
        ).astype(jnp.float32),
        lax.psum_scatter(shared.astype(jnp.bfloat16), "wa", scatter_dimension=3, tiled=True).astype(
            jnp.float32
        ),
    )
    inward_up_wa = spread(inward_up_part)
    outward_down_wa = spread(outward_down_part)
    input_grad = residual_grad + rms_back(inputs, gain_first, normed_grad)
    shared_total, inward_up_total, outward_down_total, expand_up_final, reduce_down_final = (
        lax.psum(shared_sum.astype(jnp.bfloat16), "seq").astype(jnp.float32),
        lax.psum(inward_up_wa.astype(jnp.bfloat16), "seq").astype(jnp.float32),
        lax.psum(outward_down_wa.astype(jnp.bfloat16), "seq").astype(jnp.float32),
        lax.psum(expand_up_total.astype(jnp.bfloat16), "seq").astype(jnp.float32),
        lax.psum(reduce_down_total.astype(jnp.bfloat16), "seq").astype(jnp.float32),
    )
    return (
        output,
        input_grad,
        shared_total[0],
        inward_up_total,
        outward_down_total,
        shared_total[1],
        shared_total[2],
        expand_up_final,
        reduce_down_final,
        shared_total[3],
    )


def solution(mesh):
    in_specs = (
        P(None, ("seq", "wa"), None),
        P(None, ("seq", "wa"), None),
        P(),
        P(),
        P(),
        P(),
        P(),
        P(None, "wa"),
        P("wa", None),
        P(None, None, "wa"),
        P("wa", None),
        P(),
        P(None, None, "wa"),
        P(None, None, "wa"),
        P(),
        P(),
        P(None, None, None, "wa"),
        P(None, None, "wa"),
        P(),
    )
    out_specs = (
        P(None, ("seq", "wa"), None),
        P(None, ("seq", "wa"), None),
        P(None, None, "wa"),
        P(None, None, "wa"),
        P(None, None, "wa"),
        P(None, None, "wa"),
        P(None, None, "wa"),
        P(None, None, None, "wa"),
        P(None, None, "wa"),
        P(None, None, "wa"),
    )
    return jax.shard_map(
        on_device, mesh=mesh, in_specs=in_specs, out_specs=out_specs, check_vma=False
    )
```

profile of v0, /device:TPU:0, one launch (start us, length us, event | category | flops | bytes accessed | tf_op | source)
XLA Modules:
  0.0 2172.8 jit_solution(16175263467071365012)
XLA Ops:
  16.9 22.5 %all_gather.25 = bf16[8,256,16]{2,0,1:T(8,128)(2,1)S(1)} all-gather(bf16[8,64,16]{2,0,1:T(8,128)(2,1)S(1)} %copy.463), channel_id=1, replica_groups=mesh['seq'=8,'wa'=4] {'wa'}, dimensions={1}, use_global_device_ids=true | all-gather | bytes 81920 | tf_op jit(solution)/shard_map/all_gather | solution.py:146
  41.0 111.1 %all-gather.5.cloned.1.call-done = bf16[8,256,1792]{2,1,0:T(8,128)(2,1)} async-done(((bf16[8,64,1792]{2,1,0:T(8,128)(2,1)}), bf16[8,256,1792]{2,1,0:T(8,128)(2,1)}) %all-gather.5.cloned.1.call-update) | async-done | bytes 7340048 | tf_op jit(solution)/shard_map/all_gather | solution.py:145
  173.1 47.9 %all-to-all-done = bf16[32,256,256]{2,1,0:T(8,128)(2,1)} async-done(((bf16[32,256,256]{2,1,0:T(8,128)(2,1)}), bf16[32,256,256]{2,1,0:T(8,128)(2,1)}, u32[]{:S(2)}, u32[]{:S(2)}) %all-to-all-start) | async-done | bytes 4194336 | tf_op jit(solution)/shard_map/all_to_all | solution.py:160
  259.2 78.9 %while.42 = (s32[]{:T(128)}, f32[4,273,112]{2,1,0:T(8,128)S(1)}, f32[4,273]{1,0:T(4,128)S(1)}, f32[4,4,512,112]{2,3,1,0:T(8,128)}, f32[4,4,273,112]{3,2,1,0:T(8,...) while((s32[]{:T(128)}, f32[4,273,112]{2,1,0:T(8,128)S(1)}, ...), condition=%wide.region_5.6_spmd.clone, body=%wide.region_2.5_spmd.clone.sunk | while | flops 3143546880 | bytes 64492664 | solution.py:78
  343.6 11.1 fusion.111
  370.9 25.5 %all-to-all-done.1 = bf16[4,2048,112]{2,0,1:T(4,128)(2,1)} async-done(((bf16[4,2048,112]{2,0,1:T(4,128)(2,1)}), bf16[4,2048,112]{2,0,1:T(4,128)(2,1)}, u32[]{:S(2)}, u32[]{:S(2)}) %all-to-all-start.1) | async-done | bytes 1835040 | tf_op jit(solution)/shard_map/all_to_all | solution.py:185
  425.5 243.7 %reduce-scatter.14.cloned.1.call-done = f32[8,64,1792]{2,1,0:T(8,128)} async-done(((f32[8,256,1792]{2,1,0:T(8,128)}), f32[8,64,1792]{2,1,0:T(8,128)}) %reduce-scatter.14.cloned.1.call-update) | async-done | bytes 3670032 | tf_op jit(solution)/shard_map/reduce_scatter | solution.py:194
  678.7 25.3 %all_gather.29 = bf16[8,256,16]{2,0,1:T(8,128)(2,1)S(1)} all-gather(bf16[8,64,16]{2,0,1:T(8,128)(2,1)S(1)} %copy.501), channel_id=1, replica_groups=mesh['seq'=8,'wa'=4] {'wa'}, dimensions={1}, use_global_device_ids=true | all-gather | bytes 81920 | tf_op jit(solution)/shard_map/all_gather | solution.py:234
  710.2 101.0 %all-gather.9.cloned.1.call-done = bf16[8,256,1792]{2,1,0:T(8,128)(2,1)} async-done(((bf16[8,64,1792]{2,1,0:T(8,128)(2,1)}), bf16[8,256,1792]{2,1,0:T(8,128)(2,1)}) %all-gather.9.cloned.1.call-update) | async-done | bytes 7340048 | tf_op jit(solution)/shard_map/all_gather | solution.py:233
  811.2 15.1 fusion.99
  828.5 25.5 %all_gather.27 = bf16[8,256,16]{2,0,1:T(8,128)(2,1)S(1)} all-gather(bf16[8,64,16]{2,0,1:T(8,128)(2,1)S(1)} %copy.490), channel_id=1, replica_groups=mesh['seq'=8,'wa'=4] {'wa'}, dimensions={1}, use_global_device_ids=true | all-gather | bytes 81920 | tf_op jit(solution)/shard_map/all_gather | solution.py:205
  854.2 98.6 %all-gather.7.cloned.1.call-done = bf16[8,256,1792]{2,1,0:T(8,128)(2,1)} async-done(((bf16[8,64,1792]{2,1,0:T(8,128)(2,1)}), bf16[8,256,1792]{2,1,0:T(8,128)(2,1)}) %all-gather.7.cloned.1.call-update) | async-done | bytes 7340048 | tf_op jit(solution)/shard_map/all_gather | solution.py:204
  952.9 24.8 %fusion.89 = f32[8,256,2,1216]{1,3,2,0:T(8,128)} fusion(bf16[2,1792,1216]{1,2,0:T(8,128)(2,1)} %param.32, bf16[8,256,1792]{2,1,0:T(8,128)(2,1)} %all-gather.7.cloned.1.call-done), kind=kOutput, calls=%fused_computation.145 | convolution fusion | flops 17850957824 | bytes 35979264 | tf_op jit(solution)/shard_map/std,gdf->gstf/dot_general | solution.py:31
  977.7 12.7 bitcast_add_fusion.3
  990.4 16.4 fusion.98
  1012.2 24.3 %fusion.87 = f32[8,256,1792,1]{2,1,0,3:T(8,128)S(1)} fusion(bf16[2,1792,1216]{1,2,0:T(8,128)(2,1)} %param.32, bf16[1,8,256,1216]{2,3,1,0:T(8,128)(2,1)} %get-tuple-element.700, bf16[1,8,256,1216]{2,3,1,0:T(8,128)(2,1)S(1)} %copy-done.84), kind=kOutput, calls=%fused_computation.143 | convolution fusion | flops 17855938560 | bytes 33357824 | tf_op jit(solution)/shard_map/gstf,gdf->std/dot_general | solution.py:31
  1036.5 14.1 fusion.80
  1050.6 126.1 %reduce-scatter.18.cloned.1.call-done = bf16[8,64,1792]{2,1,0:T(8,128)(2,1)} async-done(((bf16[8,256,1792]{2,1,0:T(8,128)(2,1)}), bf16[8,64,1792]{2,1,0:T(8,128)(2,1)}) %reduce-scatter.18.cloned.1.call-update) | async-done | bytes 1835024 | tf_op jit(solution)/shard_map/reduce_scatter | solution.py:251
  1186.7 19.7 all_gather.31
  1209.2 110.7 %all-gather.11.cloned.1.call-done = bf16[8,256,1792]{2,1,0:T(8,128)(2,1)} async-done(((bf16[8,64,1792]{2,1,0:T(8,128)(2,1)}), bf16[8,256,1792]{2,1,0:T(8,128)(2,1)}) %all-gather.11.cloned.1.call-update) | async-done | bytes 7340048 | tf_op jit(solution)/shard_map/all_gather | solution.py:261
  1332.7 23.8 %all-to-all-done.2 = bf16[32,256,112]{1,2,0:T(8,128)(2,1)S(1)} async-done(((bf16[32,256,112]{1,2,0:T(8,128)(2,1)}), bf16[32,256,112]{1,2,0:T(8,128)(2,1)S(1)}, u32[]{:S(2)}, u32[]{:S(2)}) %all-to-all-start.2) | async-done | bytes 1835040 | tf_op jit(solution)/shard_map/all_to_all | solution.py:272
  1379.3 236.6 %while.43 = (s32[]{:T(128)}, f32[4,273,112]{2,1,0:T(8,128)}, f32[4,273]{1,0:T(4,128)S(1)}, f32[4,4,512,16]{2,3,1,0:T(8,128)}, f32[4,4,512,16]{2,3,1,0:T(8,128)},...) while((s32[]{:T(128)}, f32[4,273,112]{2,1,0:T(8,128)}, ...), condition=%wide.region_20.21_spmd.clone, body=%wide.region_13.20_spmd.clone.sunk | while | flops 8651475968 | bytes 97057840 | solution.py:78
  1647.7 17.2 copy.524
  1680.9 12.2 reduce-scatter.24.cloned.1.call-done
  1698.4 20.3 all-to-all-done.3
  1729.3 23.5 %copy.623 = bf16[4,8,16,1792]{1,2,0,3:T(8,128)(2,1)} copy(bf16[4,8,16,1792]{3,1,2,0:T(8,128)(2,1)S(1)} %pad_maximum_fusion.17) | data formatting | bytes 3670016
  1752.8 42.7 %reshape.389 = bf16[1792,512]{1,0:T(8,128)(2,1)} reshape(bf16[1792,4,16,8]{3,2,1,0:T(8,128)(2,1)} %bitcast.466) | data formatting | bytes 3670016
  1795.8 14.8 convolution_convert_fusion
  1868.0 13.8 fusion.79
  1881.9 79.7 %reduce-scatter.16.cloned.1.call-done = bf16[8,64,1792]{2,1,0:T(8,128)(2,1)} async-done(((bf16[8,256,1792]{2,1,0:T(8,128)(2,1)}), bf16[8,64,1792]{2,1,0:T(8,128)(2,1)}) %reduce-scatter.16.cloned.1.call-update) | async-done | bytes 1835024 | tf_op jit(solution)/shard_map/reduce_scatter | solution.py:218
  1966.8 62.0 %all-reduce.11.cloned.1.call-done = (bf16[4,8,16,448]{3,1,2,0:T(8,128)(2,1)}, bf16[8,16,1024]{2,0,1:T(8,128)(2,1)}, bf16[8,16,448]{2,0,1:T(8,128)(2,1)}, bf16[8,...) async-done(((bf16[4,8,16,448]{3,1,2,0:T(8,128)(2,1)}, bf16[8,16,1024]{2,0,1:T(8,128)(2,1)}, bf16[8,16,448]{2,0,1:T(8,128)(2,1)}, bf16[8,16,2,1216]{3,0,2,1:T(8,128)(2,1)}, ...) | async-done | bytes 1769488 | tf_op jit(solution)/shard_map/psum | solution.py:304
  2037.8 120.0 %reduce-scatter.20.cloned.1.call-done = bf16[8,64,1792]{2,1,0:T(8,128)(2,1)} async-done(((bf16[8,256,1792]{2,1,0:T(8,128)(2,1)}), bf16[8,64,1792]{2,1,0:T(8,128)(2,1)}) %reduce-scatter.20.cloned.1.call-update) | async-done | bytes 1835024 | tf_op jit(solution)/shard_map/reduce_scatter | solution.py:293
  (542 shorter events, 633.5 us)
Async XLA Ops:
  7.2 398.6 %copy-start = (bf16[448,1792]{1,0:T(8,128)(2,1)S(1)}, bf16[448,1792]{1,0:T(8,128)(2,1)}, u32[]{:S(2)}) copy-start(bf16[448,1792]{1,0:T(8,128)(2,1)} %param.31) | copy-start | bytes 4816900
  7.2 144.9 %all-gather.5.cloned.1.call-start = ((), (), s32[]{:S(2)}) async-start(), calls=%async_computation.11 | async-start | bytes 9175040 | tf_op jit(solution)/shard_map/all_gather | solution.py:145
  39.7 123.5 %copy-start.43 = (bf16[8,256,16,1]{1,2,3,0:T(8,128)(2,1)}, bf16[8,256,16,1]{1,2,3,0:T(8,128)(2,1)S(1)}, u32[]{:S(2)}) copy-start(bf16[8,256,16,1]{1,2,3,0:T(8,128)(2,1)S(1)} %copy.568) | copy-start | bytes 196612
  166.9 54.0 %all-to-all-start = ((bf16[32,256,256]{2,1,0:T(8,128)(2,1)}), bf16[32,256,256]{2,1,0:T(8,128)(2,1)}, u32[]{:S(2)}, u32[]{:S(2)}) async-start(bf16[32,256,256]{2,1,0:T(8,128)(2,1)} %bitcast.475), calls=%async_computation | async-start | bytes 8388608 | tf_op jit(solution)/shard_map/all_to_all | solution.py:160
  365.4 31.0 %all-to-all-start.1 = ((bf16[4,2048,112]{2,0,1:T(4,128)(2,1)}), bf16[4,2048,112]{2,0,1:T(4,128)(2,1)}, u32[]{:S(2)}, u32[]{:S(2)}) async-start(bf16[4,2048,112]{2,0,1:T(4,128)(2,1)} %copy.476), calls=%async_computation.1 | async-start | bytes 4194304 | tf_op jit(solution)/shard_map/all_to_all | solution.py:185
  369.8 53.1 %reduce-scatter.22.cloned.1.call-start = ((), (), s32[]{:S(2)}) async-start(), calls=%async_computation.19 | async-start | bytes 163840
  405.8 263.4 %reduce-scatter.14.cloned.1.call-start = ((), (), s32[]{:S(2)}) async-start(), calls=%async_computation.12 | async-start | bytes 18350080 | tf_op jit(solution)/shard_map/reduce_scatter | solution.py:194
  413.2 255.9 %copy-start.8 = (bf16[8,64,1792]{2,1,0:T(8,128)(2,1)S(1)}, bf16[8,64,1792]{2,1,0:T(8,128)(2,1)}, u32[]{:S(2)}) copy-start(bf16[8,64,1792]{2,1,0:T(8,128)(2,1)} %param.23) | copy-start | bytes 5505028
  413.3 398.0 %all-gather.9.cloned.1.call-start = ((), (), s32[]{:S(2)}) async-start(), calls=%async_computation.15 | async-start | bytes 9175040 | tf_op jit(solution)/shard_map/all_gather | solution.py:233
  413.9 766.1 %copy-start.64 = (f32[8,64]{1,0:T(8,128)}, f32[8,64]{1,0:T(8,128)S(1)}, u32[]{:S(2)}) copy-start(f32[8,64]{1,0:T(8,128)S(1)} %compare_convert_fusion.1) | copy-start | bytes 6148
  417.2 535.7 %all-gather.7.cloned.1.call-start = ((), (), s32[]{:S(2)}) async-start(), calls=%async_computation.13 | async-start | bytes 9175040 | tf_op jit(solution)/shard_map/all_gather | solution.py:204
  425.5 246.8 %copy-start.51 = (bf16[8,64,16]{1,2,0:T(8,128)(2,1)}, bf16[8,64,16]{1,2,0:T(8,128)(2,1)S(1)}, u32[]{:S(2)}) copy-start(bf16[8,64,16]{1,2,0:T(8,128)(2,1)S(1)} %copy.620) | copy-start | bytes 49156
  425.5 248.7 %copy-start.62 = (f32[1792]{0:T(1024)S(1)}, f32[1792]{0:T(1024)}, u32[]{:S(2)}) copy-start(f32[1792]{0:T(1024)} %param.28) | copy-start | bytes 21508
  672.4 507.6 %copy-start.67 = (f32[8,64]{1,0:T(8,128)}, f32[8,64]{1,0:T(8,128)S(1)}, u32[]{:S(2)}) copy-start(f32[8,64]{1,0:T(8,128)S(1)} %fusion.197) | copy-start | bytes 6148
  675.8 500.9 %reduce-scatter.18.cloned.1.call-start = ((), (), s32[]{:S(2)}) async-start(), calls=%async_computation.16 | async-start | bytes 9175040 | tf_op jit(solution)/shard_map/reduce_scatter | solution.py:251
  704.3 286.1 %copy-start.53 = (bf16[8,256,16]{1,2,0:T(8,128)(2,1)}, bf16[8,256,16]{1,2,0:T(8,128)(2,1)S(1)}, u32[]{:S(2)}) copy-start(bf16[8,256,16]{1,2,0:T(8,128)(2,1)S(1)} %copy.502) | copy-start | bytes 196612
  1050.5 129.5 %copy-start.21 = (bf16[8,64,1792]{2,1,0:T(8,128)(2,1)S(1)}, bf16[8,64,1792]{2,1,0:T(8,128)(2,1)}, u32[]{:S(2)}) copy-start(bf16[8,64,1792]{2,1,0:T(8,128)(2,1)} %param.24) | copy-start | bytes 5505028
  1050.6 269.3 %all-gather.11.cloned.1.call-start = ((), (), s32[]{:S(2)}) async-start(), calls=%async_computation.17 | async-start | bytes 9175040 | tf_op jit(solution)/shard_map/all_gather | solution.py:261
  1329.1 27.4 %all-to-all-start.2 = ((bf16[32,256,112]{1,2,0:T(8,128)(2,1)}), bf16[32,256,112]{1,2,0:T(8,128)(2,1)S(1)}, u32[]{:S(2)}, u32[]{:S(2)}) async-start(bf16[32,256,112]{1,2,0:T(8,128)(2,1)} %bitcast.493), calls=%async_computation.5 | async-start | bytes 3670016 | tf_op jit(solution)/shard_map/all_to_all | solution.py:272
  1664.9 53.8 %all-to-all-start.3 = ((bf16[4,2048,256]{2,0,1:T(4,128)(2,1)}), bf16[4,2048,256]{2,0,1:T(4,128)(2,1)}, u32[]{:S(2)}, u32[]{:S(2)}) async-start(bf16[4,2048,256]{2,0,1:T(4,128)(2,1)} %copy.524), calls=%async_computation.6 | async-start | bytes 8388608 | tf_op jit(solution)/shard_map/all_to_all | solution.py:274
  1669.6 23.5 %reduce-scatter.24.cloned.1.call-start = ((), (), s32[]{:S(2)}) async-start(), calls=%async_computation.20 | async-start | bytes 81920
  1674.2 163.6 %reduce-scatter.26.cloned.1.call-start = ((), (), s32[]{:S(2)}) async-start(), calls=%async_computation.21 | async-start | bytes 2293760
  1795.6 166.0 %reduce-scatter.16.cloned.1.call-start = ((), (), s32[]{:S(2)}) async-start(), calls=%async_computation.14 | async-start | bytes 9175040 | tf_op jit(solution)/shard_map/reduce_scatter | solution.py:218
  1810.7 218.1 %all-reduce.11.cloned.1.call-start = ((), (), s32[]{:S(2)}) async-start(), calls=%async_computation.22 | async-start | bytes 3801088 | tf_op jit(solution)/shard_map/psum | solution.py:304
  1857.0 300.9 %reduce-scatter.20.cloned.1.call-start = ((), (), s32[]{:S(2)}) async-start(), calls=%async_computation.18 | async-start | bytes 9175040 | tf_op jit(solution)/shard_map/reduce_scatter | solution.py:293
  2030.0 127.8 %copy-start.9 = (bf16[8,64,1792]{2,1,0:T(8,128)(2,1)S(1)}, bf16[8,64,1792]{2,1,0:T(8,128)(2,1)}, u32[]{:S(2)}) copy-start(bf16[8,64,1792]{2,1,0:T(8,128)(2,1)} %param.23) | copy-start | bytes 5505028
  2030.1 127.8 %copy-start.66 = (f32[1792]{0:T(1024)S(1)}, f32[1792]{0:T(1024)}, u32[]{:S(2)}) copy-start(f32[1792]{0:T(1024)} %param.27) | copy-start | bytes 21508
  2033.6 126.6 %copy-start.70 = (f32[8,64]{1,0:T(8,128)S(1)}, f32[8,64]{1,0:T(8,128)}, u32[]{:S(2)}) copy-start(f32[8,64]{1,0:T(8,128)} %copy-done.69) | copy-start | bytes 6148
  2033.6 126.6 %copy-start.63 = (f32[1792]{0:T(1024)S(1)}, f32[1792]{0:T(1024)}, u32[]{:S(2)}) copy-start(f32[1792]{0:T(1024)} %param.28) | copy-start | bytes 21508
  2033.6 126.6 %copy-start.68 = (f32[8,64]{1,0:T(8,128)S(1)}, f32[8,64]{1,0:T(8,128)}, u32[]{:S(2)}) copy-start(f32[8,64]{1,0:T(8,128)} %copy-done.67) | copy-start | bytes 6148
  2033.6 126.6 %copy-start.72 = (f32[8,64]{1,0:T(8,128)S(1)}, f32[8,64]{1,0:T(8,128)}, u32[]{:S(2)}) copy-start(f32[8,64]{1,0:T(8,128)} %copy-done.71) | copy-start | bytes 6148
  2033.6 126.6 %copy-start.74 = (f32[8,64]{1,0:T(8,128)S(1)}, f32[8,64]{1,0:T(8,128)}, u32[]{:S(2)}) copy-start(f32[8,64]{1,0:T(8,128)} %copy-done.73) | copy-start | bytes 6148
  (78 other events, 1264.2 us)
Sparse Core Ops, SparseCore 0:
  13.8 138.2 all-gather.4
  405.9 16.9 reduce-scatter.21
  425.3 243.8 reduce-scatter.13
  670.6 140.5 all-gather.8
  812.6 140.1 all-gather.6
  1050.7 125.9 reduce-scatter.17
  1184.5 135.3 all-gather.10
  1674.3 18.7 reduce-scatter.23
  1795.7 36.8 reduce-scatter.25
  1834.7 126.7 reduce-scatter.15
  1966.5 62.1 all-reduce.10
  2030.9 126.8 reduce-scatter.19
where the time goes:
time: 2180 us; the launch traced here: 2170 us
  waiting for transfers between devices  1190 us (55%)
  matrix products  487 us (22%)
  local copies, waits for them, and re-layouts  263 us (12%)
  blocking collectives  92.9 us (4%)
  other arithmetic  91.5 us (4%)
    reduce_scatter x1, waiting for transfers between devices, on_device(): lax.psum_scatter(branch_part, 'wa', scatter_dimension=1, tiled=True)  244 us
    dot_general x28, matrix products, project(): jnp.einsum(pattern, operand_one, operand_two, preferred_element_type=jnp....  191 us
    reduce_scatter x1, waiting for transfers between devices, on_device(): lax.psum_scatter(normed_two_part.astype(jnp.bfloat16), 'wa', scatter_dime...  126 us
    unnamed x189, local copies, waits for them, and re-layouts  124 us
    reduce_scatter x1, waiting for transfers between devices, on_device(): lax.psum_scatter(normed_part.astype(jnp.bfloat16), 'wa', scatter_dimensio...  120 us
    all_gather x1, waiting for transfers between devices, on_device(): lax.all_gather(normed, 'wa', axis=1, tiled=True)  111 us
    all_gather x1, waiting for transfers between devices, on_device(): lax.all_gather(branch_grad, 'wa', axis=1, tiled=True)  111 us
    all_gather x1, waiting for transfers between devices, on_device(): lax.all_gather(top_low, 'wa', axis=1, tiled=True)  101 us
  transfers between devices with their start and end apart: 16, of which 15 were waited for; matrix products, arithmetic and copies ran while one was open for 8% of the time, Pallas kernels for 0%

commit v1 on v0

v1 whole, which is shorter than its diff:
```python
import math

import jax
import jax.numpy as jnp
import numpy as np
from jax import lax
from jax.experimental import pallas as pl
from jax.experimental.pallas import tpu as pltpu
from jax.sharding import Mesh
from jax.sharding import PartitionSpec as P

HEADS = 16
HEAD = 112
FEAT = 16
PACK = 256
PAD = 128
PAIRS = 160
ONE_LANE = HEAD

EPSILON = 1e-05
BF = jnp.bfloat16
F32 = jnp.float32

CHIPS = ("g", "b", "a")
PLANE = ("b", "a", "c")
COLUMN = ("c", "wa")
EVERY = ("g", "b", "a", "c", "wa")


def constants():
    pairs = [(i, j) for i in range(FEAT + 1) for j in range(i, FEAT + 1)]
    table = {}
    for name, lane in (("q", 0), ("k", FEAT)):
        first = np.zeros((PACK, PAIRS), np.float32)
        second = np.zeros((PACK, PAIRS), np.float32)
        for f, (i, j) in enumerate(pairs):
            if i > 0:
                first[lane + i - 1, f] = 0.5
            if j > 0:
                second[lane + j - 1, f] = 0.5
        table["first_" + name] = first
        table["second_" + name] = second
    ones = np.zeros((3, PAIRS), np.float32)
    for f, (i, j) in enumerate(pairs):
        ones[0, f] = 1.0 if i == 0 else 0.0
        ones[1, f] = 1.0 if j == 0 else 0.0
        ones[2, f] = 0.5 if i == j and i > 0 else 1.0
    value = np.zeros((PACK, PAD), np.float32)
    gate = np.zeros((PACK, PAD), np.float32)
    for i in range(HEAD):
        value[2 * FEAT + i, i] = 1.0
        gate[2 * FEAT + HEAD + i, i] = 1.0
    key = np.zeros((PACK, PAD), np.float32)
    query = np.zeros((PACK, PAD), np.float32)
    for i in range(FEAT):
        key[FEAT + i, i] = 0.25
        query[i, FEAT + i] = 0.25
    table.update(value=value, gate=gate, key=key, query=query)
    return {k: jnp.asarray(v, BF) for k, v in table.items()}, jnp.asarray(ones)


def nn(left, right):
    return lax.dot_general(left, right, (((1,), (0,)), ((), ())), preferred_element_type=F32)


def nt(left, right):
    return lax.dot_general(left, right, (((1,), (1,)), ((), ())), preferred_element_type=F32)


def lanes(shape):
    return lax.broadcasted_iota(jnp.int32, shape, 1)


def rows_of(shape):
    return lax.broadcasted_iota(jnp.int32, shape, 0)


def augmented(block, value_ref):
    value = nn(block, value_ref[...])
    return jnp.where(lanes(value.shape) == ONE_LANE, 1.0, value)


def shift_down(values, halo, by):
    rolled = pltpu.roll(values, by, 0)
    place = rows_of(values.shape)
    for row in range(by):
        rolled = jnp.where(place == row, halo[8 - by + row : 9 - by + row, :], rolled)
    return rolled


def shift_up(values, halo, by):
    count = values.shape[0]
    rolled = pltpu.roll(values, count - by, 0)
    place = rows_of(values.shape)
    for row in range(by):
        rolled = jnp.where(place == count - by + row, halo[row : row + 1, :], rolled)
    return rolled


def sigmoid(values):
    return 1.0 / (1.0 + jnp.exp(-values))


def state_kernel(block_ref, keep_ref, first_ref, second_ref, ones_ref, value_ref, out_ref):
    block = block_ref[...]
    first = nt(first_ref[...], block) + ones_ref[:, 0:1]
    second = nt(second_ref[...], block) + ones_ref[:, 1:2]
    features = (first * second * keep_ref[...]).astype(BF)
    out_ref[0] = nn(features, augmented(block, value_ref).astype(BF))


def mixer_kernel(
    block_ref, keep_ref, state_ref, halo_ref, taps_ref, first_ref, second_ref, ones_ref,
    value_ref, gate_ref, key_ref, mixed_ref, kept_ref,
):
    block = block_ref[...]
    rows = block.shape[0]
    half = rows // 2
    first = nn(block, first_ref[...]) + ones_ref[0:1, :]
    second = nn(block, second_ref[...]) + ones_ref[1:2, :]
    features = (first * second * ones_ref[2:3, :]).astype(BF)
    value = augmented(block, value_ref)
    value_low = value.astype(BF)
    key = nn(block, key_ref[...]).astype(BF)
    low_lanes = block[:, :PAD]
    query = jnp.where(lanes(low_lanes.shape) < FEAT, low_lanes, jnp.zeros_like(low_lanes))
    past = nn(features, state_ref[0])
    causal = rows_of((half, half)) >= lanes((half, half))
    sums = []
    for r in range(2):
        total = past[r * half : (r + 1) * half]
        for c in range(r + 1):
            score = 1.0 + nt(query[r * half : (r + 1) * half], key[c * half : (c + 1) * half])
            weight = (0.5 * score * score + 0.5) * keep_ref[:, c * half : (c + 1) * half]
            if r == c:
                weight = jnp.where(causal, weight, 0.0)
            total = total + nn(weight.astype(BF), value_low[c * half : (c + 1) * half])
        sums.append(total)
    total = jnp.concatenate(sums, axis=0)
    inverse = 1.0 / total[:, ONE_LANE : ONE_LANE + 1]
    attended = total * inverse
    halo = nn(halo_ref[...], value_ref[...])
    convolved = (
        taps_ref[0:1, :] * value
        + taps_ref[1:2, :] * shift_down(value, halo, 1)
        + taps_ref[2:3, :] * shift_down(value, halo, 2)
    )
    gate = nn(block, gate_ref[...])
    mixed = attended + convolved * gate * sigmoid(gate)
    place = lanes(mixed.shape)
    mixed_ref[...] = jnp.where(place < HEAD, mixed, 0.0).astype(BF)
    kept_ref[...] = jnp.where(
        place < HEAD, attended, jnp.where(place == ONE_LANE, inverse, 0.0)
    ).astype(BF)


def back_state_kernel(
    block_ref, kept_ref, grad_ref, first_ref, second_ref, ones_ref, gate_ref, scaled_ref, state_ref, edge_ref,
):
    block = block_ref[...]
    grad = grad_ref[...].astype(F32)
    kept = kept_ref[...].astype(F32)
    place = lanes(grad.shape)
    inverse = kept[:, ONE_LANE : ONE_LANE + 1]
    along = jnp.sum(grad * kept, axis=1, keepdims=True)
    scaled = (jnp.where(place == ONE_LANE, -along, grad) * inverse).astype(BF)
    scaled_ref[...] = scaled
    first = nt(first_ref[...], block) + ones_ref[:, 0:1]
    second = nt(second_ref[...], block) + ones_ref[:, 1:2]
    features = (first * second * ones_ref[:, 2:3]).astype(BF)
    state_ref[0] = nn(features, scaled)
    gate = nn(block[:8], gate_ref[...])
    edge_ref[...] = grad[:8] * gate * sigmoid(gate)


def back_mixer_kernel(
    block_ref, scaled_ref, grad_ref, keep_ref, keep_column_ref, state_ref, later_ref, halo_ref, edge_ref, taps_ref,
    first_q_ref, second_q_ref, first_k_ref, second_k_ref,
    back_first_q_ref, back_second_q_ref, back_first_k_ref, back_second_k_ref,
    ones_ref, value_ref, gate_ref, key_ref, query_ref, back_value_ref, back_gate_ref, out_ref,
):
    block = block_ref[...]
    rows = block.shape[0]
    half = rows // 2
    scaled = scaled_ref[...]
    grad = grad_ref[...].astype(F32)
    keep_column = keep_column_ref[...]
    first_q = (nn(block, first_q_ref[...]) + ones_ref[0:1, :]) * ones_ref[2:3, :]
    second_q = (nn(block, second_q_ref[...]) + ones_ref[1:2, :]) * ones_ref[2:3, :]
    first_k = (nn(block, first_k_ref[...]) + ones_ref[0:1, :]) * keep_column
    second_k = (nn(block, second_k_ref[...]) + ones_ref[1:2, :]) * keep_column
    value = augmented(block, value_ref)
    value_low = value.astype(BF)
    feature_q_grad = nt(scaled, state_ref[0])
    feature_k_grad = nt(value_low, later_ref[0])
    pack_grad = (
        nn((feature_q_grad * second_q).astype(BF), back_first_q_ref[...])
        + nn((feature_q_grad * first_q).astype(BF), back_second_q_ref[...])
        + nn((feature_k_grad * second_k).astype(BF), back_first_k_ref[...])
        + nn((feature_k_grad * first_k).astype(BF), back_second_k_ref[...])
    )
    value_grad = nn((first_k * second_k).astype(BF), later_ref[0])
    key = nn(block, key_ref[...]).astype(BF)
    query_after = nn(block, query_ref[...]).astype(BF)
    low_lanes = block[:, :PAD]
    query = jnp.where(lanes(low_lanes.shape) < FEAT, low_lanes, jnp.zeros_like(low_lanes))
    causal = rows_of((half, half)) >= lanes((half, half))
    causal_turned = rows_of((half, half)) <= lanes((half, half))
    query_sums = []
    key_sums = [0.0, 0.0]
    value_sums = [0.0, 0.0]
    for r in range(2):
        here_r = slice(r * half, (r + 1) * half)
        query_sum = 0.0
        for c in range(r + 1):
            here_c = slice(c * half, (c + 1) * half)
            score = 1.0 + nt(query[here_r], key[here_c])
            weight_grad = nt(scaled[here_r], value_low[here_c])
            score_grad = score * weight_grad * keep_ref[:, here_c]
            if r == c:
                score_grad = jnp.where(causal, score_grad, 0.0)
            query_sum = query_sum + nn(score_grad.astype(BF), key[here_c])
            turned = 1.0 + nt(key[here_c], query[here_r])
            turned_grad = nt(value_low[here_c], scaled[here_r]) * turned * keep_column[here_c]
            weight = (0.5 * turned * turned + 0.5) * keep_column[here_c]
            if r == c:
                turned_grad = jnp.where(causal_turned, turned_grad, 0.0)
                weight = jnp.where(causal_turned, weight, 0.0)
            key_sums[c] = key_sums[c] + nn(turned_grad.astype(BF), query_after[here_r])
            value_sums[c] = value_sums[c] + nn(weight.astype(BF), scaled[here_r])
        query_sums.append(query_sum)
    pack_grad = pack_grad + jnp.concatenate(
        [query_sums[0] + key_sums[0], query_sums[1] + key_sums[1]], axis=0
    )
    value_grad = value_grad + jnp.concatenate(value_sums, axis=0)
    halo = nn(halo_ref[...], value_ref[...])
    convolved = (
        taps_ref[0:1, :] * value
        + taps_ref[1:2, :] * shift_down(value, halo, 1)
        + taps_ref[2:3, :] * shift_down(value, halo, 2)
    )
    gate = nn(block, gate_ref[...])
    sig = sigmoid(gate)
    passed = grad * gate * sig
    gate_grad = grad * convolved * sig * (1.0 + gate * (1.0 - sig))
    edge = edge_ref[...]
    value_grad = (
        value_grad
        + taps_ref[0:1, :] * passed
        + taps_ref[1:2, :] * shift_up(passed, edge, 1)
        + taps_ref[2:3, :] * shift_up(passed, edge, 2)
    )
    rest = nn(value_grad.astype(BF), back_value_ref[...]) + nn(
        gate_grad.astype(BF), back_gate_ref[...]
    )
    out_ref[:, :PAD] = (rest[:, :PAD] + pack_grad).astype(BF)
    out_ref[:, PAD:] = rest[:, PAD:].astype(BF)


def whole(shape):
    return pl.BlockSpec(shape, lambda *_: (0,) * len(shape))


def by_column(rows, width):
    return pl.BlockSpec((rows, width), lambda h: (0, h))


def by_head(shape):
    return pl.BlockSpec((1,) + shape, lambda h: (h, 0, 0))


def ffn_kernel(
    normed_ref, top_ref, rank_ref, top_rank_ref, rank_turned_ref, top_rank_turned_ref,
    gate_ref, up_ref, down_ref, expand_gate_ref, expand_up_ref, reduce_ref,
    feed_in_ref, back_in_ref, small_in_ref,
    feed_ref, back_ref, small_ref, expand_gate_grad_ref, expand_up_grad_ref, reduce_grad_ref,
):
    @pl.when(pl.program_id(0) == 0)
    def _():
        feed_ref[...] = feed_in_ref[...]
        back_ref[...] = back_in_ref[...]
        small_ref[...] = small_in_ref[...]

    normed = normed_ref[...]
    rank = rank_ref[...]
    gating = nn(normed, gate_ref[...]) + nn(rank, expand_gate_ref[...])
    upward = nn(normed, up_ref[...]) + nn(rank, expand_up_ref[...])
    hidden_grad = nn(top_ref[...], down_ref[...]) + nn(top_rank_ref[...], reduce_ref[...])
    sig = sigmoid(gating)
    silu = gating * sig
    hidden = (silu * upward).astype(BF)
    up_grad = (hidden_grad * silu).astype(BF)
    gate_grad = (hidden_grad * upward * (sig + silu * (1.0 - sig))).astype(BF)
    feed_ref[...] += nt(hidden, down_ref[...])
    back_ref[...] += nt(gate_grad, gate_ref[...]) + nt(up_grad, up_ref[...])
    small_ref[0] += nt(hidden, reduce_ref[...])
    small_ref[1] += nt(gate_grad, expand_gate_ref[...]) + nt(up_grad, expand_up_ref[...])
    expand_gate_grad_ref[...] = nn(rank_turned_ref[...], gate_grad)
    expand_up_grad_ref[...] = nn(rank_turned_ref[...], up_grad)
    reduce_grad_ref[...] = nn(top_rank_turned_ref[...], hidden)


def ffn_part(normed, top, rank, top_rank, weights, expand_gate, expand_up, reduce, feed, back, small):
    rows, width = normed.shape
    ranks = rank.shape[1]
    hidden = weights.shape[1] // 3
    step = 256
    steps = hidden // step
    once = pl.Buffered(1)

    def fixed(shape):
        return pl.BlockSpec(shape, lambda *_: (0,) * len(shape), pipeline_mode=once)

    def columns(count, offset):
        return pl.BlockSpec((count, step), lambda n: (0, offset + n))

    return pl.pallas_call(
        ffn_kernel,
        grid=(steps,),
        in_specs=[
            fixed((rows, width)), fixed((rows, width)), fixed((rows, ranks)), fixed((rows, ranks)),
            fixed((ranks, rows)), fixed((ranks, rows)),
            columns(width, 0), columns(width, steps), columns(width, 2 * steps),
            columns(ranks, 0), columns(ranks, 0), columns(ranks, 0),
            fixed((rows, width)), fixed((rows, width)), fixed((2, rows, ranks)),
        ],
        out_specs=[
            fixed((rows, width)), fixed((rows, width)), fixed((2, rows, ranks)),
            columns(ranks, 0), columns(ranks, 0), columns(ranks, 0),
        ],
        out_shape=[
            jax.ShapeDtypeStruct((rows, width), F32),
            jax.ShapeDtypeStruct((rows, width), F32),
            jax.ShapeDtypeStruct((2, rows, ranks), F32),
            jax.ShapeDtypeStruct((ranks, hidden), F32),
            jax.ShapeDtypeStruct((ranks, hidden), F32),
            jax.ShapeDtypeStruct((ranks, hidden), F32),
        ],
        input_output_aliases={12: 0, 13: 1, 14: 2},
        name="ffn_part",
    )(normed, top, rank, top_rank, rank.T, top_rank.T, weights, weights, weights, expand_gate, expand_up, reduce, feed, back, small)


def rms(values, gain):
    inverse = lax.rsqrt(jnp.mean(values * values, axis=-1, keepdims=True) + EPSILON)
    return values * inverse * gain


def rms_back(values, gain, upstream):
    inverse = lax.rsqrt(jnp.mean(values * values, axis=-1, keepdims=True) + EPSILON)
    scaled = upstream * gain
    mean = jnp.mean(values * scaled, axis=-1, keepdims=True)
    return inverse * scaled - values * (inverse * inverse * inverse) * mean


def dot(left, right, dims=((1,), (0,))):
    return lax.dot_general(left, right, (dims, ((), ())), preferred_element_type=F32)


ROWS = ((0,), (0,))
TURNED = ((1,), (1,))


def pad_heads(table):
    lead = table.shape[:-1]
    split = table.reshape(lead + (-1, HEAD))
    padded = jnp.pad(split, [(0, 0)] * len(lead) + [(0, 0), (0, PAD - HEAD)])
    return padded.reshape(lead + (-1,))


def unpad_heads(table):
    lead = table.shape[:-1]
    return table.reshape(lead + (-1, PAD))[..., :HEAD].reshape(lead + (-1,))


def on_device(
    tokens, cotangent, lengths, adapter_ids, gain_first, gain_second, conv_kernel, mixer_in, mixer_out, gate_up,
    down_weight, inward_down, inward_up, outward_down, outward_up, expand_down, expand_up, reduce_down, reduce_up,
):
    sequences, slot_rows, width = tokens.shape
    ways = lax.axis_size("wa")
    chips = lax.axis_size("g") * 4
    chip = lax.axis_index(CHIPS)
    core = lax.axis_index("c")
    place = lax.axis_index("wa")
    plane = lax.axis_index(PLANE)
    sequence = core * ways + place
    rows = slot_rows * sequences
    ranks = inward_down.shape[1]
    heads_here = mixer_in.shape[1] // PACK
    out_here = mixer_out.shape[0]
    hidden_here = down_weight.shape[0]
    hidden_pad = -(-hidden_here // 256) * 256 - hidden_here
    next_place = [((d + 1) % ways, d) for d in range(ways)]
    picks, ones = constants()

    def ring(piece):
        return lax.ppermute(piece, "wa", next_place)

    def spread_weights(shard):
        slice_rows = width // 8
        piece = lax.dynamic_slice_in_dim(shard, plane * slice_rows, slice_rows, 0)
        parts = [shard]
        for _ in range(ways - 1):
            piece = ring(piece)
            parts.append(lax.all_gather(piece, PLANE, axis=0, tiled=True))
        return parts

    x = lax.all_to_all(tokens, COLUMN, 0, 0, tiled=True).reshape(rows, width)
    cot = lax.all_to_all(cotangent, COLUMN, 0, 0, tiled=True).reshape(rows, width)

    out_turned = pad_heads(mixer_out.T)
    mixer_weights = spread_weights(jnp.concatenate([mixer_in, out_turned], axis=1))
    ffn_shard = jnp.concatenate(
        [jnp.pad(t, ((0, 0), (0, hidden_pad))) for t in (gate_up[0], gate_up[1], down_weight.T)], axis=1
    )
    ffn_weights = spread_weights(ffn_shard)

    own_tables = (inward_up, outward_down, expand_up.reshape(ADAPTERS(expand_up), ranks, -1), reduce_down)

    def tables_for(target):
        which = adapter_ids[target]
        return jnp.concatenate(
            [lax.dynamic_index_in_dim(t, which, 0, keepdims=False) for t in own_tables], axis=1
        )

    def place_at(step):
        return (place + step) % ways

    tables = [tables_for(sequence)]
    for j in range(1, ways):
        pairs = [(s, (s - j) % ways) for s in range(ways)]
        tables.append(lax.ppermute(tables_for(core * ways + (place - j) % ways), "wa", pairs))
    cut = [inward_up.shape[2], outward_down.shape[2], hidden_here, hidden_here, hidden_here]
    edges = np.cumsum([0] + cut)
    split_tables = [[t[:, edges[n] : edges[n + 1]] for n in range(5)] for t in tables]

    which = adapter_ids[sequence]

    def pick(table):
        return lax.dynamic_index_in_dim(table, which, 0, keepdims=False)

    inward_first, outward_second = pick(inward_down), pick(outward_up)
    expand_first, reduce_second = pick(expand_down), pick(reduce_up)

    positions = chip * rows + jnp.arange(rows, dtype=jnp.int32)
    keep = (positions < lengths[sequence]).astype(F32)
    keep_row, keep_column = keep[None, :], keep[:, None]

    inputs = x.astype(F32)
    normed = rms(inputs, gain_first).astype(BF)
    enter = dot(normed, inward_first, TURNED).astype(BF)
    in_width = mixer_in.shape[1]
    packed = jnp.concatenate(
        [
            (dot(normed, w[:, :in_width]) + dot(enter, t[0])).astype(BF)
            for w, t in zip(mixer_weights, split_tables)
        ],
        axis=1,
    )
    taps = pad_heads(jnp.roll(conv_kernel.astype(F32), -place * out_here, axis=1))
    taps = jnp.pad(taps, ((0, 5), (0, 0)))

    def chip_shift(piece, by):
        pairs = [(i, i + by) for i in range(chips) if 0 <= i + by < chips]
        return lax.ppermute(piece, CHIPS, pairs)

    halo = chip_shift(packed[-8:], 1)

    def scan_chips(local, want_bit):
        before = jnp.zeros_like(local)
        total = local
        bit = 1
        while bit < chips:
            got = lax.ppermute(total.astype(BF), CHIPS, [(i, i ^ bit) for i in range(chips)]).astype(F32)
            take = ((chip & bit) != 0) == want_bit
            before = before + jnp.where(take, got, 0.0)
            total = total + got
            bit *= 2
        return before.astype(BF)

    pairs_shape = (PAIRS, PAD)
    first_q, second_q, first_k, second_k = (picks[n] for n in ("first_q", "second_q", "first_k", "second_k"))
    ones_column = ones.T
    head_params = pltpu.CompilerParams(dimension_semantics=("arbitrary",))
    state = pl.pallas_call(
        state_kernel,
        grid=(HEADS,),
        in_specs=[
            by_column(rows, PACK), whole((1, rows)), whole((PAIRS, PACK)), whole((PAIRS, PACK)), whole((PAIRS, 3)), whole((PACK, PAD)),
        ],
        out_specs=by_head(pairs_shape),
        out_shape=jax.ShapeDtypeStruct((HEADS,) + pairs_shape, F32),
        compiler_params=head_params,
        name="state",
    )(packed, keep_row, first_k.T, second_k.T, ones_column, picks["value"])
    before = scan_chips(state, True)
    mixed, kept = pl.pallas_call(
        mixer_kernel,
        grid=(HEADS,),
        in_specs=[
            by_column(rows, PACK), whole((1, rows)), by_head(pairs_shape), by_column(8, PACK), by_column(8, PAD),
            whole((PACK, PAIRS)), whole((PACK, PAIRS)), whole((3, PAIRS)),
            whole((PACK, PAD)), whole((PACK, PAD)), whole((PACK, PAD)),
        ],
        out_specs=[by_column(rows, PAD), by_column(rows, PAD)],
        out_shape=[jax.ShapeDtypeStruct((rows, HEADS * PAD), BF)] * 2,
        compiler_params=head_params,
        name="mixer",
    )(packed, keep_row, before, halo, taps, first_q, second_q, ones, picks["value"], picks["gate"], picks["key"])

    outward_first = jnp.concatenate([pad_heads(t[1]) for t in split_tables], axis=1)
    out_weights = jnp.concatenate([w[:, in_width:] for w in mixer_weights], axis=1)
    leave = dot(mixed, outward_first, TURNED).astype(BF)
    residual = inputs + dot(mixed, out_weights, TURNED) + dot(leave, outward_second)
    normed_two = rms(residual, gain_second).astype(BF)
    expand = dot(normed_two, expand_first, TURNED).astype(BF)
    top = jnp.where(keep_column > 0, cot, jnp.zeros_like(cot))
    top_rank = dot(top, reduce_second, TURNED).astype(BF)

    feed = jnp.zeros((rows, width), F32)
    back = jnp.zeros((rows, width), F32)
    small = jnp.zeros((2, rows, ranks), F32)
    expand_grads = []
    for w, t in zip(ffn_weights, split_tables):
        padded = [jnp.pad(t[n], ((0, 0), (0, hidden_pad))) for n in (2, 3, 4)]
        feed, back, small, g_gate, g_up, g_reduce = ffn_part(
            normed_two, top, expand, top_rank, w, padded[0], padded[1], padded[2], feed, back, small
        )
        expand_grads.append(
            jnp.concatenate([g_gate[:, :hidden_here], g_up[:, :hidden_here], g_reduce[:, :hidden_here]], axis=1)
        )
    reduce_rank = small[0].astype(BF)
    output = keep_column * (residual + feed + dot(reduce_rank, reduce_second))
    expand_grad = small[1].astype(BF)
    back = back + dot(expand_grad, expand_first)
    grad_reduce_up = dot(reduce_rank, top, ROWS)
    grad_expand_down = dot(expand_grad, normed_two, ROWS)
    residual_grad = top.astype(F32) + rms_back(residual, gain_second, back)
    branch = residual_grad.astype(BF)
    leave_grad = dot(branch, outward_second, TURNED).astype(BF)
    grad_outward_up = dot(leave, branch, ROWS)
    mixed_grad = (dot(branch, out_weights) + dot(leave_grad, outward_first)).astype(BF)
    grad_outward_down = unpad_heads(dot(leave_grad, mixed, ROWS))

    scaled, back_state, edge = pl.pallas_call(
        back_state_kernel,
        grid=(HEADS,),
        in_specs=[
            by_column(rows, PACK), by_column(rows, PAD), by_column(rows, PAD),
            whole((PAIRS, PACK)), whole((PAIRS, PACK)), whole((PAIRS, 3)), whole((PACK, PAD)),
        ],
        out_specs=[by_column(rows, PAD), by_head(pairs_shape), by_column(8, PAD)],
        out_shape=[
            jax.ShapeDtypeStruct((rows, HEADS * PAD), BF),
            jax.ShapeDtypeStruct((HEADS,) + pairs_shape, F32),
            jax.ShapeDtypeStruct((8, HEADS * PAD), F32),
        ],
        compiler_params=head_params,
        name="back_state",
    )(packed, kept, mixed_grad, first_q.T, second_q.T, ones_column, picks["gate"])
    later = scan_chips(back_state, False)
    edge = chip_shift(edge, -1)
    packed_grad = pl.pallas_call(
        back_mixer_kernel,
        grid=(HEADS,),
        in_specs=[
            by_column(rows, PACK), by_column(rows, PAD), by_column(rows, PAD), whole((1, rows)), whole((rows, 1)),
            by_head(pairs_shape), by_head(pairs_shape), by_column(8, PACK), by_column(8, PAD), by_column(8, PAD),
        ]
        + [whole((PACK, PAIRS))] * 4
        + [whole((PAIRS, PAD))] * 4
        + [whole((3, PAIRS))]
        + [whole((PACK, PAD))] * 4
        + [whole((PAD, PACK))] * 2,
        out_specs=by_column(rows, PACK),
        out_shape=jax.ShapeDtypeStruct((rows, HEADS * PACK), BF),
        compiler_params=head_params,
        name="back_mixer",
    )(
        packed, scaled, mixed_grad, keep_row, keep_column, before, later, halo, edge, taps,
        first_q, second_q, first_k, second_k,
        first_q[:PAD].T, second_q[:PAD].T, first_k[:PAD].T, second_k[:PAD].T,
        ones, picks["value"], picks["gate"], picks["key"], picks["query"], picks["value"].T, picks["gate"].T,
    )

    inward_second = jnp.concatenate([t[0] for t in split_tables], axis=1)
    enter_grad = dot(packed_grad, inward_second, TURNED).astype(BF)
    normed_grad = dot(enter_grad, inward_first)
    for j, w in enumerate(mixer_weights):
        normed_grad = normed_grad + dot(packed_grad[:, j * in_width : (j + 1) * in_width], w[:, :in_width], TURNED)
    grad_inward_up = dot(enter, packed_grad, ROWS)
    grad_inward_down = dot(enter_grad, normed, ROWS)
    input_grad = residual_grad + rms_back(inputs, gain_first, normed_grad)

    def send_back(values):
        pieces = values.astype(BF).reshape(sequences, slot_rows, width)
        return lax.all_to_all(pieces, COLUMN, 0, 0, tiled=True).astype(F32)

    seq_hot = (jnp.arange(inward_down.shape[0], dtype=jnp.int32)[:, None] == adapter_ids[None, :]).astype(F32)

    def exchange(pieces):
        got = [pieces(0)]
        for j in range(1, ways):
            pairs = [(s, (s + j) % ways) for s in range(ways)]
            got.append(lax.ppermute(pieces(j).astype(BF), "wa", pairs).astype(F32))
        summed = lax.psum(jnp.stack(got).astype(BF), CHIPS)
        other = lax.ppermute(summed, "c", [(0, 1), (1, 0)])
        hot = jnp.roll(seq_hot.reshape(-1, 2, ways), -place, axis=2)
        hot = jnp.take(hot, (core + jnp.arange(2)) % 2, axis=1)
        order = jnp.array([(-j) % ways for j in range(ways)])
        hot = jnp.take(hot, order, axis=2).reshape(-1, 2 * ways)
        both = jnp.concatenate([summed, other], axis=0).astype(F32)
        return jnp.tensordot(hot, both, axes=1, precision=lax.Precision.HIGHEST)

    def shard_of(table, j):
        size = width // ways
        return lax.dynamic_slice_in_dim(table, place_at(j) * size, size, 1)

    early = exchange(
        lambda j: jnp.concatenate(
            [
                expand_grads[j],
                grad_outward_down[:, j * out_here : (j + 1) * out_here],
                shard_of(grad_outward_up, j),
                shard_of(grad_expand_down, j),
                shard_of(grad_reduce_up, j),
            ],
            axis=1,
        )
    )
    late = exchange(
        lambda j: jnp.concatenate(
            [grad_inward_up[:, j * in_width : (j + 1) * in_width], shard_of(grad_inward_down, j)], axis=1
        )
    )
    shard = width // ways
    at = np.cumsum([0, 2 * hidden_here, hidden_here, out_here, shard, shard, shard])
    early_parts = [early[:, :, at[n] : at[n + 1]] for n in range(6)]
    return (
        send_back(output),
        send_back(input_grad),
        late[:, :, in_width:],
        late[:, :, :in_width],
        early_parts[2],
        early_parts[3],
        early_parts[4],
        early_parts[0].reshape(early.shape[0], ranks, 2, hidden_here),
        early_parts[1],
        early_parts[5],
    )


def ADAPTERS(table):
    return table.shape[0]


def solution(mesh):
    ways = mesh.shape["wa"]
    split = Mesh(mesh.devices.reshape(-1, 2, 2, 2, ways), EVERY)
    slots = P(None, EVERY, None)
    in_specs = (
        slots, slots, P(), P(), P(), P(), P(),
        P(None, "wa"), P("wa", None), P(None, None, "wa"), P("wa", None),
        P(), P(None, None, "wa"), P(None, None, "wa"), P(), P(), P(None, None, None, "wa"), P(None, None, "wa"), P(),
    )
    third = P(None, None, "wa")
    out_specs = (slots, slots, third, third, third, third, third, P(None, None, None, "wa"), third, third)
    return jax.shard_map(on_device, mesh=split, in_specs=in_specs, out_specs=out_specs, check_vma=False)
```

time: 2180 us -> 848 us (0.39)
  waiting for transfers between devices: 1190 us -> 271 us
  matrix products: 487 us -> 96.9 us
  Pallas kernels: 0 us -> 202 us
  local copies, waits for them, and re-layouts: 263 us -> 119 us
  blocking collectives: 92.9 us -> 0 us
  starting transfers between devices: 19.1 us -> 77.4 us
  other arithmetic: 91.5 us -> 50.5 us
    reduce_scatter x4 -> x0, waiting for transfers between devices: 569 us -> none  [the longest x1 244 us: on_device(): lax.psum_scatter(branch_part, 'wa', scatter_dimension=1, tiled=True)]
    all_gather x4 -> x6, waiting for transfers between devices: 421 us -> 0.03 us  [spread_weights(): parts.append(lax.all_gather(piece, PLANE, axis=0, tiled=True))]
    dot_general x121 -> x33, matrix products: 487 us -> 96.9 us  [the longest x31 95 us: dot(): lax.dot_general(left, right, (dims, ((), ())), preferred_element_type=F32)]
    ppermute x0 -> x23, waiting for transfers between devices: none -> 216 us  [the longest x6 142 us: ring(): return lax.ppermute(piece, 'wa', next_place)]
    pallas_call x0 -> x8, Pallas kernels: none -> 202 us  [the longest x4 107 us: ffn_part(): pl.pallas_call(ffn_kernel, grid=(steps,), in_specs=[fixed((rows, width)),...]
    all_to_all x4, waiting for transfers between devices: 117 us -> 0.01 us  [the longest x2 0.01 us: send_back(): return lax.all_to_all(pieces, COLUMN, 0, 0, tiled=True).astype(F32)]
    all_gather x4 -> x0, blocking collectives: 92.9 us -> none  [the longest x1 25.5 us: on_device(): lax.all_gather(expand_rank, 'wa', axis=1, tiled=True)]
    unnamed x189 -> x207, local copies, waits for them, and re-layouts: 124 us -> 50.1 us
  transfers between devices with their start and end apart: 16 -> 34, of which waited for: 15 -> 13; matrix products, arithmetic and copies ran while one was open for 8% -> 26% of each run, Pallas kernels for 0% -> 19%
where the time goes in v1:
time: 848 us; the launch traced here: 841 us
  waiting for transfers between devices  271 us (32%)
  Pallas kernels  202 us (24%)
  local copies, waits for them, and re-layouts  119 us (14%)
  matrix products  96.9 us (11%)
  starting transfers between devices  77.4 us (9%)
  other arithmetic  50.5 us (6%)
  between operations  23.7 us (3%)
    ppermute x6, waiting for transfers between devices, ring(): return lax.ppermute(piece, 'wa', next_place)  142 us
    pallas_call x4, Pallas kernels, ffn_part(): pl.pallas_call(ffn_kernel, grid=(steps,), in_specs=[fixed((rows, width)),...  107 us
    dot_general x31, matrix products, dot(): lax.dot_general(left, right, (dims, ((), ())), preferred_element_type=F32)  95 us
    psum x1, waiting for transfers between devices, exchange(): summed = lax.psum(jnp.stack(got).astype(BF), CHIPS)  54.8 us
    unnamed x207, local copies, waits for them, and re-layouts  50.1 us
    pallas_call x1, Pallas kernels, on_device(): pl.pallas_call(back_mixer_kernel, grid=(HEADS,), in_specs=[by_column(rows...  46.5 us
    ppermute x3, waiting for transfers between devices, on_device(): lax.ppermute(tables_for(core * ways + (place - j) % ways), 'wa', pairs)  39.1 us
    ppermute x4, waiting for transfers between devices, scan_chips(): lax.ppermute(total.astype(BF), CHIPS, [(i, i ^ bit) for i in range(chips)])  33.6 us
  transfers between devices with their start and end apart: 34, of which 13 were waited for; matrix products, arithmetic and copies ran while one was open for 26% of the time, Pallas kernels for 19%

profile of v1, /device:TPU:0, one launch (start us, length us, event | category | flops | bytes accessed | tf_op | source)
XLA Modules:
  0.0 840.9 jit_solution(12830600710741719046)
XLA Ops:
  19.5 14.7 %collective-permute-done = bf16[224,1536]{1,0:T(8,128)(2,1)S(1)} collective-permute-done((bf16[224,1536]{1,0:T(8,128)(2,1)S(1)}, bf16[224,1536]{1,0:T(8,128)(2,1)S(1)}, u32[]{:S(2)}, u32[]{:S(2)}) %collective-permute-start) | collective-permute-done | bytes 688160 | tf_op jit(solution)/shard_map/ppermute | solution.py:398
  39.4 14.2 %collective-permute-done.2 = bf16[224,1536]{1,0:T(8,128)(2,1)S(1)} collective-permute-done((bf16[224,1536]{1,0:T(8,128)(2,1)}, bf16[224,1536]{1,0:T(8,128)(2,1)S(1)}, u32[]{:S(2)}, u32[]{:S(2)}) %collective-permute-start.2) | collective-permute-done | bytes 688160 | tf_op jit(solution)/shard_map/ppermute | solution.py:398
  58.7 13.3 %collective-permute-done.4 = bf16[224,1536]{1,0:T(8,128)(2,1)S(1)} collective-permute-done((bf16[224,1536]{1,0:T(8,128)(2,1)}, bf16[224,1536]{1,0:T(8,128)(2,1)S(1)}, u32[]{:S(2)}, u32[]{:S(2)}) %collective-permute-start.4) | collective-permute-done | bytes 688160 | tf_op jit(solution)/shard_map/ppermute | solution.py:398
  73.0 6.1 fusion.118
  79.1 7.2 copy.135
  86.3 7.3 copy.136
  93.6 7.2 copy.105
  100.8 7.4 fusion.5.gate_ref.up_ref.down_ref
  117.2 33.9 %collective-permute-done.9 = bf16[224,3840]{1,0:T(8,128)(2,1)S(1)} collective-permute-done((bf16[224,3840]{1,0:T(8,128)(2,1)S(1)}, bf16[224,3840]{1,0:T(8,128)(2,1)S(1)}, u32[]{:S(2)}, u32[]{:S(2)}) %collective-permute-start.9) | collective-permute-done | bytes 1720352 | tf_op jit(solution)/shard_map/ppermute | solution.py:398
  156.7 33.4 %collective-permute-done.10 = bf16[224,3840]{1,0:T(8,128)(2,1)S(1)} collective-permute-done((bf16[224,3840]{1,0:T(8,128)(2,1)}, bf16[224,3840]{1,0:T(8,128)(2,1)S(1)}, u32[]{:S(2)}, u32[]{:S(2)}) %collective-permute-start.10) | collective-permute-done | bytes 1720352 | tf_op jit(solution)/shard_map/ppermute | solution.py:398
  195.5 32.5 %collective-permute-done.11 = bf16[224,3840]{1,0:T(8,128)(2,1)S(1)} collective-permute-done((bf16[224,3840]{1,0:T(8,128)(2,1)}, bf16[224,3840]{1,0:T(8,128)(2,1)S(1)}, u32[]{:S(2)}, u32[]{:S(2)}) %collective-permute-start.11) | collective-permute-done | bytes 1720352 | tf_op jit(solution)/shard_map/ppermute | solution.py:398
  262.0 39.1 %collective-permute-done.3 = bf16[16,5120]{1,0:T(8,128)(2,1)S(1)} collective-permute-done((bf16[16,5120]{1,0:T(8,128)(2,1)}, bf16[16,5120]{1,0:T(8,128)(2,1)S(1)}, u32[]{:S(2)}, u32[]{:S(2)}) %collective-permute-start.3) | collective-permute-done | bytes 163872 | tf_op jit(solution)/shard_map/ppermute | solution.py:433
  322.9 6.5 add_convert_fusion.3
  329.4 6.3 add_convert_fusion.2
  335.7 6.0 add_convert_fusion.1
  343.8 14.3 %state.1 = f32[16,160,128]{2,1,0:T(8,128)} custom-call(bf16[512,4096]{1,0:T(8,128)(2,1)} %pad_maximum_fusion.1.block_ref, f32[1,512]{1,0:T(1,128)} %compare_convert_fusion.keep_ref, bf16[160,256]{1,0:T(8,128)(2,1)} %constant.315.first_ref, bf16[160,256]{1,0:T(8,128)(2,1)} %constant.316.second_ref, f32[160,3]{1,0:T(8,128)} %constant.317.ones_ref, ...), custom_call_target="tpu_custom_call" | custom-call | tf_op jit(solution)/shard_map/state/pallas_call | solution.py:486
  366.9 24.5 %collective-permute-done.6 = bf16[16,160,128]{2,1,0:T(8,128)(2,1)S(1)} collective-permute-done((bf16[16,160,128]{2,1,0:T(8,128)(2,1)}, bf16[16,160,128]{2,1,0:T(8,128)(2,1)S(1)}, u32[]{:S(2)}, u32[]{:S(2)}) %collective-permute-start.6) | collective-permute-done | bytes 655392 | tf_op jit(solution)/shard_map/ppermute | solution.py:475
  418.1 20.0 %mixer.1 = (bf16[512,2048]{1,0:T(8,128)(2,1)}, bf16[512,2048]{1,0:T(8,128)(2,1)}) custom-call(bf16[512,4096]{1,0:T(8,128)(2,1)} %pad_maximum_fusion.1.block_ref, f32[1,512]{1,0:T(1,128)} %compare_convert_fusion.keep_ref, bf16[16,160,128]{2,1,0:T(8,128)(2,1)} %fusion.40.state_ref, bf16[8,4096]{1,0:T(8,128)(2,1)} %copy-done.48, f32[8,2048]{1,0:T(8,128)} %pad.74.taps_ref, ...), custom_call_target="tpu_custom_call" | custom-call | tf_op jit(solution)/shard_map/mixer/pallas_call | solution.py:498
  442.1 6.6 multiply_reduce_fusion.1
  457.5 26.7 %ffn_part.4 = (f32[512,1792]{1,0:T(8,128)}, f32[512,1792]{1,0:T(8,128)}, f32[2,512,16]{2,1,0:T(8,128)}, f32[16,1280]{1,0:T(8,128)}, f32[16,1280]{1,0:T(8,128)}, /*index=5*/f32[16,1280]{1,0:T(8,128)}) custom-call(bf16[512,1792]{1,0:T(8,128)(2,1)} %copy-done.3, ...), custom_call_target="tpu_custom_call", output_to_operand_aliasing={{0}: (12, {}), {1}: (13, {}), {2}: (14, {})} | custom-call | tf_op jit(solution)/shard_map/ffn_part/pallas_call | solution.py:317
  488.7 26.9 %ffn_part.5 = (f32[512,1792]{1,0:T(8,128)}, f32[512,1792]{1,0:T(8,128)}, f32[2,512,16]{2,1,0:T(8,128)}, f32[16,1280]{1,0:T(8,128)}, f32[16,1280]{1,0:T(8,128)}, /*index=5*/f32[16,1280]{1,0:T(8,128)}) custom-call(bf16[512,1792]{1,0:T(8,128)(2,1)} %copy-done.3, ...), custom_call_target="tpu_custom_call", output_to_operand_aliasing={{0}: (12, {}), {1}: (13, {}), {2}: (14, {})} | custom-call | tf_op jit(solution)/shard_map/ffn_part/pallas_call | solution.py:317
  520.1 26.7 %ffn_part.6 = (f32[512,1792]{1,0:T(8,128)}, f32[512,1792]{1,0:T(8,128)}, f32[2,512,16]{2,1,0:T(8,128)}, f32[16,1280]{1,0:T(8,128)}, f32[16,1280]{1,0:T(8,128)}, /*index=5*/f32[16,1280]{1,0:T(8,128)}) custom-call(bf16[512,1792]{1,0:T(8,128)(2,1)} %copy-done.3, ...), custom_call_target="tpu_custom_call", output_to_operand_aliasing={{0}: (12, {}), {1}: (13, {}), {2}: (14, {})} | custom-call | tf_op jit(solution)/shard_map/ffn_part/pallas_call | solution.py:317
  551.4 26.7 %ffn_part.7 = (f32[512,1792]{1,0:T(8,128)}, f32[512,1792]{1,0:T(8,128)}, f32[2,512,16]{2,1,0:T(8,128)}, f32[16,1280]{1,0:T(8,128)}, f32[16,1280]{1,0:T(8,128)}, /*index=5*/f32[16,1280]{1,0:T(8,128)}) custom-call(bf16[512,1792]{1,0:T(8,128)(2,1)} %copy-done.3, ...), custom_call_target="tpu_custom_call", output_to_operand_aliasing={{0}: (12, {}), {1}: (13, {}), {2}: (14, {})} | custom-call | tf_op jit(solution)/shard_map/ffn_part/pallas_call | solution.py:317
  590.7 6.5 add_convert_fusion.grad_ref
  597.2 14.3 %back_state.1 = (bf16[512,2048]{1,0:T(8,128)(2,1)}, f32[16,160,128]{2,1,0:T(8,128)}, f32[8,2048]{1,0:T(8,128)}) custom-call(bf16[512,4096]{1,0:T(8,128)(2,1)} %pad_maximum_fusion.1.block_ref, bf16[512,2048]{1,0:T(8,128)(2,1)} %get-tuple-element.55.kept_ref, bf16[512,2048]{1,0:T(8,128)(2,1)} %add_convert_fusion.grad_ref, ...), custom_call_target="tpu_custom_call" | custom-call | tf_op jit(solution)/shard_map/back_state/pallas_call | solution.py:546
  615.2 5.2 multiply_convert_fusion
  642.6 7.8 collective-permute-done.13
  652.6 46.5 %back_mixer.1 = bf16[512,4096]{1,0:T(8,128)(2,1)} custom-call(bf16[512,4096]{1,0:T(8,128)(2,1)} %pad_maximum_fusion.1.block_ref, bf16[512,2048]{1,0:T(8,128)(2,1)} %get-tuple-element.56.scaled_ref, bf16[512,2048]{1,0:T(8,128)(2,1)} %add_convert_fusion.grad_ref, f32[1,512]{1,0:T(1,128)} %compare_convert_fusion.keep_ref, f32[512,1]{1,0:T(8,128)} %fusion.53.keep_column_ref, ...), custom_call_target="tpu_custom_call" | custom-call | tf_op jit(solution)/shard_map/back_mixer/pallas_call | solution.py:564
  720.7 6.3 fusion.25
  727.0 6.1 fusion.21
  733.2 7.4 fusion.16
  751.4 54.8 %all-reduce.24.cloned.1.call-done = (bf16[4,16,1472]{2,1,0:T(8,128)(2,1)}, bf16[4,16,5440]{2,1,0:T(8,128)(2,1)}) async-done(((bf16[4,16,1472]{2,1,0:T(8,128)(2,1)}, bf16[4,16,5440]{2,1,0:T(8,128)(2,1)}), (bf16[4,16,1472]{2,1,0:T(8,128)(2,1)}, bf16[4,16,5440]{2,1,0:T(8,128)(2,1)})) %all-reduce.24.cloned.1.call-update) | async-done | bytes 884752 | tf_op jit(solution)/shard_map/psum | solution.py:607
  (429 shorter events, 255.0 us)
Async XLA Ops:
  7.2 315.7 %all-gather.7.cloned.1.call-start = ((), (), s32[]{:S(2)}) async-start(), calls=%async_computation.4 | async-start | bytes 6193152 | tf_op jit(solution)/shard_map/all_gather | solution.py:406
  14.3 19.8 %collective-permute-start = (bf16[224,1536]{1,0:T(8,128)(2,1)S(1)}, bf16[224,1536]{1,0:T(8,128)(2,1)S(1)}, u32[]{:S(2)}, u32[]{:S(2)}) collective-permute-start(bf16[224,1536]{1,0:T(8,128)(2,1)S(1)} %fusion.50), channel_id=1, source_target_pairs={{1,0},{2,1},{3,2},{0,3},{5,4},{6,5},{7,6},{4,7},{9,8},{10,9},{11,1... | collective-permute-start | bytes 2064392 | tf_op jit(solution)/shard_map/ppermute | solution.py:398
  35.0 294.4 %all-gather.9.cloned.1.call-start = ((), (), s32[]{:S(2)}) async-start(), calls=%async_computation.5 | async-start | bytes 6193152 | tf_op jit(solution)/shard_map/all_gather | solution.py:406
  35.1 18.5 %collective-permute-start.2 = (bf16[224,1536]{1,0:T(8,128)(2,1)}, bf16[224,1536]{1,0:T(8,128)(2,1)S(1)}, u32[]{:S(2)}, u32[]{:S(2)}) collective-permute-start(bf16[224,1536]{1,0:T(8,128)(2,1)} %copy-done.40), channel_id=1, source_target_pairs={{1,0},{2,1},{3,2},{0,3},{5,4},{6,5},{7,6},{4,7},{9,8},{10,9},{11,1... | collective-permute-start | bytes 2064392 | tf_op jit(solution)/shard_map/ppermute | solution.py:398
  54.5 281.2 %all-gather.11.cloned.1.call-start = ((), (), s32[]{:S(2)}) async-start(), calls=%async_computation.6 | async-start | bytes 6193152 | tf_op jit(solution)/shard_map/all_gather | solution.py:406
  54.5 17.5 %collective-permute-start.4 = (bf16[224,1536]{1,0:T(8,128)(2,1)}, bf16[224,1536]{1,0:T(8,128)(2,1)S(1)}, u32[]{:S(2)}, u32[]{:S(2)}) collective-permute-start(bf16[224,1536]{1,0:T(8,128)(2,1)} %copy-done.41), channel_id=1, source_target_pairs={{1,0},{2,1},{3,2},{0,3},{5,4},{6,5},{7,6},{4,7},{9,8},{10,9},{11,1... | collective-permute-start | bytes 2064392 | tf_op jit(solution)/shard_map/ppermute | solution.py:398
  72.9 415.8 %all-gather.17.cloned.1.call-start = ((), (), s32[]{:S(2)}) async-start(), calls=%async_computation.9 | async-start | bytes 15482880 | tf_op jit(solution)/shard_map/all_gather | solution.py:406
  113.2 37.9 %collective-permute-start.9 = (bf16[224,3840]{1,0:T(8,128)(2,1)S(1)}, bf16[224,3840]{1,0:T(8,128)(2,1)S(1)}, u32[]{:S(2)}, u32[]{:S(2)}) collective-permute-start(bf16[224,3840]{1,0:T(8,128)(2,1)S(1)} %constant_dynamic-slice_fusion.1), channel_id=1, source_target_pairs={{1,0},{2,1},{3,2},{0,3},{5,4},{6,5},{7,6},{4,7},{9,8},{10,9},{11,1... | collective-permute-start | bytes 5160968 | tf_op jit(solution)/shard_map/ppermute | solution.py:398
  152.3 367.8 %all-gather.15.cloned.1.call-start = ((), (), s32[]{:S(2)}) async-start(), calls=%async_computation.8 | async-start | bytes 15482880 | tf_op jit(solution)/shard_map/all_gather | solution.py:406
  152.3 37.7 %collective-permute-start.10 = (bf16[224,3840]{1,0:T(8,128)(2,1)}, bf16[224,3840]{1,0:T(8,128)(2,1)S(1)}, u32[]{:S(2)}, u32[]{:S(2)}) collective-permute-start(bf16[224,3840]{1,0:T(8,128)(2,1)} %copy-done.36), channel_id=1, source_target_pairs={{1,0},{2,1},{3,2},{0,3},{5,4},{6,5},{7,6},{4,7},{9,8},{10,9},{11,1... | collective-permute-start | bytes 5160968 | tf_op jit(solution)/shard_map/ppermute | solution.py:398
  191.2 360.1 %all-gather.13.cloned.1.call-start = ((), (), s32[]{:S(2)}) async-start(), calls=%async_computation.7 | async-start | bytes 15482880 | tf_op jit(solution)/shard_map/all_gather | solution.py:406
  191.3 36.7 %collective-permute-start.11 = (bf16[224,3840]{1,0:T(8,128)(2,1)}, bf16[224,3840]{1,0:T(8,128)(2,1)S(1)}, u32[]{:S(2)}, u32[]{:S(2)}) collective-permute-start(bf16[224,3840]{1,0:T(8,128)(2,1)} %copy-done.35), channel_id=1, source_target_pairs={{1,0},{2,1},{3,2},{0,3},{5,4},{6,5},{7,6},{4,7},{9,8},{10,9},{11,1... | collective-permute-start | bytes 5160968 | tf_op jit(solution)/shard_map/ppermute | solution.py:398
  239.3 22.6 %collective-permute-start.1 = (bf16[16,5120]{1,0:T(8,128)(2,1)S(1)}, bf16[16,5120]{1,0:T(8,128)(2,1)S(1)}, u32[]{:S(2)}, u32[]{:S(2)}) collective-permute-start(bf16[16,5120]{1,0:T(8,128)(2,1)S(1)} %concatenate.76), channel_id=1, source_target_pairs={{0,3},{1,0},{2,1},{3,2},{4,7},{5,4},{6,5},{7,6},{8,11},{9,8},{10,9... | collective-permute-start | bytes 491528 | tf_op jit(solution)/shard_map/ppermute | solution.py:433
  243.5 63.7 %all-to-all-start = ((bf16[8,64,1792]{2,1,0:T(8,128)(2,1)}), bf16[8,64,1792]{2,1,0:T(8,128)(2,1)S(1)}, u32[]{:S(2)}, u32[]{:S(2)}) async-start(bf16[8,64,1792]{2,1,0:T(8,128)(2,1)} %param.36), calls=%async_computation | async-start | bytes 3670016 | tf_op jit(solution)/shard_map/all_to_all | solution.py:409
  247.9 53.1 %collective-permute-start.3 = (bf16[16,5120]{1,0:T(8,128)(2,1)}, bf16[16,5120]{1,0:T(8,128)(2,1)S(1)}, u32[]{:S(2)}, u32[]{:S(2)}) collective-permute-start(bf16[16,5120]{1,0:T(8,128)(2,1)} %concatenate.77), channel_id=1, source_target_pairs={{0,2},{1,3},{2,0},{3,1},{4,6},{5,7},{6,4},{7,5},{8,10},{9,11},{10,... | collective-permute-start | bytes 491528 | tf_op jit(solution)/shard_map/ppermute | solution.py:433
  251.6 49.5 %collective-permute-start.5 = (bf16[16,5120]{1,0:T(8,128)(2,1)}, bf16[16,5120]{1,0:T(8,128)(2,1)S(1)}, u32[]{:S(2)}, u32[]{:S(2)}) collective-permute-start(bf16[16,5120]{1,0:T(8,128)(2,1)} %concatenate.78), channel_id=1, source_target_pairs={{0,1},{1,2},{2,3},{3,0},{4,5},{5,6},{6,7},{7,4},{8,9},{9,10},{10,1... | collective-permute-start | bytes 491528 | tf_op jit(solution)/shard_map/ppermute | solution.py:433
  307.2 54.7 %all-to-all-start.1 = ((bf16[8,64,1792]{2,1,0:T(8,128)(2,1)}), bf16[8,64,1792]{2,1,0:T(8,128)(2,1)}, u32[]{:S(2)}, u32[]{:S(2)}) async-start(bf16[8,64,1792]{2,1,0:T(8,128)(2,1)} %param.37), calls=%async_computation.1 | async-start | bytes 3670016 | tf_op jit(solution)/shard_map/all_to_all | solution.py:410
  360.4 31.0 %collective-permute-start.6 = (bf16[16,160,128]{2,1,0:T(8,128)(2,1)}, bf16[16,160,128]{2,1,0:T(8,128)(2,1)S(1)}, u32[]{:S(2)}, u32[]{:S(2)}) collective-permute-start(bf16[16,160,128]{2,1,0:T(8,128)(2,1)} %convert_element_type.208), channel_id=1, source_target_pairs={{0,8},{8,0},{16,24},{24,16},{1,9},{9,1},{17,25},{25,17},{2,10},{10... | collective-permute-start | bytes 1966088 | tf_op jit(solution)/shard_map/ppermute | solution.py:475
  392.4 22.9 %collective-permute-start.7 = (bf16[16,160,128]{2,1,0:T(8,128)(2,1)}, bf16[16,160,128]{2,1,0:T(8,128)(2,1)}, u32[]{:S(2)}, u32[]{:S(2)}) collective-permute-start(bf16[16,160,128]{2,1,0:T(8,128)(2,1)} %fusion.41), channel_id=1, source_target_pairs={{0,16},{8,24},{16,0},{24,8},{1,17},{9,25},{17,1},{25,9},{2,18},{10... | collective-permute-start | bytes 1966088 | tf_op jit(solution)/shard_map/ppermute | solution.py:475
  407.1 10.4 %collective-permute-start.8 = (bf16[8,4096]{1,0:T(8,128)(2,1)S(1)}, bf16[8,4096]{1,0:T(8,128)(2,1)S(1)}, u32[]{:S(2)}, u32[]{:S(2)}) collective-permute-start(bf16[8,4096]{1,0:T(8,128)(2,1)S(1)} %slice.295), channel_id=1, source_target_pairs={{0,8},{8,16},{16,24},{1,9},{9,17},{17,25},{2,10},{10,18},{18,26},{... | collective-permute-start | bytes 196616 | tf_op jit(solution)/shard_map/ppermute | solution.py:466
  613.7 17.5 %collective-permute-start.12 = (bf16[16,160,128]{2,1,0:T(8,128)(2,1)}, bf16[16,160,128]{2,1,0:T(8,128)(2,1)S(1)}, u32[]{:S(2)}, u32[]{:S(2)}) collective-permute-start(bf16[16,160,128]{2,1,0:T(8,128)(2,1)} %convert_element_type.230), channel_id=1, source_target_pairs={{0,8},{8,0},{16,24},{24,16},{1,9},{9,1},{17,25},{25,17},{2,10},{10... | collective-permute-start | bytes 1966088 | tf_op jit(solution)/shard_map/ppermute | solution.py:475
  620.8 31.8 %collective-permute-start.14 = (f32[8,2048]{1,0:T(8,128)}, f32[8,2048]{1,0:T(8,128)}, u32[]{:S(2)}, u32[]{:S(2)}) collective-permute-start(f32[8,2048]{1,0:T(8,128)} %get-tuple-element.58), channel_id=1, source_target_pairs={{8,0},{16,8},{24,16},{9,1},{17,9},{25,17},{10,2},{18,10},{26,18},{... | collective-permute-start | bytes 196616 | tf_op jit(solution)/shard_map/ppermute | solution.py:466
  622.8 122.2 %all-to-all-start.2 = ((bf16[8,64,1792]{2,1,0:T(8,128)(2,1)}), bf16[8,64,1792]{2,1,0:T(8,128)(2,1)}, u32[]{:S(2)}, u32[]{:S(2)}) async-start(bf16[8,64,1792]{2,1,0:T(8,128)(2,1)} %bitcast.184), calls=%async_computation.2 | async-start | bytes 3670016 | tf_op jit(solution)/shard_map/all_to_all | solution.py:598
  632.3 18.1 %collective-permute-start.13 = (bf16[16,160,128]{2,1,0:T(8,128)(2,1)}, bf16[16,160,128]{2,1,0:T(8,128)(2,1)}, u32[]{:S(2)}, u32[]{:S(2)}) collective-permute-start(bf16[16,160,128]{2,1,0:T(8,128)(2,1)} %fusion.44), channel_id=1, source_target_pairs={{0,16},{8,24},{16,0},{24,8},{1,17},{9,25},{17,1},{25,9},{2,18},{10... | collective-permute-start | bytes 1966088 | tf_op jit(solution)/shard_map/ppermute | solution.py:475
  712.0 37.6 %collective-permute-start.19 = (bf16[16,5440]{1,0:T(8,128)(2,1)S(1)}, bf16[16,5440]{1,0:T(8,128)(2,1)S(1)}, u32[]{:S(2)}, u32[]{:S(2)}) collective-permute-start(bf16[16,5440]{1,0:T(8,128)(2,1)S(1)} %concatenate.92), channel_id=1, source_target_pairs={{0,1},{1,2},{2,3},{3,0},{4,5},{5,6},{6,7},{7,4},{8,9},{9,10},{10,1... | collective-permute-start | bytes 522248 | tf_op jit(solution)/shard_map/ppermute | solution.py:606
  713.8 35.8 %collective-permute-start.20 = (bf16[16,5440]{1,0:T(8,128)(2,1)S(1)}, bf16[16,5440]{1,0:T(8,128)(2,1)S(1)}, u32[]{:S(2)}, u32[]{:S(2)}) collective-permute-start(bf16[16,5440]{1,0:T(8,128)(2,1)S(1)} %concatenate.93), channel_id=1, source_target_pairs={{0,2},{1,3},{2,0},{3,1},{4,6},{5,7},{6,4},{7,5},{8,10},{9,11},{10,... | collective-permute-start | bytes 522248 | tf_op jit(solution)/shard_map/ppermute | solution.py:606
  716.3 27.0 %collective-permute-start.15 = (bf16[16,1472]{1,0:T(8,128)(2,1)S(1)}, bf16[16,1472]{1,0:T(8,128)(2,1)S(1)}, u32[]{:S(2)}, u32[]{:S(2)}) collective-permute-start(bf16[16,1472]{1,0:T(8,128)(2,1)S(1)} %pad_maximum_fusion.8), channel_id=1, source_target_pairs={{0,1},{1,2},{2,3},{3,0},{4,5},{5,6},{6,7},{7,4},{8,9},{9,10},{10,1... | collective-permute-start | bytes 141320 | tf_op jit(solution)/shard_map/ppermute | solution.py:606
  716.7 27.6 %collective-permute-start.16 = (bf16[16,1472]{1,0:T(8,128)(2,1)S(1)}, bf16[16,1472]{1,0:T(8,128)(2,1)S(1)}, u32[]{:S(2)}, u32[]{:S(2)}) collective-permute-start(bf16[16,1472]{1,0:T(8,128)(2,1)S(1)} %pad_maximum_fusion.9), channel_id=1, source_target_pairs={{0,2},{1,3},{2,0},{3,1},{4,6},{5,7},{6,4},{7,5},{8,10},{9,11},{10,... | collective-permute-start | bytes 141320 | tf_op jit(solution)/shard_map/ppermute | solution.py:606
  718.4 25.9 %collective-permute-start.17 = (bf16[16,1472]{1,0:T(8,128)(2,1)S(1)}, bf16[16,1472]{1,0:T(8,128)(2,1)S(1)}, u32[]{:S(2)}, u32[]{:S(2)}) collective-permute-start(bf16[16,1472]{1,0:T(8,128)(2,1)S(1)} %pad_maximum_fusion.10), channel_id=1, source_target_pairs={{0,3},{1,0},{2,1},{3,2},{4,7},{5,4},{6,5},{7,6},{8,11},{9,8},{10,9... | collective-permute-start | bytes 141320 | tf_op jit(solution)/shard_map/ppermute | solution.py:606
  743.3 6.3 collective-permute-start.21
  745.0 85.2 %all-to-all-start.3 = ((bf16[8,64,1792]{2,1,0:T(8,128)(2,1)}), bf16[8,64,1792]{2,1,0:T(8,128)(2,1)}, u32[]{:S(2)}, u32[]{:S(2)}) async-start(bf16[8,64,1792]{2,1,0:T(8,128)(2,1)} %bitcast.39), calls=%async_computation.3 | async-start | bytes 3670016 | tf_op jit(solution)/shard_map/all_to_all | solution.py:598
  749.3 56.8 %all-reduce.24.cloned.1.call-start = ((), (), s32[]{:S(2)}) async-start(), calls=%async_computation.10 | async-start | bytes 1802240 | tf_op jit(solution)/shard_map/psum | solution.py:607
  (100 other events, 2136.5 us)
Sparse Core Ops, SparseCore 0:
  35.1 44.0 all-gather.6
  81.1 42.0 all-gather.8
  125.1 42.0 all-gather.10
  168.9 76.9 all-gather.16
  247.7 77.0 all-gather.14
  326.5 90.9 all-gather.12
  754.5 51.6 all-reduce.23

commit v2 on v1

v2 whole, which is shorter than its diff:
```python
import math

import jax
import jax.numpy as jnp
import numpy as np
from jax import lax
from jax.experimental import pallas as pl
from jax.experimental.pallas import tpu as pltpu
from jax.sharding import Mesh
from jax.sharding import PartitionSpec as P

HEADS = 16
HEAD = 112
FEAT = 16
PACK = 256
PAD = 128
PAIRS = 160
ONE_LANE = HEAD

EPSILON = 1e-05
BF = jnp.bfloat16
F32 = jnp.float32

CHIPS = ("g", "b", "a")
PLANE = ("b", "a", "c")
COLUMN = ("c", "wa")
EVERY = ("g", "b", "a", "c", "wa")


def constants():
    pairs = [(i, j) for i in range(FEAT + 1) for j in range(i, FEAT + 1)]
    first = np.zeros((PAD, PAIRS), np.float32)
    second = np.zeros((PAD, PAIRS), np.float32)
    ones = np.zeros((3, PAIRS), np.float32)
    for f, (i, j) in enumerate(pairs):
        if i > 0:
            first[HEAD + i - 1, f] = 0.5
        if j > 0:
            second[HEAD + j - 1, f] = 0.5
        ones[0, f] = 1.0 if i == 0 else 0.0
        ones[1, f] = 1.0 if j == 0 else 0.0
        ones[2, f] = 0.5 if i == j and i > 0 else 1.0
    order = np.zeros((PACK, PACK), np.float32)
    for i in range(FEAT):
        order[i, HEAD + i] = 1.0
        order[FEAT + i, PAD + HEAD + i] = 1.0
    for i in range(HEAD):
        order[2 * FEAT + i, i] = 1.0
        order[2 * FEAT + HEAD + i, PAD + i] = 1.0
    return jnp.asarray(first, BF), jnp.asarray(second, BF), jnp.asarray(ones), jnp.asarray(order, BF)


def nn(left, right):
    return lax.dot_general(left, right, (((1,), (0,)), ((), ())), preferred_element_type=F32)


def nt(left, right):
    return lax.dot_general(left, right, (((1,), (1,)), ((), ())), preferred_element_type=F32)


def lanes(shape):
    return lax.broadcasted_iota(jnp.int32, shape, 1)


def rows_of(shape):
    return lax.broadcasted_iota(jnp.int32, shape, 0)


def tn(left, right):
    return lax.dot_general(left, right, (((0,), (0,)), ((), ())), preferred_element_type=F32)


def halves(block):
    left, right = block[:, :PAD], block[:, PAD:]
    place = lanes(left.shape)
    zero = jnp.zeros_like(left)
    value = jnp.where(place < HEAD, left, jnp.where(place == ONE_LANE, jnp.ones_like(left), zero))
    query = jnp.where(place < HEAD, zero, left)
    gate = jnp.where(place < HEAD, right, zero)
    key = jnp.where(place < HEAD, zero, right)
    return value, query, gate, key


def shift_down(values, halo, by):
    rolled = pltpu.roll(values, by, 0)
    place = rows_of(values.shape)
    for row in range(by):
        rolled = jnp.where(place == row, halo[8 - by + row : 9 - by + row, :], rolled)
    return rolled


def shift_up(values, halo, by):
    count = values.shape[0]
    rolled = pltpu.roll(values, count - by, 0)
    place = rows_of(values.shape)
    for row in range(by):
        rolled = jnp.where(place == count - by + row, halo[row : row + 1, :], rolled)
    return rolled


def sigmoid(values):
    return 1.0 / (1.0 + jnp.exp(-values))


def state_kernel(block_ref, keep_ref, first_ref, second_ref, ones_ref, out_ref):
    block = block_ref[...]
    right = block[:, PAD:]
    first = nt(first_ref[...], right) + ones_ref[:, 0:1]
    second = nt(second_ref[...], right) + ones_ref[:, 1:2]
    features = (first * second * keep_ref[...]).astype(BF)
    out_ref[0] = nn(features, halves(block)[0])


def inside_kernel(block_ref, keep_column_ref, out_ref):
    value, query, _, key = halves(block_ref[...])
    half = value.shape[0] // 2
    value = value * keep_column_ref[...].astype(BF)
    key = key * 0.25
    causal = rows_of((half, half)) >= lanes((half, half))
    for r in range(2):
        total = 0.0
        for c in range(r + 1):
            score = 1.0 + nt(query[r * half : (r + 1) * half], key[c * half : (c + 1) * half])
            weight = 0.5 * score * score + 0.5
            if r == c:
                weight = jnp.where(causal, weight, 0.0)
            total = total + nn(weight.astype(BF), value[c * half : (c + 1) * half])
        out_ref[r * half : (r + 1) * half, :] = total


def mixer_kernel(
    block_ref, inside_ref, state_ref, halo_ref, taps_ref, first_ref, second_ref, ones_ref, mixed_ref, kept_ref
):
    block = block_ref[...]
    left = block[:, :PAD]
    first = nn(left, first_ref[...]) + ones_ref[0:1, :]
    second = nn(left, second_ref[...]) + ones_ref[1:2, :]
    features = (first * second * ones_ref[2:3, :]).astype(BF)
    value, _, gate, _ = halves(block)
    value, gate = value.astype(F32), gate.astype(F32)
    total = inside_ref[...] + nn(features, state_ref[0])
    inverse = 1.0 / total[:, ONE_LANE : ONE_LANE + 1]
    attended = total * inverse
    halo = halo_ref[:, :PAD].astype(F32)
    convolved = (
        taps_ref[0:1, :] * value
        + taps_ref[1:2, :] * shift_down(value, halo, 1)
        + taps_ref[2:3, :] * shift_down(value, halo, 2)
    )
    mixed = attended + convolved * gate * sigmoid(gate)
    place = lanes(mixed.shape)
    mixed_ref[...] = jnp.where(place < HEAD, mixed, 0.0).astype(BF)
    kept_ref[...] = jnp.where(
        place < HEAD, attended, jnp.where(place == ONE_LANE, inverse, 0.0)
    ).astype(BF)


def back_state_kernel(
    block_ref, kept_ref, grad_ref, first_ref, second_ref, ones_ref, scaled_ref, state_ref, edge_ref
):
    block = block_ref[...]
    grad = grad_ref[...].astype(F32)
    kept = kept_ref[...].astype(F32)
    place = lanes(grad.shape)
    inverse = kept[:, ONE_LANE : ONE_LANE + 1]
    along = jnp.sum(grad * kept, axis=1, keepdims=True)
    scaled = (jnp.where(place == ONE_LANE, -along, grad) * inverse).astype(BF)
    scaled_ref[...] = scaled
    left = block[:, :PAD]
    first = nt(first_ref[...], left) + ones_ref[:, 0:1]
    second = nt(second_ref[...], left) + ones_ref[:, 1:2]
    features = (first * second * ones_ref[:, 2:3]).astype(BF)
    state_ref[0] = nn(features, scaled)
    gate = block[:8, PAD:].astype(F32)
    edge_ref[...] = grad[:8] * gate * sigmoid(gate)


def back_inside_kernel(
    block_ref, scaled_ref, grad_ref, keep_column_ref, state_ref, halo_ref, taps_ref,
    first_ref, second_ref, back_first_ref, back_second_ref, ones_ref, out_ref,
):
    block = block_ref[...]
    rows = block.shape[0]
    half = rows // 2
    scaled = scaled_ref[...]
    grad = grad_ref[...].astype(F32)
    keep_column = keep_column_ref[...]
    value, query, gate, key = halves(block)
    full_value, gate = value.astype(F32), gate.astype(F32)
    value = value * keep_column.astype(BF)
    left = block[:, :PAD]
    first = (nn(left, first_ref[...]) + ones_ref[0:1, :]) * ones_ref[2:3, :]
    second = (nn(left, second_ref[...]) + ones_ref[1:2, :]) * ones_ref[2:3, :]
    feature_grad = nt(scaled, state_ref[0])
    query_grad = nn((feature_grad * second).astype(BF), back_first_ref[...]) + nn(
        (feature_grad * first).astype(BF), back_second_ref[...]
    )
    key = key * 0.25
    query_after = query * 0.25
    causal = rows_of((half, half)) >= lanes((half, half))
    query_sums = []
    key_sums = [0.0, 0.0]
    value_sums = [0.0, 0.0]
    for r in range(2):
        here_r = slice(r * half, (r + 1) * half)
        query_sum = query_grad[here_r]
        for c in range(r + 1):
            here_c = slice(c * half, (c + 1) * half)
            score = 1.0 + nt(query[here_r], key[here_c])
            score_grad = score * nt(scaled[here_r], value[here_c])
            weight = 0.5 * score * score + 0.5
            if r == c:
                score_grad = jnp.where(causal, score_grad, 0.0)
                weight = jnp.where(causal, weight, 0.0)
            score_grad = score_grad.astype(BF)
            query_sum = query_sum + nn(score_grad, key[here_c])
            key_sums[c] = key_sums[c] + tn(score_grad, query_after[here_r])
            value_sums[c] = value_sums[c] + tn(weight.astype(BF), scaled[here_r])
        query_sums.append(query_sum)
    query_grad = jnp.concatenate(query_sums, axis=0)
    key_grad = jnp.concatenate(key_sums, axis=0)
    value_grad = jnp.concatenate(value_sums, axis=0) * keep_column
    halo = halo_ref[:, :PAD].astype(F32)
    convolved = (
        taps_ref[0:1, :] * full_value
        + taps_ref[1:2, :] * shift_down(full_value, halo, 1)
        + taps_ref[2:3, :] * shift_down(full_value, halo, 2)
    )
    sig = sigmoid(gate)
    passed = grad * gate * sig
    gate_grad = grad * convolved * sig * (1.0 + gate * (1.0 - sig))
    nothing = jnp.zeros((8, PAD), F32)
    value_grad = (
        value_grad
        + taps_ref[0:1, :] * passed
        + taps_ref[1:2, :] * shift_up(passed, nothing, 1)
        + taps_ref[2:3, :] * shift_up(passed, nothing, 2)
    )
    place = lanes(query_grad.shape)
    out_ref[:, :PAD] = jnp.where(place < HEAD, value_grad, query_grad).astype(BF)
    out_ref[:, PAD:] = jnp.where(place < HEAD, gate_grad, key_grad).astype(BF)


def back_later_kernel(
    block_ref, part_ref, keep_column_ref, later_ref, edge_ref, taps_ref,
    first_ref, second_ref, back_first_ref, back_second_ref, ones_ref, out_ref,
):
    block = block_ref[...]
    keep_column = keep_column_ref[...]
    right = block[:, PAD:]
    first = (nn(right, first_ref[...]) + ones_ref[0:1, :]) * keep_column
    second = nn(right, second_ref[...]) + ones_ref[1:2, :]
    second_kept = second * keep_column
    later = later_ref[0]
    value = halves(block)[0]
    feature_grad = nt(value, later)
    key_grad = nn((feature_grad * second_kept).astype(BF), back_first_ref[...]) + nn(
        (feature_grad * first).astype(BF), back_second_ref[...]
    )
    value_grad = nn((first * second).astype(BF), later)
    place = lanes(value_grad.shape)
    row = rows_of(value_grad.shape)
    count = block.shape[0]
    edge = edge_ref[...]
    last = taps_ref[1:2, :] * edge[0:1, :] + taps_ref[2:3, :] * edge[1:2, :]
    before_last = taps_ref[2:3, :] * edge[0:1, :]
    value_grad = value_grad + jnp.where(row == count - 1, last, jnp.where(row == count - 2, before_last, 0.0))
    part = part_ref[...].astype(F32)
    out_ref[:, :PAD] = (part[:, :PAD] + jnp.where(place < HEAD, value_grad, 0.0)).astype(BF)
    out_ref[:, PAD:] = (part[:, PAD:] + jnp.where(place < HEAD, 0.0, key_grad)).astype(BF)


def whole(shape):
    return pl.BlockSpec(shape, lambda *_: (0,) * len(shape))


def by_column(rows, width):
    return pl.BlockSpec((rows, width), lambda h: (0, h))


def by_head(shape):
    return pl.BlockSpec((1,) + shape, lambda h: (h, 0, 0))


def ffn_kernel(
    normed_ref, top_ref, rank_ref, top_rank_ref, rank_turned_ref, top_rank_turned_ref,
    gate_ref, up_ref, down_ref, expand_gate_ref, expand_up_ref, reduce_ref,
    feed_in_ref, back_in_ref, small_in_ref,
    feed_ref, back_ref, small_ref, expand_gate_grad_ref, expand_up_grad_ref, reduce_grad_ref,
):
    @pl.when(pl.program_id(0) == 0)
    def _():
        feed_ref[...] = feed_in_ref[...]
        back_ref[...] = back_in_ref[...]
        small_ref[...] = small_in_ref[...]

    normed = normed_ref[...]
    rank = rank_ref[...]
    width = normed.shape[1]
    gate, up, down = (r[...].reshape(-1, width) for r in (gate_ref, up_ref, down_ref))
    expand_gate, expand_up, reduce = expand_gate_ref[0], expand_up_ref[0], reduce_ref[0]
    gating = nt(normed, gate) + nn(rank, expand_gate)
    upward = nt(normed, up) + nn(rank, expand_up)
    hidden_grad = nt(top_ref[...], down) + nn(top_rank_ref[...], reduce)
    sig = sigmoid(gating)
    silu = gating * sig
    hidden = (silu * upward).astype(BF)
    up_grad = (hidden_grad * silu).astype(BF)
    gate_grad = (hidden_grad * upward * (sig + silu * (1.0 - sig))).astype(BF)
    feed_ref[...] += nn(hidden, down)
    back_ref[...] += nn(gate_grad, gate) + nn(up_grad, up)
    small_ref[0] += nt(hidden, reduce)
    small_ref[1] += nt(gate_grad, expand_gate) + nt(up_grad, expand_up)
    expand_gate_grad_ref[0] = nn(rank_turned_ref[...], gate_grad)
    expand_up_grad_ref[0] = nn(rank_turned_ref[...], up_grad)
    reduce_grad_ref[0] = nn(top_rank_turned_ref[...], hidden)


def ffn_part(normed, top, rank, top_rank, weights, weight_specs, tables, feed, back, small):
    rows, width = normed.shape
    ranks = rank.shape[1]
    steps, _, step = tables[0].shape
    once = pl.Buffered(1)

    def fixed(shape):
        return pl.BlockSpec(shape, lambda *_: (0,) * len(shape), pipeline_mode=once)

    by_step = pl.BlockSpec((1, ranks, step), lambda n: (n, 0, 0))
    return pl.pallas_call(
        ffn_kernel,
        grid=(steps,),
        in_specs=[
            fixed((rows, width)), fixed((rows, width)), fixed((rows, ranks)), fixed((rows, ranks)),
            fixed((ranks, rows)), fixed((ranks, rows)),
            *weight_specs,
            by_step, by_step, by_step,
            fixed((rows, width)), fixed((rows, width)), fixed((2, rows, ranks)),
        ],
        out_specs=[
            fixed((rows, width)), fixed((rows, width)), fixed((2, rows, ranks)),
            by_step, by_step, by_step,
        ],
        out_shape=[
            jax.ShapeDtypeStruct((rows, width), F32),
            jax.ShapeDtypeStruct((rows, width), F32),
            jax.ShapeDtypeStruct((2, rows, ranks), F32),
        ]
        + [jax.ShapeDtypeStruct((steps, ranks, step), F32)] * 3,
        input_output_aliases={12: 0, 13: 1, 14: 2},
        name="ffn_part",
    )(normed, top, rank, top_rank, rank.T, top_rank.T, *weights, *tables, feed, back, small)


def rms(values, gain):
    inverse = lax.rsqrt(jnp.mean(values * values, axis=-1, keepdims=True) + EPSILON)
    return values * inverse * gain


def rms_back(values, gain, upstream):
    inverse = lax.rsqrt(jnp.mean(values * values, axis=-1, keepdims=True) + EPSILON)
    scaled = upstream * gain
    mean = jnp.mean(values * scaled, axis=-1, keepdims=True)
    return inverse * scaled - values * (inverse * inverse * inverse) * mean


def dot(left, right, dims=((1,), (0,))):
    return lax.dot_general(left, right, (dims, ((), ())), preferred_element_type=F32)


ROWS = ((0,), (0,))
TURNED = ((1,), (1,))


def pad_heads(table):
    lead = table.shape[:-1]
    split = table.reshape(lead + (-1, HEAD))
    padded = jnp.pad(split, [(0, 0)] * len(lead) + [(0, 0), (0, PAD - HEAD)])
    return padded.reshape(lead + (-1,))


def unpad_heads(table):
    lead = table.shape[:-1]
    return table.reshape(lead + (-1, PAD))[..., :HEAD].reshape(lead + (-1,))


def after(value, *others):
    return lax.optimization_barrier((value,) + others)[0]


SWAP = [(0, 1), (1, 0)]


def on_device(
    tokens, cotangent, lengths, adapter_ids, gain_first, gain_second, conv_kernel, mixer_in, mixer_out, gate_up,
    down_weight, inward_down, inward_up, outward_down, outward_up, expand_down, expand_up, reduce_down, reduce_up,
):
    sequences, slot_rows, width = tokens.shape
    ways = lax.axis_size("wa")
    chips = lax.axis_size("g") * 4
    chip = lax.axis_index(CHIPS)
    core = lax.axis_index("c")
    place = lax.axis_index("wa")
    plane = lax.axis_index(PLANE)
    sequence = core * ways + place
    rows = slot_rows * sequences
    ranks = inward_down.shape[1]
    adapters = inward_down.shape[0]
    in_width = mixer_in.shape[1]
    out_here = mixer_out.shape[0]
    out_width = out_here // HEAD * PAD
    hidden_here = down_weight.shape[0]
    piece_rows = -(-hidden_here // 128) * 16
    hidden_gap = 8 * piece_rows - hidden_here
    gap_at = 7 * piece_rows
    slice_rows = width // 8
    next_place = [((d + 1) % ways, d) for d in range(ways)]
    last_place = [(d, (d + 1) % ways) for d in range(ways)]
    first, second, ones, order = constants()
    barrier = lax.optimization_barrier

    def reorder(columns):
        heads = range(0, columns.shape[1], PACK)
        return jnp.concatenate([dot(columns[:, h : h + PACK], order).astype(BF) for h in heads], axis=1)

    def from_next(piece):
        return lax.ppermute(piece, "wa", next_place)

    def from_last(piece):
        return lax.ppermute(piece, "wa", last_place)

    def opposite(next_piece, last_piece):
        half = next_piece.shape[0] // 2
        return from_next(next_piece[:half]), from_last(last_piece[half:])

    def plane_all(piece):
        return lax.all_gather(piece, PLANE, axis=0, tiled=True)

    def column_exchange(values):
        return lax.all_to_all(values, COLUMN, 0, 0, tiled=True).reshape(rows, width)

    own_in = reorder(lax.dynamic_slice_in_dim(mixer_in, plane * slice_rows, slice_rows, 0))
    own_out = pad_heads(lax.dynamic_slice_in_dim(mixer_out, plane * slice_rows, slice_rows, 1).T)
    mixer_slice = jnp.concatenate([own_in, own_out], axis=1)
    turned_gate_up = jnp.swapaxes(gate_up, 1, 2)
    start = jnp.minimum(plane * piece_rows, hidden_here - piece_rows)
    fresh = plane * piece_rows <= start + jnp.arange(piece_rows)
    gate_up_slice = lax.dynamic_slice(turned_gate_up, (0, start, 0), (2, piece_rows, width))
    down_slice = lax.dynamic_slice_in_dim(down_weight, start, piece_rows, 0)
    ffn_slice = jnp.concatenate([gate_up_slice.reshape(2 * piece_rows, width), down_slice], axis=0)
    ffn_slice = jnp.where(jnp.tile(fresh, 3)[:, None], ffn_slice, 0).astype(BF)

    own_tables = (inward_up, outward_down, expand_up.reshape(adapters, ranks, -1), reduce_down)

    def tables_for(target):
        which = adapter_ids[target]
        return jnp.concatenate(
            [lax.dynamic_index_in_dim(t, which, 0, keepdims=False) for t in own_tables], axis=1
        )

    mixer_1, mixer_3 = barrier((from_next(mixer_slice), from_last(mixer_slice)))
    held = barrier(opposite(mixer_1, mixer_3) + (tokens,))
    mixer_2, tokens_in = jnp.concatenate(held[:2], axis=0), held[2]
    tables = [tables_for(sequence)]
    for j in range(1, ways):
        pairs = [(s, (s - j) % ways) for s in range(ways)]
        tables.append(lax.ppermute(tables_for(core * ways + (place - j) % ways), "wa", pairs))
    mixer_parts = (mixer_1, mixer_2, mixer_3)
    gathered_mixer = plane_all(
        jnp.concatenate([m[:, :in_width] for m in mixer_parts] + [m[:, in_width:] for m in mixer_parts], axis=1)
    )
    cut = [in_width, out_here, hidden_here, hidden_here, hidden_here]
    edges = np.cumsum([0] + cut)
    split_tables = [[t[:, edges[n] : edges[n + 1]] for n in range(5)] for t in tables]
    inward_second = [reorder(t[0]) for t in split_tables]
    outward_first = jnp.concatenate([pad_heads(t[1]) for t in split_tables], axis=1)
    held = barrier(
        (column_exchange(tokens_in), ffn_slice, reorder(mixer_in), pad_heads(mixer_out.T), outward_first)
        + tuple(inward_second)
    )
    x, ffn_slice, in_own, out_own, outward_first = held[:5]
    inward_rest, inward_second = jnp.concatenate(held[6:], axis=1), jnp.concatenate(held[5:], axis=1)
    ffn_1 = from_next(ffn_slice)
    in_split = (ways - 1) * in_width
    in_weights = (in_own, gathered_mixer[:, :in_split])
    out_weights = (out_own, gathered_mixer[:, in_split:])

    which = adapter_ids[sequence]

    def pick(table):
        return lax.dynamic_index_in_dim(table, which, 0, keepdims=False)

    inward_first, outward_second = pick(inward_down), pick(outward_up)
    expand_first, reduce_second = pick(expand_down), pick(reduce_up)
    positions = chip * rows + jnp.arange(rows, dtype=jnp.int32)
    keep = (positions < lengths[sequence]).astype(F32)
    keep_row, keep_column = keep[None, :], keep[:, None]

    inputs = x.astype(F32)
    normed = rms(inputs, gain_first).astype(BF)
    enter = dot(normed, inward_first, TURNED).astype(BF)
    packed_own = (dot(normed, in_own) + dot(enter, held[5])).astype(BF)
    ffn_1, packed_own, ffn_slice = barrier((ffn_1, packed_own, ffn_slice))
    gathered_1 = plane_all(ffn_1)
    ffn_3 = from_last(ffn_slice)
    packed_rest = (dot(normed, in_weights[1]) + dot(enter, inward_rest)).astype(BF)
    packed = jnp.concatenate([packed_own, packed_rest], axis=1)
    taps = pad_heads(jnp.roll(conv_kernel.astype(F32), -place * out_here, axis=1))
    taps = jnp.pad(taps, ((0, 5), (0, 0)))

    def chip_shift(piece, by):
        pairs = [(i, i + by) for i in range(chips) if 0 <= i + by < chips]
        return lax.ppermute(piece, CHIPS, pairs)

    halo = chip_shift(packed[-8:], 1)

    def flip(piece, bit):
        return lax.ppermute(piece, CHIPS, [(i, i ^ bit) for i in range(chips)])

    def scan_chips(local, want_bit):
        before = jnp.zeros_like(local)
        total = local
        bit = 1
        while bit < chips:
            got = flip(total.astype(BF), bit).astype(F32)
            take = ((chip & bit) != 0) == want_bit
            before = before + jnp.where(take, got, 0.0)
            total = total + got
            bit *= 2
        return before.astype(BF)

    pairs_shape = (PAIRS, PAD)
    ones_column = ones.T
    head_params = pltpu.CompilerParams(dimension_semantics=("arbitrary",))
    packed_spec, head_spec = by_column(rows, PACK), by_column(rows, PAD)
    halo_spec, edge_spec, state_spec = by_column(8, PACK), by_column(8, PAD), by_head(pairs_shape)
    turn_specs = [whole((PAIRS, PAD)), whole((PAIRS, PAD)), whole((PAIRS, 3))]
    pick_specs = [whole((PAD, PAIRS)), whole((PAD, PAIRS))]
    back_specs = [whole((PAIRS, PAD)), whole((PAIRS, PAD)), whole((3, PAIRS))]
    narrow = jax.ShapeDtypeStruct((rows, HEADS * PAD), BF)
    packed_shape = jax.ShapeDtypeStruct((rows, HEADS * PACK), BF)
    state_shape = jax.ShapeDtypeStruct((HEADS,) + pairs_shape, F32)

    state = pl.pallas_call(
        state_kernel,
        grid=(HEADS,),
        in_specs=[packed_spec, whole((1, rows))] + turn_specs,
        out_specs=state_spec,
        out_shape=state_shape,
        compiler_params=head_params,
        name="state",
    )(packed, keep_row, first.T, second.T, ones_column)
    ffn_3, cot_in = barrier((ffn_3, cotangent, state))[:2]
    gathered_3 = plane_all(ffn_3)
    cot = column_exchange(cot_in)
    before = scan_chips(state, True)
    inside = pl.pallas_call(
        inside_kernel,
        grid=(HEADS,),
        in_specs=[packed_spec, whole((rows, 1))],
        out_specs=head_spec,
        out_shape=jax.ShapeDtypeStruct((rows, HEADS * PAD), F32),
        compiler_params=head_params,
        name="inside",
    )(packed, keep_column)
    mixed, kept = pl.pallas_call(
        mixer_kernel,
        grid=(HEADS,),
        in_specs=[packed_spec, head_spec, state_spec, halo_spec, edge_spec] + pick_specs + [whole((3, PAIRS))],
        out_specs=[head_spec, head_spec],
        out_shape=[narrow, narrow],
        compiler_params=head_params,
        name="mixer",
    )(packed, inside, before, halo, taps, first, second, ones)

    side_1, side_3, cot = barrier((ffn_1, ffn_3, cot))
    far_parts = opposite(side_1, side_3)
    leave = dot(mixed, outward_first, TURNED).astype(BF)
    residual = inputs + dot(mixed[:, :out_width], out_weights[0], TURNED) + dot(mixed[:, out_width:], out_weights[1], TURNED) + dot(leave, outward_second)
    normed_two = rms(residual, gain_second).astype(BF)
    expand = dot(normed_two, expand_first, TURNED).astype(BF)
    top = jnp.where(keep_column > 0, cot, jnp.zeros_like(cot))
    top_rank = dot(top, reduce_second, TURNED).astype(BF)

    feed = jnp.zeros((rows, width), F32)
    back = jnp.zeros((rows, width), F32)
    small = jnp.zeros((2, rows, ranks), F32)

    def own_spec(which):
        return pl.BlockSpec((1, hidden_here // 2, width), lambda n: (which, n, 0))

    def piece_spec(which):
        return pl.BlockSpec((4, 1, piece_rows, width), lambda n: (n, which, 0, 0))

    specs_for = [piece_spec(t) for t in range(3)]

    def parts_of(gathered):
        return (gathered.reshape(8, 3, piece_rows, width),) * 3

    plans = [
        (0, (turned_gate_up, turned_gate_up, down_weight[None]), [own_spec(0), own_spec(1), own_spec(0)]),
        (1, parts_of(gathered_1), specs_for),
        (3, parts_of(gathered_3), specs_for),
        (2, None, specs_for),
    ]
    expand_grads = [None] * ways
    for j, weights, specs in plans:
        if j == 1:
            held = barrier((feed,) + far_parts)
            feed, gathered_far = held[0], plane_all(jnp.concatenate(held[1:], axis=0))
        if j == 2:
            weights = parts_of(gathered_far)
        chosen = jnp.stack(split_tables[j][2:5])
        if j > 0:
            empty = jnp.zeros((3, ranks, hidden_gap), BF)
            chosen = jnp.concatenate([chosen[..., :gap_at], empty, chosen[..., gap_at:]], axis=2)
        chosen = jnp.swapaxes(chosen.reshape(3, ranks, 2, -1), 1, 2)
        feed, back, small, *grads = ffn_part(
            normed_two, top, expand, top_rank, weights, specs, chosen, feed, back, small
        )
        grads = jnp.swapaxes(jnp.stack(grads), 1, 2).reshape(3, ranks, -1)
        if j > 0:
            grads = jnp.concatenate([grads[..., :gap_at], grads[..., gap_at + hidden_gap :]], axis=2)
        expand_grads[j] = [grads[0], grads[1], grads[2]]
    reduce_rank = small[0].astype(BF)
    output = keep_column * (residual + feed + dot(reduce_rank, reduce_second))
    expand_grad = small[1].astype(BF)
    back = back + dot(expand_grad, expand_first)
    grad_reduce_up = dot(reduce_rank, top, ROWS)
    grad_expand_down = dot(expand_grad, normed_two, ROWS)
    residual_grad = top.astype(F32) + rms_back(residual, gain_second, back)
    branch = residual_grad.astype(BF)
    leave_grad = dot(branch, outward_second, TURNED).astype(BF)
    grad_outward_up = dot(leave, branch, ROWS)
    mixed_grad = jnp.concatenate(
        [
            (dot(branch, w) + dot(leave_grad, t)).astype(BF)
            for w, t in zip(out_weights, (outward_first[:, :out_width], outward_first[:, out_width:]))
        ],
        axis=1,
    )
    grad_outward_down = unpad_heads(dot(leave_grad, mixed, ROWS))

    scaled, back_state, edge = pl.pallas_call(
        back_state_kernel,
        grid=(HEADS,),
        in_specs=[packed_spec, head_spec, head_spec] + turn_specs,
        out_specs=[head_spec, state_spec, edge_spec],
        out_shape=[narrow, state_shape, jax.ShapeDtypeStruct((8, HEADS * PAD), F32)],
        compiler_params=head_params,
        name="back_state",
    )(packed, kept, mixed_grad, first.T, second.T, ones_column)
    later = scan_chips(back_state, False)
    edge = chip_shift(edge, -1)
    part = pl.pallas_call(
        back_inside_kernel,
        grid=(HEADS,),
        in_specs=[packed_spec, head_spec, head_spec, whole((rows, 1)), state_spec, halo_spec, edge_spec]
        + pick_specs
        + back_specs,
        out_specs=packed_spec,
        out_shape=packed_shape,
        compiler_params=head_params,
        name="back_inside",
    )(packed, scaled, mixed_grad, keep_column, before, halo, taps, first, second, first.T, second.T, ones)
    packed_grad = pl.pallas_call(
        back_later_kernel,
        grid=(HEADS,),
        in_specs=[packed_spec, packed_spec, whole((rows, 1)), state_spec, edge_spec, edge_spec]
        + pick_specs
        + back_specs,
        out_specs=packed_spec,
        out_shape=packed_shape,
        compiler_params=head_params,
        name="back_later",
    )(packed, part, keep_column, later, edge, taps, first, second, first.T, second.T, ones)

    enter_grad = dot(packed_grad, inward_second, TURNED).astype(BF)
    normed_grad = (
        dot(packed_grad[:, :in_width], in_weights[0], TURNED)
        + dot(packed_grad[:, in_width:], in_weights[1], TURNED)
        + dot(enter_grad, inward_first)
    )
    input_grad = (branch.astype(F32) + rms_back(inputs, gain_first, normed_grad)).astype(BF)
    input_grad, packed_late = barrier((input_grad, packed_grad))
    grad_inward_up = dot(dot(enter, packed_late, ROWS).astype(BF).reshape(-1, PACK), order, TURNED).astype(BF)
    grad_inward_up = grad_inward_up.reshape(ranks, -1)
    grad_inward_down = dot(after(enter_grad, packed_late), normed, ROWS)

    def send_back(values):
        pieces = values.astype(BF).reshape(sequences, slot_rows, width)
        return lax.all_to_all(pieces, COLUMN, 0, 0, tiled=True).astype(F32)

    hot = (jnp.arange(adapters, dtype=jnp.int32)[:, None] == adapter_ids[None, :]).astype(F32)
    hot = hot.reshape(adapters, 2, ways)
    hot = jnp.where(core == 0, hot, hot[:, ::-1])
    turned = [lax.dynamic_index_in_dim(hot, (place - j) % ways, 2, keepdims=False) for j in range(ways)]
    hot = jnp.stack(turned, axis=2).reshape(adapters, 2 * ways)

    def exchange(pieces):
        got = [pieces(0).astype(BF)]
        for j in range(1, ways):
            pairs = [(s, (s + j) % ways) for s in range(ways)]
            got.append(lax.ppermute(pieces(j).astype(BF), "wa", pairs))
        summed = jnp.stack(got)
        bit = 1
        while bit < chips:
            summed = (summed.astype(F32) + flip(summed, bit).astype(F32)).astype(BF)
            bit *= 2
        both = jnp.concatenate([summed, lax.ppermute(summed, "c", SWAP)], axis=0).astype(F32)
        return jnp.tensordot(hot, both, axes=1, precision=lax.Precision.HIGHEST)

    shard = width // ways

    def shard_of(table, j):
        return lax.dynamic_slice_in_dim(table, (place + j) % ways * shard, shard, 1)

    early = exchange(
        lambda j: after(jnp.concatenate(
            expand_grads[j]
            + [
                grad_outward_down[:, j * out_here : (j + 1) * out_here],
                shard_of(grad_outward_up, j),
                shard_of(grad_expand_down, j),
                shard_of(grad_reduce_up, j),
            ],
            axis=1,
        ), scaled)
    )
    late = exchange(
        lambda j: jnp.concatenate(
            [grad_inward_up[:, j * in_width : (j + 1) * in_width], shard_of(grad_inward_down, j)], axis=1
        )
    )
    at = np.cumsum([0, 2 * hidden_here, hidden_here, out_here, shard, shard, shard])
    early_parts = [early[:, :, at[n] : at[n + 1]] for n in range(6)]
    return (
        send_back(output),
        send_back(input_grad),
        late[:, :, in_width:],
        late[:, :, :in_width],
        early_parts[2],
        early_parts[3],
        early_parts[4],
        early_parts[0].reshape(adapters, ranks, 2, hidden_here),
        early_parts[1],
        early_parts[5],
    )


def solution(mesh):
    ways = mesh.shape["wa"]
    split = Mesh(mesh.devices.reshape(-1, 2, 2, 2, ways), EVERY)
    slots = P(None, EVERY, None)
    in_specs = (
        slots, slots, P(), P(), P(), P(), P(),
        P(None, "wa"), P("wa", None), P(None, None, "wa"), P("wa", None),
        P(), P(None, None, "wa"), P(None, None, "wa"), P(), P(), P(None, None, None, "wa"), P(None, None, "wa"), P(),
    )
    third = P(None, None, "wa")
    out_specs = (slots, slots, third, third, third, third, third, P(None, None, None, "wa"), third, third)
    return jax.shard_map(on_device, mesh=split, in_specs=in_specs, out_specs=out_specs, check_vma=False)
```

time: 848 us -> 734 us (0.87)
  waiting for transfers between devices: 271 us -> 207 us
  local copies, waits for them, and re-layouts: 119 us -> 65.1 us
  Pallas kernels: 202 us -> 224 us
  matrix products: 96.9 us -> 78.4 us
  starting transfers between devices: 77.4 us -> 64.4 us
  other arithmetic: 50.5 us -> 61 us
    psum x1 -> x0, waiting for transfers between devices: 54.8 us -> none  [exchange(): summed = lax.psum(jnp.stack(got).astype(BF), CHIPS)]
    all_to_all x2, waiting for transfers between devices: 0.01 us -> 39.7 us  [column_exchange(): return lax.all_to_all(values, COLUMN, 0, 0, tiled=True).reshape(rows, width)]
    ppermute x3, waiting for transfers between devices: 39.1 us -> 0.01 us  [on_device(): lax.ppermute(tables_for(core * ways + (place - j) % ways), 'wa', pairs)]
    unnamed x207 -> x201, local copies, waits for them, and re-layouts: 50.1 us -> 17.5 us
    slice x18 -> x17, local copies, waits for them, and re-layouts: 32.7 us -> 5.68 us  [the longest x4 4.04 us: opposite(): return (from_next(next_piece[:half]), from_last(last_piece[half:]))]
    ppermute x18 -> x24, waiting for transfers between devices: 177 us -> 155 us  [the longest x4 64.4 us: from_next(): return lax.ppermute(piece, 'wa', next_place)]
    dot_general x31 -> x53, matrix products: 95 us -> 76.4 us  [dot(): lax.dot_general(left, right, (dims, ((), ())), preferred_element_type=F32)]
    pallas_call x4, Pallas kernels: 107 us -> 122 us  [ffn_part(): pl.pallas_call(ffn_kernel, grid=(steps,), in_specs=[fixed((rows, width)),...]
  transfers between devices with their start and end apart: 34 -> 37, of which waited for: 13 -> 19; matrix products, arithmetic and copies ran while one was open for 26% -> 23% of each run, Pallas kernels for 19% -> 25%
where the time goes in v2:
time: 734 us; the launch traced here: 723 us
  Pallas kernels  224 us (31%)
  waiting for transfers between devices  207 us (28%)
  matrix products  78.4 us (11%)
  local copies, waits for them, and re-layouts  65.1 us (9%)
  starting transfers between devices  64.4 us (9%)
  other arithmetic  61 us (8%)
  between operations  23.8 us (3%)
    pallas_call x4, Pallas kernels, ffn_part(): pl.pallas_call(ffn_kernel, grid=(steps,), in_specs=[fixed((rows, width)),...  122 us
    dot_general x53, matrix products, dot(): lax.dot_general(left, right, (dims, ((), ())), preferred_element_type=F32)  76.4 us
    ppermute x4, waiting for transfers between devices, from_next(): return lax.ppermute(piece, 'wa', next_place)  64.4 us
    ppermute x8, waiting for transfers between devices, flip(): return lax.ppermute(piece, CHIPS, [(i, i ^ bit) for i in range(chips)])  48 us
    all_to_all x2, waiting for transfers between devices, column_exchange(): return lax.all_to_all(values, COLUMN, 0, 0, tiled=True).reshape(rows, width)  39.7 us
    ppermute x4, waiting for transfers between devices, from_last(): return lax.ppermute(piece, 'wa', last_place)  29.2 us
    pallas_call x1, Pallas kernels, on_device(): pl.pallas_call(back_inside_kernel, grid=(HEADS,), in_specs=[packed_spec,...  28 us
    unnamed x201, local copies, waits for them, and re-layouts  17.5 us
  transfers between devices with their start and end apart: 37, of which 19 were waited for; matrix products, arithmetic and copies ran while one was open for 23% of the time, Pallas kernels for 25%

profile of v2, /device:TPU:0, one launch (start us, length us, event | category | flops | bytes accessed | tf_op | source)
XLA Modules:
  0.0 723.4 jit_solution(11972165714416846188)
XLA Ops:
  13.4 5.1 collective-permute-start
  18.5 15.8 %collective-permute-done = bf16[224,1536]{1,0:T(8,128)(2,1)S(1)} collective-permute-done((bf16[224,1536]{1,0:T(8,128)(2,1)S(1)}, bf16[224,1536]{1,0:T(8,128)(2,1)S(1)}, u32[]{:S(2)}, u32[]{:S(2)}) %collective-permute-start) | collective-permute-done | bytes 688160 | tf_op jit(solution)/shard_map/ppermute | solution.py:426
  34.3 14.5 %collective-permute-done.1 = bf16[224,1536]{1,0:T(8,128)(2,1)S(1)} collective-permute-done((bf16[224,1536]{1,0:T(8,128)(2,1)S(1)}, bf16[224,1536]{1,0:T(8,128)(2,1)S(1)}, u32[]{:S(2)}, u32[]{:S(2)}) %collective-permute-start.1) | collective-permute-done | bytes 688160 | tf_op jit(solution)/shard_map/ppermute | solution.py:429
  51.1 14.2 %collective-permute-done.2 = bf16[112,1536]{1,0:T(8,128)(2,1)S(1)} collective-permute-done((bf16[112,1536]{1,0:T(8,128)(2,1)S(1)}, bf16[112,1536]{1,0:T(8,128)(2,1)S(1)}, u32[]{:S(2)}, u32[]{:S(2)}) %collective-permute-start.2) | collective-permute-done | bytes 344096 | tf_op jit(solution)/shard_map/ppermute | solution.py:426
  103.7 39.7 %all-to-all-done = bf16[8,64,1792]{2,1,0:T(8,128)(2,1)S(1)} async-done(((bf16[8,64,1792]{2,1,0:T(8,128)(2,1)}), bf16[8,64,1792]{2,1,0:T(8,128)(2,1)S(1)}, u32[]{:S(2)}, u32[]{:S(2)}) %all-to-all-start) | async-done | bytes 1835040 | tf_op jit(solution)/shard_map/all_to_all | solution.py:439
  149.3 34.4 %collective-permute-done.7 = bf16[480,1792]{1,0:T(8,128)(2,1)} collective-permute-done((bf16[480,1792]{1,0:T(8,128)(2,1)}, bf16[480,1792]{1,0:T(8,128)(2,1)}, u32[]{:S(2)}, u32[]{:S(2)}) %collective-permute-start.7) | collective-permute-done | bytes 1720352 | tf_op jit(solution)/shard_map/ppermute | solution.py:426
  186.2 8.7 %fusion.2 = f32[512,3072]{1,0:T(8,128)S(1)} fusion(bf16[1792,4608]{1,0:T(8,128)(2,1)} %all-gather.5.cloned.1.call-done, bf16[512,1792]{1,0:T(8,128)(2,1)S(1)} %bitcast.320, f32[1792]{0:T(1024)S(1)} %copy-done.78, f32[512]{0:T(512)S(1)} %get-tuple-element.286), kind=kOutput, calls=%fused_computation.2 | convolution fusion | flops 5640814592 | bytes 19145728 | tf_op jit(solution)/shard_map/dot_general | solution.py:367
  200.1 12.5 %state.1 = f32[16,160,128]{2,1,0:T(8,128)} custom-call(bf16[512,4096]{1,0:T(8,128)(2,1)} %pad_maximum_fusion.block_ref, f32[1,512]{1,0:T(1,128)} %compare_convert_fusion.keep_ref, bf16[160,128]{1,0:T(8,128)(2,1)} %constant.243.first_ref.back_first_ref, bf16[160,128]{1,0:T(8,128)(2,1)} %constant.244.second_ref.back_second_ref, f32[160,3]{1,0:T(8,128)} %constant.245.ones_ref), custom_call_target="tpu_custom_call" | custom-call | tf_op jit(solution)/shard_map/state/pallas_call | solution.py:543
  212.6 14.7 %collective-permute-done.11 = bf16[480,1792]{1,0:T(8,128)(2,1)} collective-permute-done((bf16[480,1792]{1,0:T(8,128)(2,1)}, bf16[480,1792]{1,0:T(8,128)(2,1)}, u32[]{:S(2)}, u32[]{:S(2)}) %collective-permute-start.11) | collective-permute-done | bytes 1720352 | tf_op jit(solution)/shard_map/ppermute | solution.py:429
  243.6 20.9 %collective-permute-done.8 = bf16[16,160,128]{2,1,0:T(8,128)(2,1)} collective-permute-done((bf16[16,160,128]{2,1,0:T(8,128)(2,1)}, bf16[16,160,128]{2,1,0:T(8,128)(2,1)}, u32[]{:S(2)}, u32[]{:S(2)}) %collective-permute-start.8) | collective-permute-done | bytes 655392 | tf_op jit(solution)/shard_map/ppermute | solution.py:517
  269.2 4.3 all-to-all-start.1
  277.6 14.6 %inside.1.inside_ref = f32[512,2048]{1,0:T(8,128)} custom-call(bf16[512,4096]{1,0:T(8,128)(2,1)} %pad_maximum_fusion.block_ref, f32[512,1]{1,0:T(8,128)} %fusion.55.keep_column_ref), custom_call_target="tpu_custom_call" | custom-call | tf_op jit(solution)/shard_map/inside/pallas_call | solution.py:556
  295.2 15.6 %mixer.1 = (bf16[512,2048]{1,0:T(8,128)(2,1)}, bf16[512,2048]{1,0:T(8,128)(2,1)}) custom-call(bf16[512,4096]{1,0:T(8,128)(2,1)} %pad_maximum_fusion.block_ref, f32[512,2048]{1,0:T(8,128)} %inside.1.inside_ref, bf16[16,160,128]{2,1,0:T(8,128)(2,1)} %fusion.34.state_ref, bf16[8,4096]{1,0:T(8,128)(2,1)} %copy-done.40, f32[8,2048]{1,0:T(8,128)} %pad.36.taps_ref, ...), custom_call_target="tpu_custom_call" | custom-call | tf_op jit(solution)/shard_map/mixer/pallas_call | solution.py:565
  317.1 6.0 multiply_reduce_fusion.1
  343.4 30.1 %ffn_part.4 = (f32[512,1792]{1,0:T(8,128)}, f32[512,1792]{1,0:T(8,128)}, f32[2,512,16]{2,1,0:T(8,128)}, f32[2,16,608]{2,1,0:T(8,128)}, f32[2,16,608]{2,1,0:T(8,128)}, /*index=5*/f32[2,16,608]{2,1,0:T(8,128)}) custom-call(bf16[512,1792]{1,0:T(8,128)(2,1)} %copy-done.4, ...), custom_call_target="tpu_custom_call", output_to_operand_aliasing={{0}: (12, {}), {1}: (13, {}), {2}: (14, {})} | custom-call | tf_op jit(solution)/shard_map/ffn_part/pallas_call | solution.py:329
  383.8 32.2 %ffn_part.5 = (f32[512,1792]{1,0:T(8,128)}, f32[512,1792]{1,0:T(8,128)}, f32[2,512,16]{2,1,0:T(8,128)}, f32[2,16,640]{2,1,0:T(8,128)}, f32[2,16,640]{2,1,0:T(8,128)}, /*index=5*/f32[2,16,640]{2,1,0:T(8,128)}) custom-call(bf16[512,1792]{1,0:T(8,128)(2,1)} %copy-done.4, ...), custom_call_target="tpu_custom_call", output_to_operand_aliasing={{0}: (12, {}), {1}: (13, {}), {2}: (14, {})} | custom-call | tf_op jit(solution)/shard_map/ffn_part/pallas_call | solution.py:329
  417.9 30.1 %ffn_part.6 = (f32[512,1792]{1,0:T(8,128)}, f32[512,1792]{1,0:T(8,128)}, f32[2,512,16]{2,1,0:T(8,128)}, f32[2,16,640]{2,1,0:T(8,128)}, f32[2,16,640]{2,1,0:T(8,128)}, /*index=5*/f32[2,16,640]{2,1,0:T(8,128)}) custom-call(bf16[512,1792]{1,0:T(8,128)(2,1)} %copy-done.4, ...), custom_call_target="tpu_custom_call", output_to_operand_aliasing={{0}: (12, {}), {1}: (13, {}), {2}: (14, {})} | custom-call | tf_op jit(solution)/shard_map/ffn_part/pallas_call | solution.py:329
  453.2 29.7 %ffn_part.7 = (f32[512,1792]{1,0:T(8,128)}, f32[512,1792]{1,0:T(8,128)}, f32[2,512,16]{2,1,0:T(8,128)}, f32[2,16,640]{2,1,0:T(8,128)}, f32[2,16,640]{2,1,0:T(8,128)}, /*index=5*/f32[2,16,640]{2,1,0:T(8,128)}) custom-call(bf16[512,1792]{1,0:T(8,128)(2,1)} %copy-done.4, ...), custom_call_target="tpu_custom_call", output_to_operand_aliasing={{0}: (12, {}), {1}: (13, {}), {2}: (14, {})} | custom-call | tf_op jit(solution)/shard_map/ffn_part/pallas_call | solution.py:329
  483.0 4.1 multiply_reduce_fusion
  495.9 5.0 fusion.4
  503.2 14.0 %back_state.1 = (bf16[512,2048]{1,0:T(8,128)(2,1)}, f32[16,160,128]{2,1,0:T(8,128)}, f32[8,2048]{1,0:T(8,128)}) custom-call(bf16[512,4096]{1,0:T(8,128)(2,1)} %pad_maximum_fusion.block_ref, bf16[512,2048]{1,0:T(8,128)(2,1)} %get-tuple-element.109.kept_ref, bf16[512,2048]{1,0:T(8,128)(2,1)} %pad_maximum_fusion.2.grad_ref, ...), custom_call_target="tpu_custom_call" | custom-call | tf_op jit(solution)/shard_map/back_state/pallas_call | solution.py:643
  525.6 10.7 %collective-permute-done.14 = bf16[16,160,128]{2,1,0:T(8,128)(2,1)S(1)} collective-permute-done((bf16[16,160,128]{2,1,0:T(8,128)(2,1)S(1)}, bf16[16,160,128]{2,1,0:T(8,128)(2,1)S(1)}, u32[]{:S(2)}, u32[]{:S(2)}) %collective-permute-start.14) | collective-permute-done | bytes 655392 | tf_op jit(solution)/shard_map/ppermute | solution.py:517
  542.3 4.9 all-to-all-start.2
  547.1 28.0 %back_inside.1.part_ref = bf16[512,4096]{1,0:T(8,128)(2,1)} custom-call(bf16[512,4096]{1,0:T(8,128)(2,1)} %pad_maximum_fusion.block_ref, bf16[512,2048]{1,0:T(8,128)(2,1)} %get-tuple-element.110.scaled_ref, bf16[512,2048]{1,0:T(8,128)(2,1)} %pad_maximum_fusion.2.grad_ref, f32[512,1]{1,0:T(8,128)} %fusion.55.keep_column_ref, ...), custom_call_target="tpu_custom_call" | custom-call | tf_op jit(solution)/shard_map/back_inside/pallas_call | solution.py:654
  580.8 16.7 %back_later.1 = bf16[512,4096]{1,0:T(8,128)(2,1)} custom-call(bf16[512,4096]{1,0:T(8,128)(2,1)} %pad_maximum_fusion.block_ref, bf16[512,4096]{1,0:T(8,128)(2,1)} %back_inside.1.part_ref, f32[512,1]{1,0:T(8,128)} %fusion.55.keep_column_ref, bf16[16,160,128]{2,1,0:T(8,128)(2,1)} %fusion.37.later_ref, f32[8,2048]{1,0:T(8,128)} %collective-permute-done.16.edge_ref, ...), custom_call_target="tpu_custom_call" | custom-call | tf_op jit(solution)/shard_map/back_later/pallas_call | solution.py:665
  602.7 10.4 %fusion = f32[512,1792]{1,0:T(8,128)} fusion(bf16[1792,4608]{1,0:T(8,128)(2,1)} %all-gather.5.cloned.1.call-done, bf16[512,4096]{1,0:T(8,128)(2,1)S(1)} %copy-done.11), kind=kOutput, calls=%fused_computation | convolution fusion | flops 5637144576 | bytes 17825792 | tf_op jit(solution)/shard_map/dot_general | solution.py:367
  613.1 4.5 fusion.17
  631.7 6.8 collective-permute-done.24
  652.2 6.3 collective-permute-done.26
  664.0 6.1 all-to-all-start.3
  672.0 8.2 %collective-permute-done.27 = bf16[4,16,5440]{2,0,1:T(4,128)(2,1)S(1)} collective-permute-done((bf16[4,16,5440]{2,0,1:T(4,128)(2,1)S(1)}, bf16[4,16,5440]{2,0,1:T(4,128)(2,1)S(1)}, u32[]{:S(2)}, u32[]{:S(2)}) %collective-permute-start.27) | collective-permute-done | bytes 696352 | tf_op jit(solution)/shard_map/ppermute | solution.py:517
  704.5 8.5 %all-to-all-done.3 = bf16[8,64,1792]{2,1,0:T(8,128)(2,1)} async-done(((bf16[8,64,1792]{2,1,0:T(8,128)(2,1)}), bf16[8,64,1792]{2,1,0:T(8,128)(2,1)}, u32[]{:S(2)}, u32[]{:S(2)}) %all-to-all-start.3) | async-done | bytes 1835040 | tf_op jit(solution)/shard_map/all_to_all | solution.py:691
  (483 shorter events, 222.1 us)
Async XLA Ops:
  7.2 179.0 %all-gather.5.cloned.1.call-start = ((), (), s32[]{:S(2)}) async-start(), calls=%async_computation.4 | async-start | bytes 18579456 | tf_op jit(solution)/shard_map/all_gather | solution.py:436
  13.4 20.9 %collective-permute-start = (bf16[224,1536]{1,0:T(8,128)(2,1)S(1)}, bf16[224,1536]{1,0:T(8,128)(2,1)S(1)}, u32[]{:S(2)}, u32[]{:S(2)}) collective-permute-start(bf16[224,1536]{1,0:T(8,128)(2,1)S(1)} %bitcast_dynamic-update-slice_fusion), channel_id=1, source_target_pairs={{1,0},{2,1},{3,2},{0,3},{5,4},{6,5},{7,6},{4,7},{9,8},{10,9},{11,1... | collective-permute-start | bytes 2064392 | tf_op jit(solution)/shard_map/ppermute | solution.py:426
  18.5 30.3 %collective-permute-start.1 = (bf16[224,1536]{1,0:T(8,128)(2,1)S(1)}, bf16[224,1536]{1,0:T(8,128)(2,1)S(1)}, u32[]{:S(2)}, u32[]{:S(2)}) collective-permute-start(bf16[224,1536]{1,0:T(8,128)(2,1)S(1)} %bitcast_dynamic-update-slice_fusion), channel_id=1, source_target_pairs={{0,1},{1,2},{2,3},{3,0},{4,5},{5,6},{6,7},{7,4},{8,9},{9,10},{10,1... | collective-permute-start | bytes 2064392 | tf_op jit(solution)/shard_map/ppermute | solution.py:429
  48.9 16.4 %collective-permute-start.2 = (bf16[112,1536]{1,0:T(8,128)(2,1)S(1)}, bf16[112,1536]{1,0:T(8,128)(2,1)S(1)}, u32[]{:S(2)}, u32[]{:S(2)}) collective-permute-start(bf16[112,1536]{1,0:T(8,128)(2,1)S(1)} %slice.322), channel_id=1, source_target_pairs={{1,0},{2,1},{3,2},{0,3},{5,4},{6,5},{7,6},{4,7},{9,8},{10,9},{11,1... | collective-permute-start | bytes 1032200 | tf_op jit(solution)/shard_map/ppermute | solution.py:426
  50.7 14.5 %collective-permute-start.3 = (bf16[112,1536]{1,0:T(8,128)(2,1)S(1)}, bf16[112,1536]{1,0:T(8,128)(2,1)S(1)}, u32[]{:S(2)}, u32[]{:S(2)}) collective-permute-start(bf16[112,1536]{1,0:T(8,128)(2,1)S(1)} %slice.323), channel_id=1, source_target_pairs={{0,1},{1,2},{2,3},{3,0},{4,5},{5,6},{6,7},{7,4},{8,9},{9,10},{10,1... | collective-permute-start | bytes 1032200 | tf_op jit(solution)/shard_map/ppermute | solution.py:429
  79.0 17.4 %collective-permute-start.6 = (bf16[16,5120]{1,0:T(8,128)(2,1)S(1)}, bf16[16,5120]{1,0:T(8,128)(2,1)S(1)}, u32[]{:S(2)}, u32[]{:S(2)}) collective-permute-start(bf16[16,5120]{1,0:T(8,128)(2,1)S(1)} %concatenate.130), channel_id=1, source_target_pairs={{0,1},{1,2},{2,3},{3,0},{4,5},{5,6},{6,7},{7,4},{8,9},{9,10},{10,1... | collective-permute-start | bytes 491528 | tf_op jit(solution)/shard_map/ppermute | solution.py:466
  80.9 15.4 %collective-permute-start.5 = (bf16[16,5120]{1,0:T(8,128)(2,1)S(1)}, bf16[16,5120]{1,0:T(8,128)(2,1)S(1)}, u32[]{:S(2)}, u32[]{:S(2)}) collective-permute-start(bf16[16,5120]{1,0:T(8,128)(2,1)S(1)} %concatenate.129), channel_id=1, source_target_pairs={{0,2},{1,3},{2,0},{3,1},{4,6},{5,7},{6,4},{7,5},{8,10},{9,11},{10,... | collective-permute-start | bytes 491528 | tf_op jit(solution)/shard_map/ppermute | solution.py:466
  82.7 13.5 %collective-permute-start.4 = (bf16[16,5120]{1,0:T(8,128)(2,1)S(1)}, bf16[16,5120]{1,0:T(8,128)(2,1)S(1)}, u32[]{:S(2)}, u32[]{:S(2)}) collective-permute-start(bf16[16,5120]{1,0:T(8,128)(2,1)S(1)} %concatenate.128), channel_id=1, source_target_pairs={{0,3},{1,0},{2,1},{3,2},{4,7},{5,4},{6,5},{7,6},{8,11},{9,8},{10,9... | collective-permute-start | bytes 491528 | tf_op jit(solution)/shard_map/ppermute | solution.py:466
  96.6 46.8 %all-to-all-start = ((bf16[8,64,1792]{2,1,0:T(8,128)(2,1)}), bf16[8,64,1792]{2,1,0:T(8,128)(2,1)S(1)}, u32[]{:S(2)}, u32[]{:S(2)}) async-start(bf16[8,64,1792]{2,1,0:T(8,128)(2,1)} %param.23), calls=%async_computation | async-start | bytes 3670016 | tf_op jit(solution)/shard_map/all_to_all | solution.py:439
  100.6 283.2 %all-gather.11.cloned.1.call-start = ((), (), s32[]{:S(2)}) async-start(), calls=%async_computation.7 | async-start | bytes 15482880 | tf_op jit(solution)/shard_map/all_gather | solution.py:436
  143.4 40.2 %collective-permute-start.7 = (bf16[480,1792]{1,0:T(8,128)(2,1)}, bf16[480,1792]{1,0:T(8,128)(2,1)}, u32[]{:S(2)}, u32[]{:S(2)}) collective-permute-start(bf16[480,1792]{1,0:T(8,128)(2,1)} %maximum_select_fusion), channel_id=1, source_target_pairs={{1,0},{2,1},{3,2},{0,3},{5,4},{6,5},{7,6},{4,7},{9,8},{10,9},{11,1... | collective-permute-start | bytes 5160968 | tf_op jit(solution)/shard_map/ppermute | solution.py:426
  183.7 234.2 %all-gather.9.cloned.1.call-start = ((), (), s32[]{:S(2)}) async-start(), calls=%async_computation.6 | async-start | bytes 15482880 | tf_op jit(solution)/shard_map/all_gather | solution.py:436
  185.7 41.7 %collective-permute-start.11 = (bf16[480,1792]{1,0:T(8,128)(2,1)}, bf16[480,1792]{1,0:T(8,128)(2,1)}, u32[]{:S(2)}, u32[]{:S(2)}) collective-permute-start(bf16[480,1792]{1,0:T(8,128)(2,1)} %maximum_select_fusion), channel_id=1, source_target_pairs={{0,1},{1,2},{2,3},{3,0},{4,5},{5,6},{6,7},{7,4},{8,9},{9,10},{10,1... | collective-permute-start | bytes 5160968 | tf_op jit(solution)/shard_map/ppermute | solution.py:429
  233.4 31.2 %collective-permute-start.8 = (bf16[16,160,128]{2,1,0:T(8,128)(2,1)}, bf16[16,160,128]{2,1,0:T(8,128)(2,1)}, u32[]{:S(2)}, u32[]{:S(2)}) collective-permute-start(bf16[16,160,128]{2,1,0:T(8,128)(2,1)} %convert_element_type.328), channel_id=1, source_target_pairs={{0,8},{8,0},{16,24},{24,16},{1,9},{9,1},{17,25},{25,17},{2,10},{10... | collective-permute-start | bytes 1966088 | tf_op jit(solution)/shard_map/ppermute | solution.py:517
  267.0 25.2 %collective-permute-start.9 = (bf16[16,160,128]{2,1,0:T(8,128)(2,1)}, bf16[16,160,128]{2,1,0:T(8,128)(2,1)}, u32[]{:S(2)}, u32[]{:S(2)}) collective-permute-start(bf16[16,160,128]{2,1,0:T(8,128)(2,1)} %fusion.35), channel_id=1, source_target_pairs={{0,16},{8,24},{16,0},{24,8},{1,17},{9,25},{17,1},{25,9},{2,18},{10... | collective-permute-start | bytes 1966088 | tf_op jit(solution)/shard_map/ppermute | solution.py:517
  269.2 56.2 %all-to-all-start.1 = ((bf16[8,64,1792]{2,1,0:T(8,128)(2,1)}), bf16[8,64,1792]{2,1,0:T(8,128)(2,1)}, u32[]{:S(2)}, u32[]{:S(2)}) async-start(bf16[8,64,1792]{2,1,0:T(8,128)(2,1)} %param.24), calls=%async_computation.1 | async-start | bytes 3670016 | tf_op jit(solution)/shard_map/all_to_all | solution.py:439
  273.5 179.7 %all-gather.7.cloned.1.call-start = ((), (), s32[]{:S(2)}) async-start(), calls=%async_computation.5 | async-start | bytes 15482880 | tf_op jit(solution)/shard_map/all_gather | solution.py:436
  274.3 20.3 %collective-permute-start.10 = (bf16[8,4096]{1,0:T(8,128)(2,1)S(1)}, bf16[8,4096]{1,0:T(8,128)(2,1)S(1)}, u32[]{:S(2)}, u32[]{:S(2)}) collective-permute-start(bf16[8,4096]{1,0:T(8,128)(2,1)S(1)} %fusion.89), channel_id=1, source_target_pairs={{0,8},{8,16},{16,24},{1,9},{9,17},{17,25},{2,10},{10,18},{18,26},{... | collective-permute-start | bytes 196616 | tf_op jit(solution)/shard_map/ppermute | solution.py:512
  327.3 46.3 %collective-permute-start.12 = (bf16[240,1792]{1,0:T(8,128)(2,1)S(1)}, bf16[240,1792]{1,0:T(8,128)(2,1)}, u32[]{:S(2)}, u32[]{:S(2)}) collective-permute-start(bf16[240,1792]{1,0:T(8,128)(2,1)S(1)} %slice.360), channel_id=1, source_target_pairs={{1,0},{2,1},{3,2},{0,3},{5,4},{6,5},{7,6},{4,7},{9,8},{10,9},{11,1... | collective-permute-start | bytes 2580488 | tf_op jit(solution)/shard_map/ppermute | solution.py:426
  333.0 40.6 %collective-permute-start.13 = (bf16[240,1792]{1,0:T(8,128)(2,1)}, bf16[240,1792]{1,0:T(8,128)(2,1)}, u32[]{:S(2)}, u32[]{:S(2)}) collective-permute-start(bf16[240,1792]{1,0:T(8,128)(2,1)} %slice.361), channel_id=1, source_target_pairs={{0,1},{1,2},{2,3},{3,0},{4,5},{5,6},{6,7},{7,4},{8,9},{9,10},{10,1... | collective-permute-start | bytes 2580488 | tf_op jit(solution)/shard_map/ppermute | solution.py:429
  518.7 17.6 %collective-permute-start.14 = (bf16[16,160,128]{2,1,0:T(8,128)(2,1)S(1)}, bf16[16,160,128]{2,1,0:T(8,128)(2,1)S(1)}, u32[]{:S(2)}, u32[]{:S(2)}) collective-permute-start(bf16[16,160,128]{2,1,0:T(8,128)(2,1)S(1)} %convert_element_type.351), channel_id=1, source_target_pairs={{0,8},{8,0},{16,24},{24,16},{1,9},{9,1},{17,25},{25,17},{2,10},{10... | collective-permute-start | bytes 1966088 | tf_op jit(solution)/shard_map/ppermute | solution.py:517
  522.7 58.1 %collective-permute-start.16 = (f32[8,2048]{1,0:T(8,128)}, f32[8,2048]{1,0:T(8,128)}, u32[]{:S(2)}, u32[]{:S(2)}) collective-permute-start(f32[8,2048]{1,0:T(8,128)} %get-tuple-element.112), channel_id=1, source_target_pairs={{8,0},{16,8},{24,16},{9,1},{17,9},{25,17},{10,2},{18,10},{26,18},{... | collective-permute-start | bytes 196616 | tf_op jit(solution)/shard_map/ppermute | solution.py:512
  538.6 40.0 %collective-permute-start.15 = (bf16[16,160,128]{2,1,0:T(8,128)(2,1)}, bf16[16,160,128]{2,1,0:T(8,128)(2,1)}, u32[]{:S(2)}, u32[]{:S(2)}) collective-permute-start(bf16[16,160,128]{2,1,0:T(8,128)(2,1)} %fusion.38), channel_id=1, source_target_pairs={{0,16},{8,24},{16,0},{24,8},{1,17},{9,25},{17,1},{25,9},{2,18},{10... | collective-permute-start | bytes 1966088 | tf_op jit(solution)/shard_map/ppermute | solution.py:517
  542.3 121.7 %all-to-all-start.2 = ((bf16[8,64,1792]{2,1,0:T(8,128)(2,1)}), bf16[8,64,1792]{2,1,0:T(8,128)(2,1)}, u32[]{:S(2)}, u32[]{:S(2)}) async-start(bf16[8,64,1792]{2,1,0:T(8,128)(2,1)} %bitcast.69), calls=%async_computation.2 | async-start | bytes 3670016 | tf_op jit(solution)/shard_map/all_to_all | solution.py:691
  622.1 9.3 %collective-permute-start.23 = (bf16[16,5440]{1,0:T(8,128)(2,1)S(1)}, bf16[16,5440]{1,0:T(8,128)(2,1)S(1)}, u32[]{:S(2)}, u32[]{:S(2)}) collective-permute-start(bf16[16,5440]{1,0:T(8,128)(2,1)S(1)} %concatenate.157), channel_id=1, source_target_pairs={{0,1},{1,2},{2,3},{3,0},{4,5},{5,6},{6,7},{7,4},{8,9},{9,10},{10,1... | collective-permute-start | bytes 522248 | tf_op jit(solution)/shard_map/ppermute | solution.py:703
  624.4 14.1 %collective-permute-start.24 = (bf16[16,5440]{1,0:T(8,128)(2,1)S(1)}, bf16[16,5440]{1,0:T(8,128)(2,1)S(1)}, u32[]{:S(2)}, u32[]{:S(2)}) collective-permute-start(bf16[16,5440]{1,0:T(8,128)(2,1)S(1)} %concatenate.159), channel_id=1, source_target_pairs={{0,2},{1,3},{2,0},{3,1},{4,6},{5,7},{6,4},{7,5},{8,10},{9,11},{10,... | collective-permute-start | bytes 522248 | tf_op jit(solution)/shard_map/ppermute | solution.py:703
  626.9 11.8 %collective-permute-start.25 = (bf16[16,5440]{1,0:T(8,128)(2,1)S(1)}, bf16[16,5440]{1,0:T(8,128)(2,1)S(1)}, u32[]{:S(2)}, u32[]{:S(2)}) collective-permute-start(bf16[16,5440]{1,0:T(8,128)(2,1)S(1)} %concatenate.161), channel_id=1, source_target_pairs={{0,3},{1,0},{2,1},{3,2},{4,7},{5,4},{6,5},{7,6},{8,11},{9,8},{10,9... | collective-permute-start | bytes 522248 | tf_op jit(solution)/shard_map/ppermute | solution.py:703
  640.7 17.8 %collective-permute-start.26 = (bf16[4,16,5440]{2,0,1:T(4,128)(2,1)S(1)}, bf16[4,16,5440]{2,0,1:T(4,128)(2,1)}, u32[]{:S(2)}, u32[]{:S(2)}) collective-permute-start(bf16[4,16,5440]{2,0,1:T(4,128)(2,1)S(1)} %pad_maximum_fusion.4), channel_id=1, source_target_pairs={{0,8},{8,0},{16,24},{24,16},{1,9},{9,1},{17,25},{25,17},{2,10},{10... | collective-permute-start | bytes 2088968 | tf_op jit(solution)/shard_map/ppermute | solution.py:517
  661.4 18.7 %collective-permute-start.27 = (bf16[4,16,5440]{2,0,1:T(4,128)(2,1)S(1)}, bf16[4,16,5440]{2,0,1:T(4,128)(2,1)S(1)}, u32[]{:S(2)}, u32[]{:S(2)}) collective-permute-start(bf16[4,16,5440]{2,0,1:T(4,128)(2,1)S(1)} %add_convert_fusion.4), channel_id=1, source_target_pairs={{0,16},{8,24},{16,0},{24,8},{1,17},{9,25},{17,1},{25,9},{2,18},{10... | collective-permute-start | bytes 2088968 | tf_op jit(solution)/shard_map/ppermute | solution.py:517
  664.0 49.0 %all-to-all-start.3 = ((bf16[8,64,1792]{2,1,0:T(8,128)(2,1)}), bf16[8,64,1792]{2,1,0:T(8,128)(2,1)}, u32[]{:S(2)}, u32[]{:S(2)}) async-start(bf16[8,64,1792]{2,1,0:T(8,128)(2,1)} %bitcast.71), calls=%async_computation.3 | async-start | bytes 3670016 | tf_op jit(solution)/shard_map/all_to_all | solution.py:691
  670.7 11.8 %collective-permute-start.21 = (bf16[4,16,1472]{2,0,1:T(4,128)(2,1)S(1)}, bf16[4,16,1472]{2,0,1:T(4,128)(2,1)S(1)}, u32[]{:S(2)}, u32[]{:S(2)}) collective-permute-start(bf16[4,16,1472]{2,0,1:T(4,128)(2,1)S(1)} %add_convert_fusion.6), channel_id=1, source_target_pairs={{0,16},{8,24},{16,0},{24,8},{1,17},{9,25},{17,1},{25,9},{2,18},{10... | collective-permute-start | bytes 565256 | tf_op jit(solution)/shard_map/ppermute | solution.py:517
  680.5 9.8 %collective-permute-start.28 = (bf16[4,16,5440]{2,0,1:T(4,128)(2,1)S(1)}, bf16[4,16,5440]{2,0,1:T(4,128)(2,1)S(1)}, u32[]{:S(2)}, u32[]{:S(2)}) collective-permute-start(bf16[4,16,5440]{2,0,1:T(4,128)(2,1)S(1)} %add_convert_fusion.3), channel_id=1, source_target_pairs={{0,4},{4,0},{1,5},{5,1},{2,6},{6,2},{3,7},{7,3},{8,12},{12,8},{9,1... | collective-permute-start | bytes 2088968 | tf_op jit(solution)/shard_map/ppermute | solution.py:709
  (95 other events, 1555.6 us)
Sparse Core Ops, SparseCore 0:
  67.0 88.9 all-gather.4
  183.8 90.0 all-gather.10
  275.8 76.9 all-gather.8
  376.6 76.5 all-gather.6

commit v3 on v2

--- a/solution.py
+++ b/solution.py
@@ -282,18 +282,29 @@
     return pl.BlockSpec((1,) + shape, lambda h: (h, 0, 0))
 
 
-def ffn_kernel(
+def first_ffn_kernel(*refs):
+    @pl.when(pl.program_id(0) == 0)
+    def _():
+        for ref in refs[12:15]:
+            ref[...] = jnp.zeros_like(ref)
+
+    ffn_body(*refs)
+
+
+def later_ffn_kernel(*refs):
+    @pl.when(pl.program_id(0) == 0)
+    def _():
+        for old, ref in zip(refs[12:15], refs[15:18]):
+            ref[...] = old[...]
+
+    ffn_body(*refs[:12], *refs[15:])
+
+
+def ffn_body(
     normed_ref, top_ref, rank_ref, top_rank_ref, rank_turned_ref, top_rank_turned_ref,
     gate_ref, up_ref, down_ref, expand_gate_ref, expand_up_ref, reduce_ref,
-    feed_in_ref, back_in_ref, small_in_ref,
     feed_ref, back_ref, small_ref, expand_gate_grad_ref, expand_up_grad_ref, reduce_grad_ref,
 ):
-    @pl.when(pl.program_id(0) == 0)
-    def _():
-        feed_ref[...] = feed_in_ref[...]
-        back_ref[...] = back_in_ref[...]
-        small_ref[...] = small_in_ref[...]
-
     normed = normed_ref[...]
     rank = rank_ref[...]
     width = normed.shape[1]
@@ -316,7 +327,7 @@
     reduce_grad_ref[0] = nn(top_rank_turned_ref[...], hidden)
 
 
-def ffn_part(normed, top, rank, top_rank, weights, weight_specs, tables, feed, back, small):
+def ffn_part(normed, top, rank, top_rank, weights, weight_specs, tables, sums):
     rows, width = normed.shape
     ranks = rank.shape[1]
     steps, _, step = tables[0].shape
@@ -327,14 +338,14 @@
 
     by_step = pl.BlockSpec((1, ranks, step), lambda n: (n, 0, 0))
     return pl.pallas_call(
-        ffn_kernel,
+        later_ffn_kernel if sums else first_ffn_kernel,
         grid=(steps,),
         in_specs=[
             fixed((rows, width)), fixed((rows, width)), fixed((rows, ranks)), fixed((rows, ranks)),
             fixed((ranks, rows)), fixed((ranks, rows)),
             *weight_specs,
             by_step, by_step, by_step,
-            fixed((rows, width)), fixed((rows, width)), fixed((2, rows, ranks)),
+            *([fixed((rows, width)), fixed((rows, width)), fixed((2, rows, ranks))] if sums else []),
         ],
         out_specs=[
             fixed((rows, width)), fixed((rows, width)), fixed((2, rows, ranks)),
@@ -346,9 +357,9 @@
             jax.ShapeDtypeStruct((2, rows, ranks), F32),
         ]
         + [jax.ShapeDtypeStruct((steps, ranks, step), F32)] * 3,
-        input_output_aliases={12: 0, 13: 1, 14: 2},
+        input_output_aliases={12: 0, 13: 1, 14: 2} if sums else {},
         name="ffn_part",
-    )(normed, top, rank, top_rank, rank.T, top_rank.T, *weights, *tables, feed, back, small)
+    )(normed, top, rank, top_rank, rank.T, top_rank.T, *weights, *tables, *sums)
 
 
 def rms(values, gain):
@@ -428,10 +439,6 @@
     def from_last(piece):
         return lax.ppermute(piece, "wa", last_place)
 
-    def opposite(next_piece, last_piece):
-        half = next_piece.shape[0] // 2
-        return from_next(next_piece[:half]), from_last(last_piece[half:])
-
     def plane_all(piece):
         return lax.all_gather(piece, PLANE, axis=0, tiled=True)
 
@@ -457,32 +464,38 @@
             [lax.dynamic_index_in_dim(t, which, 0, keepdims=False) for t in own_tables], axis=1
         )
 
-    mixer_1, mixer_3 = barrier((from_next(mixer_slice), from_last(mixer_slice)))
-    held = barrier(opposite(mixer_1, mixer_3) + (tokens,))
-    mixer_2, tokens_in = jnp.concatenate(held[:2], axis=0), held[2]
-    tables = [tables_for(sequence)]
+    prepared = [tables_for(sequence)]
+    for j in range(1, ways):
+        prepared.append(tables_for(core * ways + (place - j) % ways))
+    held = barrier((from_next(mixer_slice), mixer_slice, ffn_slice) + tuple(prepared))
+    (mixer_1, mixer_slice, ffn_slice), prepared = held[:3], held[3:]
+    mixer_2, mixer_3 = from_next(mixer_1), from_last(mixer_slice)
+    gathered_near = plane_all(mixer_1)
+    tables = [prepared[0]]
     for j in range(1, ways):
         pairs = [(s, (s - j) % ways) for s in range(ways)]
-        tables.append(lax.ppermute(tables_for(core * ways + (place - j) % ways), "wa", pairs))
-    mixer_parts = (mixer_1, mixer_2, mixer_3)
-    gathered_mixer = plane_all(
-        jnp.concatenate([m[:, :in_width] for m in mixer_parts] + [m[:, in_width:] for m in mixer_parts], axis=1)
+        tables.append(lax.ppermute(prepared[j], "wa", pairs))
+    held = barrier((mixer_2, mixer_3, ffn_slice, pad_heads(mixer_out.T)) + tuple(tables[1:]))
+    (mixer_2, mixer_3, ffn_slice, out_own), tables[1:] = held[:4], held[4:]
+    gathered_rest = plane_all(
+        jnp.concatenate(
+            [mixer_2[:, :in_width], mixer_3[:, :in_width], mixer_2[:, in_width:], mixer_3[:, in_width:]], axis=1
+        )
     )
     cut = [in_width, out_here, hidden_here, hidden_here, hidden_here]
     edges = np.cumsum([0] + cut)
     split_tables = [[t[:, edges[n] : edges[n + 1]] for n in range(5)] for t in tables]
-    inward_second = [reorder(t[0]) for t in split_tables]
+    inward_second = reorder(jnp.concatenate([t[0] for t in split_tables], axis=1))
     outward_first = jnp.concatenate([pad_heads(t[1]) for t in split_tables], axis=1)
-    held = barrier(
-        (column_exchange(tokens_in), ffn_slice, reorder(mixer_in), pad_heads(mixer_out.T), outward_first)
-        + tuple(inward_second)
-    )
-    x, ffn_slice, in_own, out_own, outward_first = held[:5]
-    inward_rest, inward_second = jnp.concatenate(held[6:], axis=1), jnp.concatenate(held[5:], axis=1)
-    ffn_1 = from_next(ffn_slice)
-    in_split = (ways - 1) * in_width
-    in_weights = (in_own, gathered_mixer[:, :in_split])
-    out_weights = (out_own, gathered_mixer[:, in_split:])
+    ffn_1, tokens_in, in_own = barrier((from_next(ffn_slice), tokens, reorder(mixer_in)))
+    gathered_1 = plane_all(ffn_1)
+    in_split = (ways - 2) * in_width
+    in_weights = jnp.concatenate([in_own, gathered_near[:, :in_width], gathered_rest[:, :in_split]], axis=1)
+    out_weights = jnp.concatenate([out_own, gathered_near[:, in_width:], gathered_rest[:, in_split:]], axis=1)
+    x, ffn_slice, in_weights, out_weights, inward_second, outward_first = barrier(
+        (column_exchange(tokens_in), ffn_slice, in_weights, out_weights, inward_second, outward_first)
+    )
+    ffn_3 = from_last(ffn_slice)
 
     which = adapter_ids[sequence]
 
@@ -498,12 +511,7 @@
     inputs = x.astype(F32)
     normed = rms(inputs, gain_first).astype(BF)
     enter = dot(normed, inward_first, TURNED).astype(BF)
-    packed_own = (dot(normed, in_own) + dot(enter, held[5])).astype(BF)
-    ffn_1, packed_own, ffn_slice = barrier((ffn_1, packed_own, ffn_slice))
-    gathered_1 = plane_all(ffn_1)
-    ffn_3 = from_last(ffn_slice)
-    packed_rest = (dot(normed, in_weights[1]) + dot(enter, inward_rest)).astype(BF)
-    packed = jnp.concatenate([packed_own, packed_rest], axis=1)
+    packed = (dot(normed, in_weights) + dot(enter, inward_second)).astype(BF)
     taps = pad_heads(jnp.roll(conv_kernel.astype(F32), -place * out_here, axis=1))
     taps = jnp.pad(taps, ((0, 5), (0, 0)))
 
@@ -511,17 +519,21 @@
         pairs = [(i, i + by) for i in range(chips) if 0 <= i + by < chips]
         return lax.ppermute(piece, CHIPS, pairs)
 
-    halo = chip_shift(packed[-8:], 1)
-
-    def flip(piece, bit):
-        return lax.ppermute(piece, CHIPS, [(i, i ^ bit) for i in range(chips)])
-
-    def scan_chips(local, want_bit):
+
+    def flip(piece, bit, keep_pair=lambda i: True):
+        return lax.ppermute(piece, CHIPS, [(i, i ^ bit) for i in range(chips) if keep_pair(i)])
+
+    def scan_chips(local, sent, want_bit, ahead):
         before = jnp.zeros_like(local)
         total = local
         bit = 1
         while bit < chips:
-            got = flip(total.astype(BF), bit).astype(F32)
+            if bit > 1:
+                sent = total.astype(BF)
+            if bit == 2:
+                sent = ahead(sent)
+            last = 2 * bit >= chips
+            got = flip(sent, bit, lambda i: not last or ((i & bit) == 0) == want_bit).astype(F32)
             take = ((chip & bit) != 0) == want_bit
             before = before + jnp.where(take, got, 0.0)
             total = total + got
@@ -549,10 +561,12 @@
         compiler_params=head_params,
         name="state",
     )(packed, keep_row, first.T, second.T, ones_column)
-    ffn_3, cot_in = barrier((ffn_3, cotangent, state))[:2]
+    state_sent, last_rows = barrier((state.astype(BF), packed[-8:]))
+    ffn_3, cot_in, halo = barrier((ffn_3, cotangent, chip_shift(last_rows, 1)))
     gathered_3 = plane_all(ffn_3)
     cot = column_exchange(cot_in)
-    before = scan_chips(state, True)
+    before = scan_chips(state, state_sent, True, lambda sent: sent)
+    staged = []
     inside = pl.pallas_call(
         inside_kernel,
         grid=(HEADS,),
@@ -562,6 +576,8 @@
         compiler_params=head_params,
         name="inside",
     )(packed, keep_column)
+    ffn_1, cot, inside, before = barrier((ffn_1, cot, inside, before))
+    ffn_2 = from_next(ffn_1)
     mixed, kept = pl.pallas_call(
         mixer_kernel,
         grid=(HEADS,),
@@ -572,18 +588,14 @@
         name="mixer",
     )(packed, inside, before, halo, taps, first, second, ones)
 
-    side_1, side_3, cot = barrier((ffn_1, ffn_3, cot))
-    far_parts = opposite(side_1, side_3)
     leave = dot(mixed, outward_first, TURNED).astype(BF)
-    residual = inputs + dot(mixed[:, :out_width], out_weights[0], TURNED) + dot(mixed[:, out_width:], out_weights[1], TURNED) + dot(leave, outward_second)
+    residual = inputs + dot(mixed, out_weights, TURNED) + dot(leave, outward_second)
     normed_two = rms(residual, gain_second).astype(BF)
-    expand = dot(normed_two, expand_first, TURNED).astype(BF)
     top = jnp.where(keep_column > 0, cot, jnp.zeros_like(cot))
     top_rank = dot(top, reduce_second, TURNED).astype(BF)
-
-    feed = jnp.zeros((rows, width), F32)
-    back = jnp.zeros((rows, width), F32)
-    small = jnp.zeros((2, rows, ranks), F32)
+    normed_two, ffn_2, top, top_rank = barrier((normed_two, ffn_2, top, top_rank))
+    gathered_far = plane_all(ffn_2)
+    expand = dot(normed_two, expand_first, TURNED).astype(BF)
 
     def own_spec(which):
         return pl.BlockSpec((1, hidden_here // 2, width), lambda n: (which, n, 0))
@@ -600,29 +612,23 @@
         (0, (turned_gate_up, turned_gate_up, down_weight[None]), [own_spec(0), own_spec(1), own_spec(0)]),
         (1, parts_of(gathered_1), specs_for),
         (3, parts_of(gathered_3), specs_for),
-        (2, None, specs_for),
+        (2, parts_of(gathered_far), specs_for),
     ]
-    expand_grads = [None] * ways
+    expand_grads, sums = [None] * ways, ()
     for j, weights, specs in plans:
-        if j == 1:
-            held = barrier((feed,) + far_parts)
-            feed, gathered_far = held[0], plane_all(jnp.concatenate(held[1:], axis=0))
-        if j == 2:
-            weights = parts_of(gathered_far)
         chosen = jnp.stack(split_tables[j][2:5])
         if j > 0:
             empty = jnp.zeros((3, ranks, hidden_gap), BF)
             chosen = jnp.concatenate([chosen[..., :gap_at], empty, chosen[..., gap_at:]], axis=2)
         chosen = jnp.swapaxes(chosen.reshape(3, ranks, 2, -1), 1, 2)
-        feed, back, small, *grads = ffn_part(
-            normed_two, top, expand, top_rank, weights, specs, chosen, feed, back, small
-        )
+        *sums, g_gate, g_up, g_reduce = ffn_part(normed_two, top, expand, top_rank, weights, specs, chosen, tuple(sums))
+        sums, grads = tuple(sums), (g_gate, g_up, g_reduce)
         grads = jnp.swapaxes(jnp.stack(grads), 1, 2).reshape(3, ranks, -1)
         if j > 0:
             grads = jnp.concatenate([grads[..., :gap_at], grads[..., gap_at + hidden_gap :]], axis=2)
         expand_grads[j] = [grads[0], grads[1], grads[2]]
+    feed, back, small = sums
     reduce_rank = small[0].astype(BF)
-    output = keep_column * (residual + feed + dot(reduce_rank, reduce_second))
     expand_grad = small[1].astype(BF)
     back = back + dot(expand_grad, expand_first)
     grad_reduce_up = dot(reduce_rank, top, ROWS)
@@ -631,13 +637,7 @@
     branch = residual_grad.astype(BF)
     leave_grad = dot(branch, outward_second, TURNED).astype(BF)
     grad_outward_up = dot(leave, branch, ROWS)
-    mixed_grad = jnp.concatenate(
-        [
-            (dot(branch, w) + dot(leave_grad, t)).astype(BF)
-            for w, t in zip(out_weights, (outward_first[:, :out_width], outward_first[:, out_width:]))
-        ],
-        axis=1,
-    )
+    mixed_grad = (dot(branch, out_weights) + dot(leave_grad, outward_first)).astype(BF)
     grad_outward_down = unpad_heads(dot(leave_grad, mixed, ROWS))
 
     scaled, back_state, edge = pl.pallas_call(
@@ -649,19 +649,81 @@
         compiler_params=head_params,
         name="back_state",
     )(packed, kept, mixed_grad, first.T, second.T, ones_column)
-    later = scan_chips(back_state, False)
+    hot = (jnp.arange(adapters, dtype=jnp.int32)[:, None] == adapter_ids[None, :]).astype(F32)
+    hot = hot.reshape(adapters, 2, ways)
+    hot = jnp.where(core == 0, hot, hot[:, ::-1])
+    turned = [lax.dynamic_index_in_dim(hot, (place - j) % ways, 2, keepdims=False) for j in range(ways)]
+    turned = [lax.dynamic_index_in_dim(jnp.stack(turned, axis=2), (chip % 4) ^ k, 2, keepdims=False) for k in range(4)]
+    hot = jnp.stack(turned, axis=2).reshape(adapters, 8)
+    same_rank = jnp.eye(ranks, dtype=F32)[None, :, None, :]
+    hot_rows = (hot[:, None, :, None] * same_rank).reshape(adapters * ranks, 8 * ranks).astype(BF)
+
+    def exchange_places(pieces):
+        got = [pieces(0).astype(BF)]
+        for j in range(1, ways):
+            pairs = [(s, (s + j) % ways) for s in range(ways)]
+            got.append(lax.ppermute(pieces(j).astype(BF), "wa", pairs))
+        return jnp.stack(got)
+
+    def exchange_chips(table):
+        bit = 4
+        while bit < chips:
+            table = (table.astype(F32) + flip(table, bit).astype(F32)).astype(BF)
+            bit *= 2
+
+        def sequence_at(other):
+            return lax.dynamic_index_in_dim(table, (chip % 4) ^ other, 0, keepdims=False)
+
+        summed = sum([flip(sequence_at(k), k).astype(F32) for k in range(1, 4)], sequence_at(0).astype(F32)).astype(BF)
+        parts = jnp.concatenate([summed] + [flip(summed, k) for k in range(1, 4)], axis=0)
+        parts = jnp.concatenate([parts, lax.ppermute(parts, "c", SWAP)], axis=0)
+        return dot(hot_rows, parts).reshape(adapters, ranks, -1)
+
+    shard = width // ways
+
+    def shard_of(table, j):
+        return lax.dynamic_slice_in_dim(table, (place + j) % ways * shard, shard, 1)
+
+    any_space = pl.BlockSpec(memory_space=pl.ANY)
+
+    def back_inside(base, scaled, old):
+        def shift(spec):
+            return pl.BlockSpec(spec.block_shape, lambda h, m=spec.index_map: m(h + base))
+
+        return pl.pallas_call(
+            back_inside_kernel if old is None else lambda *refs: back_inside_kernel(*refs[:12], refs[-1]),
+            grid=(HEADS // 2,),
+            in_specs=[
+                shift(packed_spec), shift(head_spec), shift(head_spec), whole((rows, 1)),
+                shift(state_spec), shift(halo_spec), shift(edge_spec),
+            ]
+            + pick_specs
+            + back_specs
+            + ([] if old is None else [any_space]),
+            out_specs=shift(packed_spec),
+            out_shape=packed_shape,
+            input_output_aliases={} if old is None else {12: 0},
+            compiler_params=head_params,
+            name="back_inside",
+        )(
+            packed, scaled, mixed_grad, keep_column, before, halo, taps, first, second, first.T, second.T, ones,
+            *(() if old is None else (old,)),
+        )
+
+    def inside_first(sent):
+        sent, part, again, *rest = barrier((sent, back_inside(0, scaled, None), scaled, feed) + outer_grads)
+        staged.append((back_inside(HEADS // 2, again, part), rest))
+        return sent
+
+    outer_grads = (grad_outward_down, grad_outward_up, grad_expand_down, grad_reduce_up)
     edge = chip_shift(edge, -1)
-    part = pl.pallas_call(
-        back_inside_kernel,
-        grid=(HEADS,),
-        in_specs=[packed_spec, head_spec, head_spec, whole((rows, 1)), state_spec, halo_spec, edge_spec]
-        + pick_specs
-        + back_specs,
-        out_specs=packed_spec,
-        out_shape=packed_shape,
-        compiler_params=head_params,
-        name="back_inside",
-    )(packed, scaled, mixed_grad, keep_column, before, halo, taps, first, second, first.T, second.T, ones)
+    later = scan_chips(back_state, back_state.astype(BF), False, inside_first)
+    part, (feed, *outer_grads) = staged[0]
+    output = (keep_column * (residual + feed + dot(reduce_rank, reduce_second))).astype(BF)
+
+    def send_back(values):
+        return lax.all_to_all(values.reshape(sequences, slot_rows, -1), COLUMN, 0, 0, tiled=True)
+
     packed_grad = pl.pallas_call(
         back_later_kernel,
         grid=(HEADS,),
@@ -674,76 +736,43 @@
         name="back_later",
     )(packed, part, keep_column, later, edge, taps, first, second, first.T, second.T, ones)
 
+    packed_grad, back_first = barrier((packed_grad, send_back(output[:, : width // 2])))
+    back_last = send_back(after(output[:, width // 2 :], back_first))
     enter_grad = dot(packed_grad, inward_second, TURNED).astype(BF)
     normed_grad = (
-        dot(packed_grad[:, :in_width], in_weights[0], TURNED)
-        + dot(packed_grad[:, in_width:], in_weights[1], TURNED)
-        + dot(enter_grad, inward_first)
+        dot(packed_grad, in_weights, TURNED) + dot(enter_grad, inward_first)
     )
     input_grad = (branch.astype(F32) + rms_back(inputs, gain_first, normed_grad)).astype(BF)
-    input_grad, packed_late = barrier((input_grad, packed_grad))
-    grad_inward_up = dot(dot(enter, packed_late, ROWS).astype(BF).reshape(-1, PACK), order, TURNED).astype(BF)
+    grad_inward_up = dot(dot(enter, packed_grad, ROWS).astype(BF).reshape(-1, PACK), order, TURNED).astype(BF)
     grad_inward_up = grad_inward_up.reshape(ranks, -1)
-    grad_inward_down = dot(after(enter_grad, packed_late), normed, ROWS)
-
-    def send_back(values):
-        pieces = values.astype(BF).reshape(sequences, slot_rows, width)
-        return lax.all_to_all(pieces, COLUMN, 0, 0, tiled=True).astype(F32)
-
-    hot = (jnp.arange(adapters, dtype=jnp.int32)[:, None] == adapter_ids[None, :]).astype(F32)
-    hot = hot.reshape(adapters, 2, ways)
-    hot = jnp.where(core == 0, hot, hot[:, ::-1])
-    turned = [lax.dynamic_index_in_dim(hot, (place - j) % ways, 2, keepdims=False) for j in range(ways)]
-    hot = jnp.stack(turned, axis=2).reshape(adapters, 2 * ways)
-
-    def exchange(pieces):
-        got = [pieces(0).astype(BF)]
-        for j in range(1, ways):
-            pairs = [(s, (s + j) % ways) for s in range(ways)]
-            got.append(lax.ppermute(pieces(j).astype(BF), "wa", pairs))
-        summed = jnp.stack(got)
-        bit = 1
-        while bit < chips:
-            summed = (summed.astype(F32) + flip(summed, bit).astype(F32)).astype(BF)
-            bit *= 2
-        both = jnp.concatenate([summed, lax.ppermute(summed, "c", SWAP)], axis=0).astype(F32)
-        return jnp.tensordot(hot, both, axes=1, precision=lax.Precision.HIGHEST)
-
-    shard = width // ways
-
-    def shard_of(table, j):
-        return lax.dynamic_slice_in_dim(table, (place + j) % ways * shard, shard, 1)
-
-    early = exchange(
-        lambda j: after(jnp.concatenate(
+    grad_inward_down = dot(enter_grad, normed, ROWS)
+
+    places = exchange_places(
+        lambda j: jnp.concatenate(
             expand_grads[j]
-            + [
-                grad_outward_down[:, j * out_here : (j + 1) * out_here],
-                shard_of(grad_outward_up, j),
-                shard_of(grad_expand_down, j),
-                shard_of(grad_reduce_up, j),
-            ],
+            + [outer_grads[0][:, j * out_here : (j + 1) * out_here]]
+            + [shard_of(t, j) for t in outer_grads[1:]]
+            + [grad_inward_up[:, j * in_width : (j + 1) * in_width], shard_of(grad_inward_down, j)],
             axis=1,
-        ), scaled)
-    )
-    late = exchange(
-        lambda j: jnp.concatenate(
-            [grad_inward_up[:, j * in_width : (j + 1) * in_width], shard_of(grad_inward_down, j)], axis=1
         )
     )
-    at = np.cumsum([0, 2 * hidden_here, hidden_here, out_here, shard, shard, shard])
-    early_parts = [early[:, :, at[n] : at[n + 1]] for n in range(6)]
+    input_grad, places, back_last = barrier((input_grad, places, back_last))
+    input_first = send_back(input_grad[:, : width // 2])
+    input_last = send_back(after(input_grad[:, width // 2 :], input_first))
+    sums = exchange_chips(places)
+    at = np.cumsum([0, 2 * hidden_here, hidden_here, out_here, shard, shard, shard, in_width, shard])
+    grads = [sums[:, :, at[n] : at[n + 1]] for n in range(8)]
     return (
-        send_back(output),
-        send_back(input_grad),
-        late[:, :, in_width:],
-        late[:, :, :in_width],
-        early_parts[2],
-        early_parts[3],
-        early_parts[4],
-        early_parts[0].reshape(adapters, ranks, 2, hidden_here),
-        early_parts[1],
-        early_parts[5],
+        jnp.concatenate([back_first, back_last], axis=2).astype(F32),
+        jnp.concatenate([input_first, input_last], axis=2).astype(F32),
+        grads[7],
+        grads[6],
+        grads[2],
+        grads[3],
+        grads[4],
+        grads[0].reshape(adapters, ranks, 2, hidden_here),
+        grads[1],
+        grads[5],
     )
 
 

time: 734 us -> 706 us (0.962)
  waiting for transfers between devices: 207 us -> 133 us
  matrix products: 78.4 us -> 99.5 us
  local copies, waits for them, and re-layouts: 65.1 us -> 81.6 us
  starting transfers between devices: 64.4 us -> 76.5 us
    ppermute x4, waiting for transfers between devices: 64.4 us -> 34.1 us  [from_next(): return lax.ppermute(piece, 'wa', next_place)]
    all_to_all x2, waiting for transfers between devices: 39.7 us -> 11.2 us  [column_exchange(): return lax.all_to_all(values, COLUMN, 0, 0, tiled=True).reshape(rows, width)]
    ppermute x4 -> x2, waiting for transfers between devices: 29.2 us -> 3.03 us  [from_last(): return lax.ppermute(piece, 'wa', last_place)]
    dot_general x53 -> x48, matrix products: 76.4 us -> 99.5 us  [dot(): lax.dot_general(left, right, (dims, ((), ())), preferred_element_type=F32)]
    concatenate x10 -> x14, local copies, waits for them, and re-layouts: 0.72 us -> 16.7 us  [the longest x13 14.6 us: on_device(): jnp.concatenate(expand_grads[j] + [outer_grads[0][:, j * out_here:(j + 1)...]
    all_to_all x2 -> x4, starting transfers between devices: 11 us -> 20.1 us  [send_back(): lax.all_to_all(values.reshape(sequences, slot_rows, -1), COLUMN, 0, 0, ti...]
    slice x10 -> x19, local copies, waits for them, and re-layouts: 6.99 us -> 14.6 us  [the longest x4 4.54 us: on_device(): grads = [sums[:, :, at[n]:at[n + 1]] for n in range(8)]]
    all_to_all x2 -> x4, waiting for transfers between devices: 8.52 us -> 14.9 us  [send_back(): lax.all_to_all(values.reshape(sequences, slot_rows, -1), COLUMN, 0, 0, ti...]
  transfers between devices with their start and end apart: 37 -> 36, of which waited for: 19 -> 16; matrix products, arithmetic and copies ran while one was open for 23% -> 26% of each run, Pallas kernels for 25% -> 26%
where the time goes in v3:
time: 706 us; the launch traced here: 695 us
  Pallas kernels  224 us (32%)
  waiting for transfers between devices  133 us (19%)
  matrix products  99.5 us (14%)
  local copies, waits for them, and re-layouts  81.6 us (12%)
  starting transfers between devices  76.5 us (11%)
  other arithmetic  56.6 us (8%)
  between operations  23.5 us (3%)
    pallas_call x4, Pallas kernels, ffn_part(): pl.pallas_call(later_ffn_kernel if sums else first_ffn_kernel, grid=(step...  121 us
    dot_general x48, matrix products, dot(): lax.dot_general(left, right, (dims, ((), ())), preferred_element_type=F32)  99.5 us
    ppermute x4, waiting for transfers between devices, from_next(): return lax.ppermute(piece, 'wa', next_place)  34.1 us
    ppermute x3, waiting for transfers between devices, on_device(): tables.append(lax.ppermute(prepared[j], 'wa', pairs))  30.7 us
    pallas_call x2, Pallas kernels, back_inside(): pl.pallas_call(back_inside_kernel if old is None else lambda *refs: back_...  30.1 us
    ppermute x10, waiting for transfers between devices, flip(): lax.ppermute(piece, CHIPS, [(i, i ^ bit) for i in range(chips) if keep_pa...  29.9 us
    all_to_all x4, starting transfers between devices, send_back(): lax.all_to_all(values.reshape(sequences, slot_rows, -1), COLUMN, 0, 0, ti...  20.1 us
    ppermute x10, starting transfers between devices, flip(): lax.ppermute(piece, CHIPS, [(i, i ^ bit) for i in range(chips) if keep_pa...  17.5 us
  transfers between devices with their start and end apart: 36, of which 16 were waited for; matrix products, arithmetic and copies ran while one was open for 26% of the time, Pallas kernels for 26%

profile of v3, /device:TPU:0, one launch (start us, length us, event | category | flops | bytes accessed | tf_op | source)
XLA Modules:
  0.0 694.6 jit_solution(11484604221598855088)
XLA Ops:
  16.7 5.1 collective-permute-start
  52.5 25.5 %collective-permute-done.3 = bf16[16,5120]{1,0:T(8,128)(2,1)} collective-permute-done((bf16[16,5120]{1,0:T(8,128)(2,1)}, bf16[16,5120]{1,0:T(8,128)(2,1)}, u32[]{:S(2)}, u32[]{:S(2)}) %collective-permute-start.3) | collective-permute-done | bytes 163872 | tf_op jit(solution)/shard_map/ppermute | solution.py:477
  78.0 5.3 collective-permute-done.4
  95.3 30.0 %collective-permute-done.6 = bf16[480,1792]{1,0:T(8,128)(2,1)S(1)} collective-permute-done((bf16[480,1792]{1,0:T(8,128)(2,1)}, bf16[480,1792]{1,0:T(8,128)(2,1)S(1)}, u32[]{:S(2)}, u32[]{:S(2)}) %collective-permute-start.6) | collective-permute-done | bytes 1720352 | tf_op jit(solution)/shard_map/ppermute | solution.py:437
  134.8 4.9 all-to-all-start
  143.3 6.0 copy.83
  156.1 6.5 pad_maximum_fusion.1
  165.2 6.1 pad_maximum_fusion
  171.4 11.2 %all-to-all-done = bf16[8,64,1792]{2,1,0:T(8,128)(2,1)S(1)} async-done(((bf16[8,64,1792]{2,1,0:T(8,128)(2,1)}), bf16[8,64,1792]{2,1,0:T(8,128)(2,1)S(1)}, u32[]{:S(2)}, u32[]{:S(2)}) %all-to-all-start) | async-done | bytes 1835040 | tf_op jit(solution)/shard_map/all_to_all | solution.py:446
  183.9 11.1 %fusion.119 = f32[512,4096]{1,0:T(8,128)S(1)} fusion(bf16[1792,4096]{1,0:T(8,128)(2,1)} %pad_maximum_fusion, bf16[512,1792]{1,0:T(8,128)(2,1)S(1)} %bitcast.336, f32[1792]{0:T(1024)S(1)} %copy-done.62, f32[512]{0:T(512)S(1)} %get-tuple-element.269), kind=kOutput, calls=%fused_computation.305 | convolution fusion | flops 7519862784 | bytes 24912896 | tf_op jit(solution)/shard_map/dot_general | solution.py:378
  199.8 12.6 %state.1 = f32[16,160,128]{2,1,0:T(8,128)} custom-call(bf16[512,4096]{1,0:T(8,128)(2,1)} %copy-done.1, f32[1,512]{1,0:T(1,128)} %compare_convert_fusion.keep_ref, bf16[160,128]{1,0:T(8,128)(2,1)} %constant.277.first_ref.back_first_ref.refs_9_, bf16[160,128]{1,0:T(8,128)(2,1)} %constant.278.second_ref.back_second_ref.refs_10_, f32[160,3]{1,0:T(8,128)} %constant.279.ones_ref), custom_call_target="tpu_custom_call" | custom-call | tf_op jit(solution)/shard_map/state/pallas_call | solution.py:555
  230.9 16.9 %collective-permute-done.9 = bf16[16,160,128]{2,1,0:T(8,128)(2,1)S(1)} collective-permute-done((bf16[16,160,128]{2,1,0:T(8,128)(2,1)}, bf16[16,160,128]{2,1,0:T(8,128)(2,1)S(1)}, u32[]{:S(2)}, u32[]{:S(2)}) %collective-permute-start.9) | collective-permute-done | bytes 655392 | tf_op jit(solution)/shard_map/ppermute | solution.py:524
  257.0 14.4 %inside.1.inside_ref = f32[512,2048]{1,0:T(8,128)} custom-call(bf16[512,4096]{1,0:T(8,128)(2,1)} %copy-done.1, f32[512,1]{1,0:T(8,128)} %fusion.48.keep_column_ref.refs_3_), custom_call_target="tpu_custom_call" | custom-call | tf_op jit(solution)/shard_map/inside/pallas_call | solution.py:570
  271.4 5.8 collective-permute-done.10
  283.4 15.6 %mixer.1 = (bf16[512,2048]{1,0:T(8,128)(2,1)}, bf16[512,2048]{1,0:T(8,128)(2,1)}) custom-call(bf16[512,4096]{1,0:T(8,128)(2,1)} %copy-done.1, f32[512,2048]{1,0:T(8,128)} %inside.1.inside_ref, bf16[16,160,128]{2,1,0:T(8,128)(2,1)} %fusion.16.state_ref.refs_4_, bf16[8,4096]{1,0:T(8,128)(2,1)} %copy-done.28, f32[8,2048]{1,0:T(8,128)} %pad.36.taps_ref.refs_6_, ...), custom_call_target="tpu_custom_call" | custom-call | tf_op jit(solution)/shard_map/mixer/pallas_call | solution.py:581
  301.2 7.9 %fusion.128 = f32[512,1792]{1,0:T(8,128)S(1)} fusion(bf16[512,2048]{1,0:T(8,128)(2,1)} %get-tuple-element.118, bf16[1792,2048]{1,0:T(8,128)(2,1)} %pad_maximum_fusion.1), kind=kOutput, calls=%fused_computation.312 | convolution fusion | flops 3758096384 | bytes 13107200 | tf_op jit(solution)/shard_map/dot_general | solution.py:378
  329.7 29.3 %ffn_part.4 = (f32[512,1792]{1,0:T(8,128)}, f32[512,1792]{1,0:T(8,128)}, f32[2,512,16]{2,1,0:T(8,128)}, f32[2,16,608]{2,1,0:T(8,128)}, f32[2,16,608]{2,1,0:T(8,128)}, /*index=5*/f32[2,16,608]{2,1,0:T(8,128)}) custom-call(bf16[512,1792]{1,0:T(8,128)(2,1)} %copy-done.8, bf16[512,1792]{1,0:T(8,128)(2,1)} %copy-done.2, bf16[512,16]{1,0:T(8,128)(2,1)} %copy.96.refs_2_, ...), custom_call_target="tpu_custom_call" | custom-call | tf_op jit(solution)/shard_map/ffn_part/pallas_call | solution.py:340
  359.0 31.6 %ffn_part.5 = (f32[512,1792]{1,0:T(8,128)}, f32[512,1792]{1,0:T(8,128)}, f32[2,512,16]{2,1,0:T(8,128)}, f32[2,16,640]{2,1,0:T(8,128)}, f32[2,16,640]{2,1,0:T(8,128)}, /*index=5*/f32[2,16,640]{2,1,0:T(8,128)}) custom-call(bf16[512,1792]{1,0:T(8,128)(2,1)} %copy-done.8, ...), custom_call_target="tpu_custom_call", output_to_operand_aliasing={{0}: (12, {}), {1}: (13, {}), {2}: (14, {})} | custom-call | tf_op jit(solution)/shard_map/ffn_part/pallas_call | solution.py:340
  394.8 30.2 %ffn_part.6 = (f32[512,1792]{1,0:T(8,128)}, f32[512,1792]{1,0:T(8,128)}, f32[2,512,16]{2,1,0:T(8,128)}, f32[2,16,640]{2,1,0:T(8,128)}, f32[2,16,640]{2,1,0:T(8,128)}, /*index=5*/f32[2,16,640]{2,1,0:T(8,128)}) custom-call(bf16[512,1792]{1,0:T(8,128)(2,1)} %copy-done.8, ...), custom_call_target="tpu_custom_call", output_to_operand_aliasing={{0}: (12, {}), {1}: (13, {}), {2}: (14, {})} | custom-call | tf_op jit(solution)/shard_map/ffn_part/pallas_call | solution.py:340
  426.8 29.7 %ffn_part.7 = (f32[512,1792]{1,0:T(8,128)}, f32[512,1792]{1,0:T(8,128)}, f32[2,512,16]{2,1,0:T(8,128)}, f32[2,16,640]{2,1,0:T(8,128)}, f32[2,16,640]{2,1,0:T(8,128)}, /*index=5*/f32[2,16,640]{2,1,0:T(8,128)}) custom-call(bf16[512,1792]{1,0:T(8,128)(2,1)} %copy-done.8, ...), custom_call_target="tpu_custom_call", output_to_operand_aliasing={{0}: (12, {}), {1}: (13, {}), {2}: (14, {})} | custom-call | tf_op jit(solution)/shard_map/ffn_part/pallas_call | solution.py:340
  467.1 8.7 %add_convert_fusion.1.grad_ref.refs_2_ = bf16[512,2048]{1,0:T(8,128)(2,1)} fusion(f32[512,2048]{1,0:T(8,128)S(1)} %fusion.129, bf16[512,1792]{1,0:T(8,128)(2,1)S(1)} %add_convert_fusion.2, bf16[1792,2048]{1,0:T(8,128)(2,1)} %pad_maximum_fusion.1), kind=kOutput, calls=%fused_computation.9 | convolution fusion | flops 3760193536 | bytes 15466496 | tf_op jit(solution)/shard_map/dot_general | solution.py:378
  475.7 13.9 %back_state.1 = (bf16[512,2048]{1,0:T(8,128)(2,1)}, f32[16,160,128]{2,1,0:T(8,128)}, f32[8,2048]{1,0:T(8,128)}) custom-call(bf16[512,4096]{1,0:T(8,128)(2,1)} %copy-done.1, bf16[512,2048]{1,0:T(8,128)(2,1)} %get-tuple-element.117.kept_ref, bf16[512,2048]{1,0:T(8,128)(2,1)} %add_convert_fusion.1.grad_ref.refs_2_, ...), custom_call_target="tpu_custom_call" | custom-call | tf_op jit(solution)/shard_map/back_state/pallas_call | solution.py:643
  495.8 15.1 %back_inside.2.refs_12_ = bf16[512,4096]{1,0:T(8,128)(2,1)} custom-call(bf16[512,4096]{1,0:T(8,128)(2,1)} %copy-done.1, bf16[512,2048]{1,0:T(8,128)(2,1)} %get-tuple-element.142.scaled_ref.refs_1_, bf16[512,2048]{1,0:T(8,128)(2,1)} %add_convert_fusion.1.grad_ref.refs_2_, f32[512,1]{1,0:T(8,128)} %fusion.48.keep_column_ref.refs_3_, ...), custom_call_target="tpu_custom_call" | custom-call | tf_op jit(solution)/shard_map/back_inside/pallas_call | solution.py:693
  520.4 4.7 all-to-all-start.2
  528.6 15.0 %back_inside.3.part_ref = bf16[512,4096]{1,0:T(8,128)(2,1)} custom-call(bf16[512,4096]{1,0:T(8,128)(2,1)} %copy-done.1, bf16[512,2048]{1,0:T(8,128)(2,1)} %get-tuple-element.142.scaled_ref.refs_1_, bf16[512,2048]{1,0:T(8,128)(2,1)} %add_convert_fusion.1.grad_ref.refs_2_, f32[512,1]{1,0:T(8,128)} %fusion.48.keep_column_ref.refs_3_, ...), custom_call_target="tpu_custom_call", output_to_operand_aliasing={{}: (12, {})} | custom-call | tf_op jit(solution)/shard_map/back_inside/pallas_call | solution.py:693
  548.4 16.7 %back_later.1 = bf16[512,4096]{1,0:T(8,128)(2,1)} custom-call(bf16[512,4096]{1,0:T(8,128)(2,1)} %copy-done.1, bf16[512,4096]{1,0:T(8,128)(2,1)} %back_inside.3.part_ref, f32[512,1]{1,0:T(8,128)} %fusion.48.keep_column_ref.refs_3_, bf16[16,160,128]{2,1,0:T(8,128)(2,1)} %fusion.20.later_ref, f32[8,2048]{1,0:T(8,128)} %collective-permute-done.14.edge_ref, ...), custom_call_target="tpu_custom_call" | custom-call | tf_op jit(solution)/shard_map/back_later/pallas_call | solution.py:727
  574.0 5.1 all-to-all-start.3
  594.2 15.8 %fusion.8 = (f32[512]{0:T(512)S(1)}, f32[512,1792]{1,0:T(8,128)}) fusion(bf16[512,1792]{1,0:T(8,128)(2,1)S(1)} %bitcast.340, f32[1792]{0:T(1024)} %param.27, f32[512,1792]{1,0:T(8,128)} %fusion.63, bf16[512,4096]{1,0:T(8,128)(2,1)} %back_later.1, bf16[1792,4096]{1,0:T(8,128)(2,1)} %pad_maximum_fusion), kind=kOutput, calls=%fused_computation.18 | convolution fusion | flops 7520779776 | bytes 28058624 | tf_op jit(solution)/shard_map/dot_general | solution.py:378
  610.1 4.9 fusion.7
  628.8 6.8 all-to-all-start.4
  653.3 5.5 all-to-all-done.4
  676.1 9.4 %all-to-all-done.5 = bf16[8,64,896]{2,1,0:T(8,128)(2,1)S(1)} async-done(((bf16[8,64,896]{2,1,0:T(8,128)(2,1)}), bf16[8,64,896]{2,1,0:T(8,128)(2,1)S(1)}, u32[]{:S(2)}, u32[]{:S(2)}) %all-to-all-start.5) | async-done | bytes 917536 | tf_op jit(solution)/shard_map/all_to_all | solution.py:725
  (418 shorter events, 243.9 us)
Async XLA Ops:
  7.2 142.1 %all-gather.6.cloned.1.call-start = ((), (), s32[]{:S(2)}) async-start(), calls=%async_computation.6 | async-start | bytes 6193152 | tf_op jit(solution)/shard_map/all_gather | solution.py:443
  16.7 21.9 %collective-permute-start = (bf16[224,1536]{1,0:T(8,128)(2,1)}, bf16[224,1536]{1,0:T(8,128)(2,1)S(1)}, u32[]{:S(2)}, u32[]{:S(2)}) collective-permute-start(bf16[224,1536]{1,0:T(8,128)(2,1)} %bitcast_dynamic-update-slice_fusion), channel_id=1, source_target_pairs={{1,0},{2,1},{3,2},{0,3},{5,4},{6,5},{7,6},{4,7},{9,8},{10,9},{11,1... | collective-permute-start | bytes 2064392 | tf_op jit(solution)/shard_map/ppermute | solution.py:437
  39.5 114.0 %all-gather.8.cloned.1.call-start = ((), (), s32[]{:S(2)}) async-start(), calls=%async_computation.7 | async-start | bytes 12386304 | tf_op jit(solution)/shard_map/all_gather | solution.py:443
  39.6 43.7 %collective-permute-start.1 = (bf16[224,1536]{1,0:T(8,128)(2,1)}, bf16[224,1536]{1,0:T(8,128)(2,1)S(1)}, u32[]{:S(2)}, u32[]{:S(2)}) collective-permute-start(bf16[224,1536]{1,0:T(8,128)(2,1)} %copy-done.26), channel_id=1, source_target_pairs={{1,0},{2,1},{3,2},{0,3},{5,4},{6,5},{7,6},{4,7},{9,8},{10,9},{11,1... | collective-permute-start | bytes 2064392 | tf_op jit(solution)/shard_map/ppermute | solution.py:437
  42.0 41.3 %collective-permute-start.2 = (bf16[224,1536]{1,0:T(8,128)(2,1)}, bf16[224,1536]{1,0:T(8,128)(2,1)}, u32[]{:S(2)}, u32[]{:S(2)}) collective-permute-start(bf16[224,1536]{1,0:T(8,128)(2,1)} %bitcast_dynamic-update-slice_fusion), channel_id=1, source_target_pairs={{0,1},{1,2},{2,3},{3,0},{4,5},{5,6},{6,7},{7,4},{8,9},{9,10},{10,1... | collective-permute-start | bytes 2064392 | tf_op jit(solution)/shard_map/ppermute | solution.py:440
  42.0 36.0 %collective-permute-start.3 = (bf16[16,5120]{1,0:T(8,128)(2,1)}, bf16[16,5120]{1,0:T(8,128)(2,1)}, u32[]{:S(2)}, u32[]{:S(2)}) collective-permute-start(bf16[16,5120]{1,0:T(8,128)(2,1)} %concatenate.119), channel_id=1, source_target_pairs={{0,3},{1,0},{2,1},{3,2},{4,7},{5,4},{6,5},{7,6},{8,11},{9,8},{10,9... | collective-permute-start | bytes 491528 | tf_op jit(solution)/shard_map/ppermute | solution.py:477
  45.8 37.4 %collective-permute-start.4 = (bf16[16,5120]{1,0:T(8,128)(2,1)}, bf16[16,5120]{1,0:T(8,128)(2,1)S(1)}, u32[]{:S(2)}, u32[]{:S(2)}) collective-permute-start(bf16[16,5120]{1,0:T(8,128)(2,1)} %concatenate.120), channel_id=1, source_target_pairs={{0,2},{1,3},{2,0},{3,1},{4,6},{5,7},{6,4},{7,5},{8,10},{9,11},{10,... | collective-permute-start | bytes 491528 | tf_op jit(solution)/shard_map/ppermute | solution.py:477
  45.8 37.4 %collective-permute-start.5 = (bf16[16,5120]{1,0:T(8,128)(2,1)}, bf16[16,5120]{1,0:T(8,128)(2,1)}, u32[]{:S(2)}, u32[]{:S(2)}) collective-permute-start(bf16[16,5120]{1,0:T(8,128)(2,1)} %concatenate.121), channel_id=1, source_target_pairs={{0,1},{1,2},{2,3},{3,0},{4,5},{5,6},{6,7},{7,4},{8,9},{9,10},{10,1... | collective-permute-start | bytes 491528 | tf_op jit(solution)/shard_map/ppermute | solution.py:477
  86.6 272.4 %all-gather.14.cloned.1.call-start = ((), (), s32[]{:S(2)}) async-start(), calls=%async_computation.10 | async-start | bytes 15482880 | tf_op jit(solution)/shard_map/all_gather | solution.py:443
  86.6 38.8 %collective-permute-start.6 = (bf16[480,1792]{1,0:T(8,128)(2,1)}, bf16[480,1792]{1,0:T(8,128)(2,1)S(1)}, u32[]{:S(2)}, u32[]{:S(2)}) collective-permute-start(bf16[480,1792]{1,0:T(8,128)(2,1)} %maximum_select_fusion), channel_id=1, source_target_pairs={{1,0},{2,1},{3,2},{0,3},{5,4},{6,5},{7,6},{4,7},{9,8},{10,9},{11,1... | collective-permute-start | bytes 5160968 | tf_op jit(solution)/shard_map/ppermute | solution.py:437
  134.8 47.8 %all-to-all-start = ((bf16[8,64,1792]{2,1,0:T(8,128)(2,1)}), bf16[8,64,1792]{2,1,0:T(8,128)(2,1)S(1)}, u32[]{:S(2)}, u32[]{:S(2)}) async-start(bf16[8,64,1792]{2,1,0:T(8,128)(2,1)} %param.23), calls=%async_computation | async-start | bytes 3670016 | tf_op jit(solution)/shard_map/all_to_all | solution.py:446
  139.7 255.0 %all-gather.12.cloned.1.call-start = ((), (), s32[]{:S(2)}) async-start(), calls=%async_computation.9 | async-start | bytes 15482880 | tf_op jit(solution)/shard_map/all_gather | solution.py:443
  182.6 42.3 %collective-permute-start.7 = (bf16[480,1792]{1,0:T(8,128)(2,1)}, bf16[480,1792]{1,0:T(8,128)(2,1)}, u32[]{:S(2)}, u32[]{:S(2)}) collective-permute-start(bf16[480,1792]{1,0:T(8,128)(2,1)} %maximum_select_fusion), channel_id=1, source_target_pairs={{0,1},{1,2},{2,3},{3,0},{4,5},{5,6},{6,7},{7,4},{8,9},{9,10},{10,1... | collective-permute-start | bytes 5160968 | tf_op jit(solution)/shard_map/ppermute | solution.py:440
  224.9 54.5 %all-to-all-start.1 = ((bf16[8,64,1792]{2,1,0:T(8,128)(2,1)}), bf16[8,64,1792]{2,1,0:T(8,128)(2,1)}, u32[]{:S(2)}, u32[]{:S(2)}) async-start(bf16[8,64,1792]{2,1,0:T(8,128)(2,1)} %param.24), calls=%async_computation.1 | async-start | bytes 3670016 | tf_op jit(solution)/shard_map/all_to_all | solution.py:446
  229.3 197.6 %all-gather.10.cloned.1.call-start = ((), (), s32[]{:S(2)}) async-start(), calls=%async_computation.8 | async-start | bytes 15482880 | tf_op jit(solution)/shard_map/all_gather | solution.py:443
  229.3 18.4 %collective-permute-start.9 = (bf16[16,160,128]{2,1,0:T(8,128)(2,1)}, bf16[16,160,128]{2,1,0:T(8,128)(2,1)S(1)}, u32[]{:S(2)}, u32[]{:S(2)}) collective-permute-start(bf16[16,160,128]{2,1,0:T(8,128)(2,1)} %convert_element_type.296), channel_id=1, source_target_pairs={{0,8},{8,0},{16,24},{24,16},{1,9},{9,1},{17,25},{25,17},{2,10},{10... | collective-permute-start | bytes 1966088 | tf_op jit(solution)/shard_map/ppermute | solution.py:524
  250.0 27.2 %collective-permute-start.10 = (bf16[16,160,128]{2,1,0:T(8,128)(2,1)}, bf16[16,160,128]{2,1,0:T(8,128)(2,1)}, u32[]{:S(2)}, u32[]{:S(2)}) collective-permute-start(bf16[16,160,128]{2,1,0:T(8,128)(2,1)} %fusion.17), channel_id=1, source_target_pairs={{0,16},{8,24},{1,17},{9,25},{2,18},{10,26},{3,19},{11,27},{4,20},{... | collective-permute-start | bytes 1966088 | tf_op jit(solution)/shard_map/ppermute | solution.py:524
  279.4 40.6 %collective-permute-start.11 = (bf16[480,1792]{1,0:T(8,128)(2,1)}, bf16[480,1792]{1,0:T(8,128)(2,1)}, u32[]{:S(2)}, u32[]{:S(2)}) collective-permute-start(bf16[480,1792]{1,0:T(8,128)(2,1)} %copy-done.24), channel_id=1, source_target_pairs={{1,0},{2,1},{3,2},{0,3},{5,4},{6,5},{7,6},{4,7},{9,8},{10,9},{11,1... | collective-permute-start | bytes 5160968 | tf_op jit(solution)/shard_map/ppermute | solution.py:437
  491.9 22.6 %collective-permute-start.12 = (bf16[16,160,128]{2,1,0:T(8,128)(2,1)}, bf16[16,160,128]{2,1,0:T(8,128)(2,1)S(1)}, u32[]{:S(2)}, u32[]{:S(2)}) collective-permute-start(bf16[16,160,128]{2,1,0:T(8,128)(2,1)} %convert_element_type.314), channel_id=1, source_target_pairs={{0,8},{8,0},{16,24},{24,16},{1,9},{9,1},{17,25},{25,17},{2,10},{10... | collective-permute-start | bytes 1966088 | tf_op jit(solution)/shard_map/ppermute | solution.py:524
  520.4 44.7 %all-to-all-start.2 = ((bf16[8,64,896]{2,1,0:T(8,128)(2,1)}), bf16[8,64,896]{2,1,0:T(8,128)(2,1)S(1)}, u32[]{:S(2)}, u32[]{:S(2)}) async-start(bf16[8,64,896]{2,1,0:T(8,128)(2,1)} %bitcast.71), calls=%async_computation.2 | async-start | bytes 1835008 | tf_op jit(solution)/shard_map/all_to_all | solution.py:725
  525.3 23.1 %collective-permute-start.14 = (f32[8,2048]{1,0:T(8,128)}, f32[8,2048]{1,0:T(8,128)}, u32[]{:S(2)}, u32[]{:S(2)}) collective-permute-start(f32[8,2048]{1,0:T(8,128)} %get-tuple-element.145), channel_id=1, source_target_pairs={{8,0},{16,8},{24,16},{9,1},{17,9},{25,17},{10,2},{18,10},{26,18},{... | collective-permute-start | bytes 196616 | tf_op jit(solution)/shard_map/ppermute | solution.py:520
  526.6 20.6 %collective-permute-start.13 = (bf16[16,160,128]{2,1,0:T(8,128)(2,1)S(1)}, bf16[16,160,128]{2,1,0:T(8,128)(2,1)S(1)}, u32[]{:S(2)}, u32[]{:S(2)}) collective-permute-start(bf16[16,160,128]{2,1,0:T(8,128)(2,1)S(1)} %fusion.18), channel_id=1, source_target_pairs={{16,0},{24,8},{17,1},{25,9},{18,2},{26,10},{19,3},{27,11},{20,4},{... | collective-permute-start | bytes 1966088 | tf_op jit(solution)/shard_map/ppermute | solution.py:524
  574.0 46.1 %all-to-all-start.3 = ((bf16[8,64,896]{2,1,0:T(8,128)(2,1)}), bf16[8,64,896]{2,1,0:T(8,128)(2,1)}, u32[]{:S(2)}, u32[]{:S(2)}) async-start(bf16[8,64,896]{2,1,0:T(8,128)(2,1)} %bitcast.106), calls=%async_computation.3 | async-start | bytes 1835008 | tf_op jit(solution)/shard_map/all_to_all | solution.py:725
  584.8 32.0 %collective-permute-start.15 = (bf16[16,6912]{1,0:T(8,128)(2,1)}, bf16[16,6912]{1,0:T(8,128)(2,1)}, u32[]{:S(2)}, u32[]{:S(2)}) collective-permute-start(bf16[16,6912]{1,0:T(8,128)(2,1)} %concatenate.144), channel_id=1, source_target_pairs={{0,1},{1,2},{2,3},{3,0},{4,5},{5,6},{6,7},{7,4},{8,9},{9,10},{10,1... | collective-permute-start | bytes 663560 | tf_op jit(solution)/shard_map/ppermute | solution.py:665
  588.7 29.1 %collective-permute-start.16 = (bf16[16,6912]{1,0:T(8,128)(2,1)}, bf16[16,6912]{1,0:T(8,128)(2,1)}, u32[]{:S(2)}, u32[]{:S(2)}) collective-permute-start(bf16[16,6912]{1,0:T(8,128)(2,1)} %concatenate.146), channel_id=1, source_target_pairs={{0,2},{1,3},{2,0},{3,1},{4,6},{5,7},{6,4},{7,5},{8,10},{9,11},{10,... | collective-permute-start | bytes 663560 | tf_op jit(solution)/shard_map/ppermute | solution.py:665
  592.7 25.0 %collective-permute-start.17 = (bf16[16,6912]{1,0:T(8,128)(2,1)}, bf16[16,6912]{1,0:T(8,128)(2,1)}, u32[]{:S(2)}, u32[]{:S(2)}) collective-permute-start(bf16[16,6912]{1,0:T(8,128)(2,1)} %concatenate.148), channel_id=1, source_target_pairs={{0,3},{1,0},{2,1},{3,2},{4,7},{5,4},{6,5},{7,6},{8,11},{9,8},{10,9... | collective-permute-start | bytes 663560 | tf_op jit(solution)/shard_map/ppermute | solution.py:665
  622.1 13.6 %collective-permute-start.18 = (bf16[16,6912]{1,0:T(8,128)(2,1)}, bf16[16,6912]{1,0:T(8,128)(2,1)}, u32[]{:S(2)}, u32[]{:S(2)}) collective-permute-start(bf16[16,6912]{1,0:T(8,128)(2,1)} %get-tuple-element.181), channel_id=1, source_target_pairs={{0,8},{8,0},{16,24},{24,16},{1,9},{9,1},{17,25},{25,17},{2,10},{10... | collective-permute-start | bytes 663560 | tf_op jit(solution)/shard_map/ppermute | solution.py:524
  624.7 12.1 %collective-permute-start.19 = (bf16[16,6912]{1,0:T(8,128)(2,1)}, bf16[16,6912]{1,0:T(8,128)(2,1)}, u32[]{:S(2)}, u32[]{:S(2)}) collective-permute-start(bf16[16,6912]{1,0:T(8,128)(2,1)} %get-tuple-element.183), channel_id=1, source_target_pairs={{0,16},{8,24},{16,0},{24,8},{1,17},{9,25},{17,1},{25,9},{2,18},{10... | collective-permute-start | bytes 663560 | tf_op jit(solution)/shard_map/ppermute | solution.py:524
  628.8 30.0 %all-to-all-start.4 = ((bf16[8,64,896]{2,1,0:T(8,128)(2,1)}), bf16[8,64,896]{2,1,0:T(8,128)(2,1)S(1)}, u32[]{:S(2)}, u32[]{:S(2)}) async-start(bf16[8,64,896]{2,1,0:T(8,128)(2,1)} %bitcast.107), calls=%async_computation.4 | async-start | bytes 1835008 | tf_op jit(solution)/shard_map/all_to_all | solution.py:725
  640.3 11.4 %collective-permute-start.22 = (bf16[16,6912]{1,0:T(8,128)(2,1)S(1)}, bf16[16,6912]{1,0:T(8,128)(2,1)S(1)}, u32[]{:S(2)}, u32[]{:S(2)}) collective-permute-start(bf16[16,6912]{1,0:T(8,128)(2,1)S(1)} %get-tuple-element.171), channel_id=1, source_target_pairs={{0,16},{8,24},{16,0},{24,8},{1,17},{9,25},{17,1},{25,9},{2,18},{10... | collective-permute-start | bytes 663560 | tf_op jit(solution)/shard_map/ppermute | solution.py:524
  651.8 12.2 %collective-permute-start.24 = (bf16[64,6912]{1,0:T(8,128)(2,1)S(1)}, bf16[64,6912]{1,0:T(8,128)(2,1)}, u32[]{:S(2)}, u32[]{:S(2)}) collective-permute-start(bf16[64,6912]{1,0:T(8,128)(2,1)S(1)} %pad_maximum_fusion.5), channel_id=1, source_target_pairs={{0,4},{4,0},{1,5},{5,1},{2,6},{6,2},{3,7},{7,3},{8,12},{12,8},{9,1... | collective-permute-start | bytes 2654216 | tf_op jit(solution)/shard_map/ppermute | solution.py:679
  658.8 26.7 %all-to-all-start.5 = ((bf16[8,64,896]{2,1,0:T(8,128)(2,1)}), bf16[8,64,896]{2,1,0:T(8,128)(2,1)S(1)}, u32[]{:S(2)}, u32[]{:S(2)}) async-start(bf16[8,64,896]{2,1,0:T(8,128)(2,1)} %bitcast.108), calls=%async_computation.5 | async-start | bytes 1835008 | tf_op jit(solution)/shard_map/all_to_all | solution.py:725
  (73 other events, 1295.5 us)
Sparse Core Ops, SparseCore 0:
  39.7 42.0 all-gather.5
  86.7 66.7 all-gather.7
  155.4 77.7 all-gather.13
  235.0 86.9 all-gather.11
  323.7 76.9 all-gather.9

commit v4 on v3

--- a/solution.py
+++ b/solution.py
@@ -492,9 +492,16 @@
     in_split = (ways - 2) * in_width
     in_weights = jnp.concatenate([in_own, gathered_near[:, :in_width], gathered_rest[:, :in_split]], axis=1)
     out_weights = jnp.concatenate([out_own, gathered_near[:, in_width:], gathered_rest[:, in_split:]], axis=1)
-    x, ffn_slice, in_weights, out_weights, inward_second, outward_first = barrier(
-        (column_exchange(tokens_in), ffn_slice, in_weights, out_weights, inward_second, outward_first)
-    )
+    x, ffn_slice, in_weights, out_weights, inward_second = barrier(
+        (column_exchange(tokens_in), ffn_slice, in_weights, out_weights, inward_second)
+    )
+    ffn_tables = []
+    for j in range(ways):
+        chosen = jnp.stack(split_tables[j][2:5])
+        if j > 0:
+            empty = jnp.zeros((3, ranks, hidden_gap), BF)
+            chosen = jnp.concatenate([chosen[..., :gap_at], empty, chosen[..., gap_at:]], axis=2)
+        ffn_tables.append(jnp.swapaxes(chosen.reshape(3, ranks, 2, -1), 1, 2))
     ffn_3 = from_last(ffn_slice)
 
     which = adapter_ids[sequence]
@@ -576,7 +583,8 @@
         compiler_params=head_params,
         name="inside",
     )(packed, keep_column)
-    ffn_1, cot, inside, before = barrier((ffn_1, cot, inside, before))
+    held = barrier((ffn_1, cot, inside, before, outward_first) + tuple(ffn_tables))
+    (ffn_1, cot, inside, before, outward_first), ffn_tables = held[:5], held[5:]
     ffn_2 = from_next(ffn_1)
     mixed, kept = pl.pallas_call(
         mixer_kernel,
@@ -616,12 +624,7 @@
     ]
     expand_grads, sums = [None] * ways, ()
     for j, weights, specs in plans:
-        chosen = jnp.stack(split_tables[j][2:5])
-        if j > 0:
-            empty = jnp.zeros((3, ranks, hidden_gap), BF)
-            chosen = jnp.concatenate([chosen[..., :gap_at], empty, chosen[..., gap_at:]], axis=2)
-        chosen = jnp.swapaxes(chosen.reshape(3, ranks, 2, -1), 1, 2)
-        *sums, g_gate, g_up, g_reduce = ffn_part(normed_two, top, expand, top_rank, weights, specs, chosen, tuple(sums))
+        *sums, g_gate, g_up, g_reduce = ffn_part(normed_two, top, expand, top_rank, weights, specs, ffn_tables[j], tuple(sums))
         sums, grads = tuple(sums), (g_gate, g_up, g_reduce)
         grads = jnp.swapaxes(jnp.stack(grads), 1, 2).reshape(3, ranks, -1)
         if j > 0:
@@ -743,9 +746,15 @@
         dot(packed_grad, in_weights, TURNED) + dot(enter_grad, inward_first)
     )
     input_grad = (branch.astype(F32) + rms_back(inputs, gain_first, normed_grad)).astype(BF)
-    grad_inward_up = dot(dot(enter, packed_grad, ROWS).astype(BF).reshape(-1, PACK), order, TURNED).astype(BF)
+    input_grad, back_last, late_grad, late_enter = barrier((input_grad, back_last, packed_grad, enter_grad))
+    third = -(-width // 384) * 128
+    input_first = send_back(input_grad[:, :third])
+    input_next = send_back(after(input_grad[:, third : 2 * third], input_first))
+    input_last = send_back(after(input_grad[:, 2 * third :], input_next))
+    late_grad, late_enter = barrier((late_grad, late_enter, input_first))[:2]
+    grad_inward_up = dot(dot(enter, late_grad, ROWS).astype(BF).reshape(-1, PACK), order, TURNED).astype(BF)
     grad_inward_up = grad_inward_up.reshape(ranks, -1)
-    grad_inward_down = dot(enter_grad, normed, ROWS)
+    grad_inward_down = dot(late_enter, normed, ROWS)
 
     places = exchange_places(
         lambda j: jnp.concatenate(
@@ -756,15 +765,12 @@
             axis=1,
         )
     )
-    input_grad, places, back_last = barrier((input_grad, places, back_last))
-    input_first = send_back(input_grad[:, : width // 2])
-    input_last = send_back(after(input_grad[:, width // 2 :], input_first))
-    sums = exchange_chips(places)
+    sums = exchange_chips(after(places, input_next))
     at = np.cumsum([0, 2 * hidden_here, hidden_here, out_here, shard, shard, shard, in_width, shard])
     grads = [sums[:, :, at[n] : at[n + 1]] for n in range(8)]
     return (
         jnp.concatenate([back_first, back_last], axis=2).astype(F32),
-        jnp.concatenate([input_first, input_last], axis=2).astype(F32),
+        jnp.concatenate([input_first, input_next, input_last], axis=2).astype(F32),
         grads[7],
         grads[6],
         grads[2],

time: 706 us -> 735 us (1.041)
  waiting for transfers between devices: 133 us -> 155 us
  starting transfers between devices: 76.5 us -> 85.4 us
    ppermute x3, waiting for transfers between devices: 1.02 us -> 23.7 us  [exchange_places(): got.append(lax.ppermute(pieces(j).astype(BF), 'wa', pairs))]
    all_to_all x4 -> x5, waiting for transfers between devices: 14.9 us -> 22.8 us  [send_back(): lax.all_to_all(values.reshape(sequences, slot_rows, -1), COLUMN, 0, 0, ti...]
    concatenate x13, local copies, waits for them, and re-layouts: 14.6 us -> 6.74 us  [on_device(): jnp.concatenate(expand_grads[j] + [outer_grads[0][:, j * out_here:(j + 1)...]
    all_to_all x4 -> x5, starting transfers between devices: 20.1 us -> 26.9 us  [send_back(): lax.all_to_all(values.reshape(sequences, slot_rows, -1), COLUMN, 0, 0, ti...]
  transfers between devices with their start and end apart: 36 -> 37, of which waited for: 16 -> 15; matrix products, arithmetic and copies ran while one was open for 26% -> 24% of each run, Pallas kernels for 26% -> 25%
where the time goes in v4:
time: 735 us; the launch traced here: 724 us
  Pallas kernels  224 us (30%)
  waiting for transfers between devices  155 us (21%)
  matrix products  99.3 us (14%)
  starting transfers between devices  85.4 us (12%)
  local copies, waits for them, and re-layouts  77.8 us (11%)
  other arithmetic  58.3 us (8%)
  between operations  23.8 us (3%)
    pallas_call x4, Pallas kernels, ffn_part(): pl.pallas_call(later_ffn_kernel if sums else first_ffn_kernel, grid=(step...  121 us
    dot_general x48, matrix products, dot(): lax.dot_general(left, right, (dims, ((), ())), preferred_element_type=F32)  99.3 us
    ppermute x4, waiting for transfers between devices, from_next(): return lax.ppermute(piece, 'wa', next_place)  32.5 us
    ppermute x3, waiting for transfers between devices, on_device(): tables.append(lax.ppermute(prepared[j], 'wa', pairs))  30.9 us
    pallas_call x2, Pallas kernels, back_inside(): pl.pallas_call(back_inside_kernel if old is None else lambda *refs: back_...  30 us
    all_to_all x5, starting transfers between devices, send_back(): lax.all_to_all(values.reshape(sequences, slot_rows, -1), COLUMN, 0, 0, ti...  26.9 us
    ppermute x10, waiting for transfers between devices, flip(): lax.ppermute(piece, CHIPS, [(i, i ^ bit) for i in range(chips) if keep_pa...  24.5 us
    ppermute x3, waiting for transfers between devices, exchange_places(): got.append(lax.ppermute(pieces(j).astype(BF), 'wa', pairs))  23.7 us
  transfers between devices with their start and end apart: 37, of which 15 were waited for; matrix products, arithmetic and copies ran while one was open for 24% of the time, Pallas kernels for 25%

profile of v4, /device:TPU:0, one launch (start us, length us, event | category | flops | bytes accessed | tf_op | source)
XLA Modules:
  0.0 724.2 jit_solution(7812147189022267144)
XLA Ops:
  16.7 5.1 collective-permute-start
  52.5 25.4 %collective-permute-done.3 = bf16[16,5120]{1,0:T(8,128)(2,1)S(1)} collective-permute-done((bf16[16,5120]{1,0:T(8,128)(2,1)}, bf16[16,5120]{1,0:T(8,128)(2,1)S(1)}, u32[]{:S(2)}, u32[]{:S(2)}) %collective-permute-start.3) | collective-permute-done | bytes 163872 | tf_op jit(solution)/shard_map/ppermute | solution.py:477
  77.9 5.5 collective-permute-done.4
  95.5 30.0 %collective-permute-done.6 = bf16[480,1792]{1,0:T(8,128)(2,1)S(1)} collective-permute-done((bf16[480,1792]{1,0:T(8,128)(2,1)}, bf16[480,1792]{1,0:T(8,128)(2,1)S(1)}, u32[]{:S(2)}, u32[]{:S(2)}) %collective-permute-start.6) | collective-permute-done | bytes 1720352 | tf_op jit(solution)/shard_map/ppermute | solution.py:437
  141.4 6.0 copy.83
  147.4 6.1 all-gather.8.cloned.1.call-done
  156.2 6.5 pad_maximum_fusion.1
  165.3 6.2 pad_maximum_fusion
  171.5 7.6 %all-to-all-done = bf16[8,64,1792]{2,1,0:T(8,128)(2,1)S(1)} async-done(((bf16[8,64,1792]{2,1,0:T(8,128)(2,1)}), bf16[8,64,1792]{2,1,0:T(8,128)(2,1)S(1)}, u32[]{:S(2)}, u32[]{:S(2)}) %all-to-all-start) | async-done | bytes 1835040 | tf_op jit(solution)/shard_map/all_to_all | solution.py:446
  180.7 11.1 %fusion.120 = f32[512,4096]{1,0:T(8,128)S(1)} fusion(bf16[1792,4096]{1,0:T(8,128)(2,1)} %pad_maximum_fusion, bf16[512,1792]{1,0:T(8,128)(2,1)S(1)} %bitcast.335, f32[1792]{0:T(1024)S(1)} %copy-done.73, f32[512]{0:T(512)S(1)} %get-tuple-element.287), kind=kOutput, calls=%fused_computation.305 | convolution fusion | flops 7519862784 | bytes 24912896 | tf_op jit(solution)/shard_map/dot_general | solution.py:378
  196.6 12.5 %state.1 = f32[16,160,128]{2,1,0:T(8,128)} custom-call(bf16[512,4096]{1,0:T(8,128)(2,1)} %copy-done.1, f32[1,512]{1,0:T(1,128)} %compare_convert_fusion.keep_ref, bf16[160,128]{1,0:T(8,128)(2,1)} %constant.277.first_ref.back_first_ref.refs_9_, bf16[160,128]{1,0:T(8,128)(2,1)} %constant.278.second_ref.back_second_ref.refs_10_, f32[160,3]{1,0:T(8,128)} %constant.279.ones_ref), custom_call_target="tpu_custom_call" | custom-call | tf_op jit(solution)/shard_map/state/pallas_call | solution.py:562
  240.3 17.5 %collective-permute-done.9 = bf16[16,160,128]{2,1,0:T(8,128)(2,1)S(1)} collective-permute-done((bf16[16,160,128]{2,1,0:T(8,128)(2,1)}, bf16[16,160,128]{2,1,0:T(8,128)(2,1)S(1)}, u32[]{:S(2)}, u32[]{:S(2)}) %collective-permute-start.9) | collective-permute-done | bytes 655392 | tf_op jit(solution)/shard_map/ppermute | solution.py:531
  264.9 14.5 %inside.1.inside_ref = f32[512,2048]{1,0:T(8,128)} custom-call(bf16[512,4096]{1,0:T(8,128)(2,1)} %copy-done.1, f32[512,1]{1,0:T(8,128)} %fusion.50.keep_column_ref.refs_3_), custom_call_target="tpu_custom_call" | custom-call | tf_op jit(solution)/shard_map/inside/pallas_call | solution.py:577
  285.5 15.7 %mixer.1 = (bf16[512,2048]{1,0:T(8,128)(2,1)}, bf16[512,2048]{1,0:T(8,128)(2,1)}) custom-call(bf16[512,4096]{1,0:T(8,128)(2,1)} %copy-done.1, f32[512,2048]{1,0:T(8,128)} %inside.1.inside_ref, bf16[16,160,128]{2,1,0:T(8,128)(2,1)} %fusion.18.state_ref.refs_4_, bf16[8,4096]{1,0:T(8,128)(2,1)} %copy-done.24, f32[8,2048]{1,0:T(8,128)} %pad.36.taps_ref.refs_6_, ...), custom_call_target="tpu_custom_call" | custom-call | tf_op jit(solution)/shard_map/mixer/pallas_call | solution.py:589
  303.4 7.7 %fusion.129 = f32[512,1792]{1,0:T(8,128)S(1)} fusion(bf16[512,2048]{1,0:T(8,128)(2,1)} %get-tuple-element.127, bf16[1792,2048]{1,0:T(8,128)(2,1)} %pad_maximum_fusion.1), kind=kOutput, calls=%fused_computation.312 | convolution fusion | flops 3758096384 | bytes 13107200 | tf_op jit(solution)/shard_map/dot_general | solution.py:378
  326.8 29.1 %ffn_part.4 = (f32[512,1792]{1,0:T(8,128)}, f32[512,1792]{1,0:T(8,128)}, f32[2,512,16]{2,1,0:T(8,128)}, f32[2,16,608]{2,1,0:T(8,128)}, f32[2,16,608]{2,1,0:T(8,128)}, /*index=5*/f32[2,16,608]{2,1,0:T(8,128)}) custom-call(bf16[512,1792]{1,0:T(8,128)(2,1)} %copy-done.8, bf16[512,1792]{1,0:T(8,128)(2,1)} %copy-done.2, bf16[512,16]{1,0:T(8,128)(2,1)} %copy.96.refs_2_, ...), custom_call_target="tpu_custom_call" | custom-call | tf_op jit(solution)/shard_map/ffn_part/pallas_call | solution.py:340
  356.0 32.1 %ffn_part.5 = (f32[512,1792]{1,0:T(8,128)}, f32[512,1792]{1,0:T(8,128)}, f32[2,512,16]{2,1,0:T(8,128)}, f32[2,16,640]{2,1,0:T(8,128)}, f32[2,16,640]{2,1,0:T(8,128)}, /*index=5*/f32[2,16,640]{2,1,0:T(8,128)}) custom-call(bf16[512,1792]{1,0:T(8,128)(2,1)} %copy-done.8, ...), custom_call_target="tpu_custom_call", output_to_operand_aliasing={{0}: (12, {}), {1}: (13, {}), {2}: (14, {})} | custom-call | tf_op jit(solution)/shard_map/ffn_part/pallas_call | solution.py:340
  390.6 30.1 %ffn_part.6 = (f32[512,1792]{1,0:T(8,128)}, f32[512,1792]{1,0:T(8,128)}, f32[2,512,16]{2,1,0:T(8,128)}, f32[2,16,640]{2,1,0:T(8,128)}, f32[2,16,640]{2,1,0:T(8,128)}, /*index=5*/f32[2,16,640]{2,1,0:T(8,128)}) custom-call(bf16[512,1792]{1,0:T(8,128)(2,1)} %copy-done.8, ...), custom_call_target="tpu_custom_call", output_to_operand_aliasing={{0}: (12, {}), {1}: (13, {}), {2}: (14, {})} | custom-call | tf_op jit(solution)/shard_map/ffn_part/pallas_call | solution.py:340
  420.8 29.8 %ffn_part.7 = (f32[512,1792]{1,0:T(8,128)}, f32[512,1792]{1,0:T(8,128)}, f32[2,512,16]{2,1,0:T(8,128)}, f32[2,16,640]{2,1,0:T(8,128)}, f32[2,16,640]{2,1,0:T(8,128)}, /*index=5*/f32[2,16,640]{2,1,0:T(8,128)}) custom-call(bf16[512,1792]{1,0:T(8,128)(2,1)} %copy-done.8, ...), custom_call_target="tpu_custom_call", output_to_operand_aliasing={{0}: (12, {}), {1}: (13, {}), {2}: (14, {})} | custom-call | tf_op jit(solution)/shard_map/ffn_part/pallas_call | solution.py:340
  461.1 8.6 %add_convert_fusion.1.grad_ref.refs_2_ = bf16[512,2048]{1,0:T(8,128)(2,1)} fusion(f32[512,2048]{1,0:T(8,128)S(1)} %fusion.130, bf16[512,1792]{1,0:T(8,128)(2,1)S(1)} %add_convert_fusion.2, bf16[1792,2048]{1,0:T(8,128)(2,1)} %pad_maximum_fusion.1), kind=kOutput, calls=%fused_computation.9 | convolution fusion | flops 3760193536 | bytes 15466496 | tf_op jit(solution)/shard_map/dot_general | solution.py:378
  469.7 13.9 %back_state.1 = (bf16[512,2048]{1,0:T(8,128)(2,1)}, f32[16,160,128]{2,1,0:T(8,128)}, f32[8,2048]{1,0:T(8,128)}) custom-call(bf16[512,4096]{1,0:T(8,128)(2,1)} %copy-done.1, bf16[512,2048]{1,0:T(8,128)(2,1)} %get-tuple-element.126.kept_ref, bf16[512,2048]{1,0:T(8,128)(2,1)} %add_convert_fusion.1.grad_ref.refs_2_, ...), custom_call_target="tpu_custom_call" | custom-call | tf_op jit(solution)/shard_map/back_state/pallas_call | solution.py:646
  490.8 15.1 %back_inside.2.refs_12_ = bf16[512,4096]{1,0:T(8,128)(2,1)} custom-call(bf16[512,4096]{1,0:T(8,128)(2,1)} %copy-done.1, bf16[512,2048]{1,0:T(8,128)(2,1)} %get-tuple-element.155.scaled_ref.refs_1_, bf16[512,2048]{1,0:T(8,128)(2,1)} %add_convert_fusion.1.grad_ref.refs_2_, f32[512,1]{1,0:T(8,128)} %fusion.50.keep_column_ref.refs_3_, ...), custom_call_target="tpu_custom_call" | custom-call | tf_op jit(solution)/shard_map/back_inside/pallas_call | solution.py:696
  524.9 15.0 %back_inside.3.part_ref = bf16[512,4096]{1,0:T(8,128)(2,1)} custom-call(bf16[512,4096]{1,0:T(8,128)(2,1)} %copy-done.1, bf16[512,2048]{1,0:T(8,128)(2,1)} %get-tuple-element.155.scaled_ref.refs_1_, bf16[512,2048]{1,0:T(8,128)(2,1)} %add_convert_fusion.1.grad_ref.refs_2_, f32[512,1]{1,0:T(8,128)} %fusion.50.keep_column_ref.refs_3_, ...), custom_call_target="tpu_custom_call", output_to_operand_aliasing={{}: (12, {})} | custom-call | tf_op jit(solution)/shard_map/back_inside/pallas_call | solution.py:696
  541.4 16.7 %back_later.1 = bf16[512,4096]{1,0:T(8,128)(2,1)} custom-call(bf16[512,4096]{1,0:T(8,128)(2,1)} %copy-done.1, bf16[512,4096]{1,0:T(8,128)(2,1)} %back_inside.3.part_ref, f32[512,1]{1,0:T(8,128)} %fusion.50.keep_column_ref.refs_3_, bf16[16,160,128]{2,1,0:T(8,128)(2,1)} %fusion.22.later_ref, f32[8,2048]{1,0:T(8,128)} %collective-permute-done.14.edge_ref, ...), custom_call_target="tpu_custom_call" | custom-call | tf_op jit(solution)/shard_map/back_later/pallas_call | solution.py:730
  570.1 15.9 %fusion.8 = (f32[512]{0:T(512)S(1)}, f32[512,1792]{1,0:T(8,128)}) fusion(bf16[512,1792]{1,0:T(8,128)(2,1)S(1)} %bitcast.338, f32[1792]{0:T(1024)S(1)} %copy-done.74, f32[512,1792]{1,0:T(8,128)} %fusion.13, bf16[512,4096]{1,0:T(8,128)(2,1)} %back_later.1, bf16[1792,4096]{1,0:T(8,128)(2,1)} %pad_maximum_fusion), kind=kOutput, calls=%fused_computation.18 | convolution fusion | flops 7520779776 | bytes 28058624 | tf_op jit(solution)/shard_map/dot_general | solution.py:378
  593.3 5.1 all-to-all-start.4
  602.1 13.9 %all-to-all-done.4 = bf16[8,64,640]{2,1,0:T(8,128)(2,1)} async-done(((bf16[8,64,640]{2,1,0:T(8,128)(2,1)}), bf16[8,64,640]{2,1,0:T(8,128)(2,1)}, u32[]{:S(2)}, u32[]{:S(2)}) %all-to-all-start.4) | async-done | bytes 655392 | tf_op jit(solution)/shard_map/all_to_all | solution.py:728
  633.7 11.6 %collective-permute-done.15 = bf16[16,6912]{1,0:T(8,128)(2,1)S(1)} collective-permute-done((bf16[16,6912]{1,0:T(8,128)(2,1)S(1)}, bf16[16,6912]{1,0:T(8,128)(2,1)S(1)}, u32[]{:S(2)}, u32[]{:S(2)}) %collective-permute-start.15) | collective-permute-done | bytes 221216 | tf_op jit(solution)/shard_map/ppermute | solution.py:668
  645.4 12.1 %collective-permute-done.16 = bf16[16,6912]{1,0:T(8,128)(2,1)} collective-permute-done((bf16[16,6912]{1,0:T(8,128)(2,1)S(1)}, bf16[16,6912]{1,0:T(8,128)(2,1)}, u32[]{:S(2)}, u32[]{:S(2)}) %collective-permute-start.16) | collective-permute-done | bytes 221216 | tf_op jit(solution)/shard_map/ppermute | solution.py:668
  668.4 6.5 collective-permute-done.19
  683.6 8.2 %all-to-all-start.6 = ((bf16[8,64,512]{2,1,0:T(8,128)(2,1)}), bf16[8,64,512]{2,1,0:T(8,128)(2,1)S(1)}, u32[]{:S(2)}, u32[]{:S(2)}) async-start(bf16[8,64,512]{2,1,0:T(8,128)(2,1)} %bitcast.75), calls=%async_computation.6 | async-start | bytes 1048576 | tf_op jit(solution)/shard_map/all_to_all | solution.py:728
  697.6 8.9 %all-to-all-done.6 = bf16[8,64,512]{2,1,0:T(8,128)(2,1)S(1)} async-done(((bf16[8,64,512]{2,1,0:T(8,128)(2,1)}), bf16[8,64,512]{2,1,0:T(8,128)(2,1)S(1)}, u32[]{:S(2)}, u32[]{:S(2)}) %all-to-all-start.6) | async-done | bytes 524320 | tf_op jit(solution)/shard_map/all_to_all | solution.py:728
  (443 shorter events, 250.5 us)
Async XLA Ops:
  7.2 140.2 %all-gather.6.cloned.1.call-start = ((), (), s32[]{:S(2)}) async-start(), calls=%async_computation.7 | async-start | bytes 6193152 | tf_op jit(solution)/shard_map/all_gather | solution.py:443
  16.7 21.9 %collective-permute-start = (bf16[224,1536]{1,0:T(8,128)(2,1)}, bf16[224,1536]{1,0:T(8,128)(2,1)S(1)}, u32[]{:S(2)}, u32[]{:S(2)}) collective-permute-start(bf16[224,1536]{1,0:T(8,128)(2,1)} %bitcast_dynamic-update-slice_fusion), channel_id=1, source_target_pairs={{1,0},{2,1},{3,2},{0,3},{5,4},{6,5},{7,6},{4,7},{9,8},{10,9},{11,1... | collective-permute-start | bytes 2064392 | tf_op jit(solution)/shard_map/ppermute | solution.py:437
  39.6 114.0 %all-gather.8.cloned.1.call-start = ((), (), s32[]{:S(2)}) async-start(), calls=%async_computation.8 | async-start | bytes 12386304 | tf_op jit(solution)/shard_map/all_gather | solution.py:443
  39.6 43.8 %collective-permute-start.1 = (bf16[224,1536]{1,0:T(8,128)(2,1)}, bf16[224,1536]{1,0:T(8,128)(2,1)S(1)}, u32[]{:S(2)}, u32[]{:S(2)}) collective-permute-start(bf16[224,1536]{1,0:T(8,128)(2,1)} %copy-done.22), channel_id=1, source_target_pairs={{1,0},{2,1},{3,2},{0,3},{5,4},{6,5},{7,6},{4,7},{9,8},{10,9},{11,1... | collective-permute-start | bytes 2064392 | tf_op jit(solution)/shard_map/ppermute | solution.py:437
  42.0 41.4 %collective-permute-start.2 = (bf16[224,1536]{1,0:T(8,128)(2,1)}, bf16[224,1536]{1,0:T(8,128)(2,1)}, u32[]{:S(2)}, u32[]{:S(2)}) collective-permute-start(bf16[224,1536]{1,0:T(8,128)(2,1)} %bitcast_dynamic-update-slice_fusion), channel_id=1, source_target_pairs={{0,1},{1,2},{2,3},{3,0},{4,5},{5,6},{6,7},{7,4},{8,9},{9,10},{10,1... | collective-permute-start | bytes 2064392 | tf_op jit(solution)/shard_map/ppermute | solution.py:440
  42.0 35.9 %collective-permute-start.3 = (bf16[16,5120]{1,0:T(8,128)(2,1)}, bf16[16,5120]{1,0:T(8,128)(2,1)S(1)}, u32[]{:S(2)}, u32[]{:S(2)}) collective-permute-start(bf16[16,5120]{1,0:T(8,128)(2,1)} %concatenate.119), channel_id=1, source_target_pairs={{0,3},{1,0},{2,1},{3,2},{4,7},{5,4},{6,5},{7,6},{8,11},{9,8},{10,9... | collective-permute-start | bytes 491528 | tf_op jit(solution)/shard_map/ppermute | solution.py:477
  45.8 37.6 %collective-permute-start.4 = (bf16[16,5120]{1,0:T(8,128)(2,1)}, bf16[16,5120]{1,0:T(8,128)(2,1)}, u32[]{:S(2)}, u32[]{:S(2)}) collective-permute-start(bf16[16,5120]{1,0:T(8,128)(2,1)} %concatenate.120), channel_id=1, source_target_pairs={{0,2},{1,3},{2,0},{3,1},{4,6},{5,7},{6,4},{7,5},{8,10},{9,11},{10,... | collective-permute-start | bytes 491528 | tf_op jit(solution)/shard_map/ppermute | solution.py:477
  45.8 37.6 %collective-permute-start.5 = (bf16[16,5120]{1,0:T(8,128)(2,1)}, bf16[16,5120]{1,0:T(8,128)(2,1)}, u32[]{:S(2)}, u32[]{:S(2)}) collective-permute-start(bf16[16,5120]{1,0:T(8,128)(2,1)} %concatenate.121), channel_id=1, source_target_pairs={{0,1},{1,2},{2,3},{3,0},{4,5},{5,6},{6,7},{7,4},{8,9},{9,10},{10,1... | collective-permute-start | bytes 491528 | tf_op jit(solution)/shard_map/ppermute | solution.py:477
  86.7 269.3 %all-gather.14.cloned.1.call-start = ((), (), s32[]{:S(2)}) async-start(), calls=%async_computation.11 | async-start | bytes 15482880 | tf_op jit(solution)/shard_map/all_gather | solution.py:443
  86.8 38.7 %collective-permute-start.6 = (bf16[480,1792]{1,0:T(8,128)(2,1)}, bf16[480,1792]{1,0:T(8,128)(2,1)S(1)}, u32[]{:S(2)}, u32[]{:S(2)}) collective-permute-start(bf16[480,1792]{1,0:T(8,128)(2,1)} %maximum_select_fusion), channel_id=1, source_target_pairs={{1,0},{2,1},{3,2},{0,3},{5,4},{6,5},{7,6},{4,7},{9,8},{10,9},{11,1... | collective-permute-start | bytes 5160968 | tf_op jit(solution)/shard_map/ppermute | solution.py:437
  131.3 47.8 %all-to-all-start = ((bf16[8,64,1792]{2,1,0:T(8,128)(2,1)}), bf16[8,64,1792]{2,1,0:T(8,128)(2,1)S(1)}, u32[]{:S(2)}, u32[]{:S(2)}) async-start(bf16[8,64,1792]{2,1,0:T(8,128)(2,1)} %param.23), calls=%async_computation | async-start | bytes 3670016 | tf_op jit(solution)/shard_map/all_to_all | solution.py:446
  136.3 254.4 %all-gather.12.cloned.1.call-start = ((), (), s32[]{:S(2)}) async-start(), calls=%async_computation.10 | async-start | bytes 15482880 | tf_op jit(solution)/shard_map/all_gather | solution.py:443
  179.1 42.5 %collective-permute-start.7 = (bf16[480,1792]{1,0:T(8,128)(2,1)}, bf16[480,1792]{1,0:T(8,128)(2,1)}, u32[]{:S(2)}, u32[]{:S(2)}) collective-permute-start(bf16[480,1792]{1,0:T(8,128)(2,1)} %maximum_select_fusion), channel_id=1, source_target_pairs={{0,1},{1,2},{2,3},{3,0},{4,5},{5,6},{6,7},{7,4},{8,9},{9,10},{10,1... | collective-permute-start | bytes 5160968 | tf_op jit(solution)/shard_map/ppermute | solution.py:440
  225.0 56.6 %all-to-all-start.1 = ((bf16[8,64,1792]{2,1,0:T(8,128)(2,1)}), bf16[8,64,1792]{2,1,0:T(8,128)(2,1)}, u32[]{:S(2)}, u32[]{:S(2)}) async-start(bf16[8,64,1792]{2,1,0:T(8,128)(2,1)} %param.24), calls=%async_computation.1 | async-start | bytes 3670016 | tf_op jit(solution)/shard_map/all_to_all | solution.py:446
  229.4 191.4 %all-gather.10.cloned.1.call-start = ((), (), s32[]{:S(2)}) async-start(), calls=%async_computation.9 | async-start | bytes 15482880 | tf_op jit(solution)/shard_map/all_gather | solution.py:443
  234.4 23.5 %collective-permute-start.9 = (bf16[16,160,128]{2,1,0:T(8,128)(2,1)}, bf16[16,160,128]{2,1,0:T(8,128)(2,1)S(1)}, u32[]{:S(2)}, u32[]{:S(2)}) collective-permute-start(bf16[16,160,128]{2,1,0:T(8,128)(2,1)} %convert_element_type.296), channel_id=1, source_target_pairs={{0,8},{8,0},{16,24},{24,16},{1,9},{9,1},{17,25},{25,17},{2,10},{10... | collective-permute-start | bytes 1966088 | tf_op jit(solution)/shard_map/ppermute | solution.py:531
  260.1 19.3 %collective-permute-start.10 = (bf16[16,160,128]{2,1,0:T(8,128)(2,1)}, bf16[16,160,128]{2,1,0:T(8,128)(2,1)}, u32[]{:S(2)}, u32[]{:S(2)}) collective-permute-start(bf16[16,160,128]{2,1,0:T(8,128)(2,1)} %fusion.19), channel_id=1, source_target_pairs={{0,16},{8,24},{1,17},{9,25},{2,18},{10,26},{3,19},{11,27},{4,20},{... | collective-permute-start | bytes 1966088 | tf_op jit(solution)/shard_map/ppermute | solution.py:531
  281.6 38.9 %collective-permute-start.11 = (bf16[480,1792]{1,0:T(8,128)(2,1)}, bf16[480,1792]{1,0:T(8,128)(2,1)}, u32[]{:S(2)}, u32[]{:S(2)}) collective-permute-start(bf16[480,1792]{1,0:T(8,128)(2,1)} %copy-done.20), channel_id=1, source_target_pairs={{1,0},{2,1},{3,2},{0,3},{5,4},{6,5},{7,6},{4,7},{9,8},{10,9},{11,1... | collective-permute-start | bytes 5160968 | tf_op jit(solution)/shard_map/ppermute | solution.py:437
  485.9 23.6 %collective-permute-start.12 = (bf16[16,160,128]{2,1,0:T(8,128)(2,1)}, bf16[16,160,128]{2,1,0:T(8,128)(2,1)S(1)}, u32[]{:S(2)}, u32[]{:S(2)}) collective-permute-start(bf16[16,160,128]{2,1,0:T(8,128)(2,1)} %convert_element_type.314), channel_id=1, source_target_pairs={{0,8},{8,0},{16,24},{24,16},{1,9},{9,1},{17,25},{25,17},{2,10},{10... | collective-permute-start | bytes 1966088 | tf_op jit(solution)/shard_map/ppermute | solution.py:531
  515.4 42.7 %all-to-all-start.2 = ((bf16[8,64,896]{2,1,0:T(8,128)(2,1)}), bf16[8,64,896]{2,1,0:T(8,128)(2,1)S(1)}, u32[]{:S(2)}, u32[]{:S(2)}) async-start(bf16[8,64,896]{2,1,0:T(8,128)(2,1)} %bitcast.71), calls=%async_computation.2 | async-start | bytes 1835008 | tf_op jit(solution)/shard_map/all_to_all | solution.py:728
  521.3 19.0 %collective-permute-start.13 = (bf16[16,160,128]{2,1,0:T(8,128)(2,1)S(1)}, bf16[16,160,128]{2,1,0:T(8,128)(2,1)S(1)}, u32[]{:S(2)}, u32[]{:S(2)}) collective-permute-start(bf16[16,160,128]{2,1,0:T(8,128)(2,1)S(1)} %fusion.20), channel_id=1, source_target_pairs={{16,0},{24,8},{17,1},{25,9},{18,2},{26,10},{19,3},{27,11},{20,4},{... | collective-permute-start | bytes 1966088 | tf_op jit(solution)/shard_map/ppermute | solution.py:531
  523.5 17.9 %collective-permute-start.14 = (f32[8,2048]{1,0:T(8,128)}, f32[8,2048]{1,0:T(8,128)}, u32[]{:S(2)}, u32[]{:S(2)}) collective-permute-start(f32[8,2048]{1,0:T(8,128)} %get-tuple-element.158), channel_id=1, source_target_pairs={{8,0},{16,8},{24,16},{9,1},{17,9},{25,17},{10,2},{18,10},{26,18},{... | collective-permute-start | bytes 196616 | tf_op jit(solution)/shard_map/ppermute | solution.py:527
  558.1 32.7 %all-to-all-start.3 = ((bf16[8,64,896]{2,1,0:T(8,128)(2,1)}), bf16[8,64,896]{2,1,0:T(8,128)(2,1)}, u32[]{:S(2)}, u32[]{:S(2)}) async-start(bf16[8,64,896]{2,1,0:T(8,128)(2,1)} %bitcast.72), calls=%async_computation.3 | async-start | bytes 1835008 | tf_op jit(solution)/shard_map/all_to_all | solution.py:728
  593.3 22.8 %all-to-all-start.4 = ((bf16[8,64,640]{2,1,0:T(8,128)(2,1)}), bf16[8,64,640]{2,1,0:T(8,128)(2,1)}, u32[]{:S(2)}, u32[]{:S(2)}) async-start(bf16[8,64,640]{2,1,0:T(8,128)(2,1)} %bitcast.345), calls=%async_computation.4 | async-start | bytes 1310720 | tf_op jit(solution)/shard_map/all_to_all | solution.py:728
  620.9 37.8 %all-to-all-start.5 = ((bf16[8,64,640]{2,1,0:T(8,128)(2,1)}), bf16[8,64,640]{2,1,0:T(8,128)(2,1)S(1)}, u32[]{:S(2)}, u32[]{:S(2)}) async-start(bf16[8,64,640]{2,1,0:T(8,128)(2,1)} %bitcast.74), calls=%async_computation.5 | async-start | bytes 1310720 | tf_op jit(solution)/shard_map/all_to_all | solution.py:728
  625.4 20.0 %collective-permute-start.15 = (bf16[16,6912]{1,0:T(8,128)(2,1)S(1)}, bf16[16,6912]{1,0:T(8,128)(2,1)S(1)}, u32[]{:S(2)}, u32[]{:S(2)}) collective-permute-start(bf16[16,6912]{1,0:T(8,128)(2,1)S(1)} %concatenate.146), channel_id=1, source_target_pairs={{0,1},{1,2},{2,3},{3,0},{4,5},{5,6},{6,7},{7,4},{8,9},{9,10},{10,1... | collective-permute-start | bytes 663560 | tf_op jit(solution)/shard_map/ppermute | solution.py:668
  627.5 30.0 %collective-permute-start.16 = (bf16[16,6912]{1,0:T(8,128)(2,1)S(1)}, bf16[16,6912]{1,0:T(8,128)(2,1)}, u32[]{:S(2)}, u32[]{:S(2)}) collective-permute-start(bf16[16,6912]{1,0:T(8,128)(2,1)S(1)} %concatenate.148), channel_id=1, source_target_pairs={{0,2},{1,3},{2,0},{3,1},{4,6},{5,7},{6,4},{7,5},{8,10},{9,11},{10,... | collective-permute-start | bytes 663560 | tf_op jit(solution)/shard_map/ppermute | solution.py:668
  630.9 26.6 %collective-permute-start.17 = (bf16[16,6912]{1,0:T(8,128)(2,1)S(1)}, bf16[16,6912]{1,0:T(8,128)(2,1)}, u32[]{:S(2)}, u32[]{:S(2)}) collective-permute-start(bf16[16,6912]{1,0:T(8,128)(2,1)S(1)} %concatenate.150), channel_id=1, source_target_pairs={{0,3},{1,0},{2,1},{3,2},{4,7},{5,4},{6,5},{7,6},{8,11},{9,8},{10,9... | collective-permute-start | bytes 663560 | tf_op jit(solution)/shard_map/ppermute | solution.py:668
  676.8 15.0 %collective-permute-start.21 = (bf16[16,6912]{1,0:T(8,128)(2,1)S(1)}, bf16[16,6912]{1,0:T(8,128)(2,1)S(1)}, u32[]{:S(2)}, u32[]{:S(2)}) collective-permute-start(bf16[16,6912]{1,0:T(8,128)(2,1)S(1)} %get-tuple-element.189), channel_id=1, source_target_pairs={{0,8},{8,0},{16,24},{24,16},{1,9},{9,1},{17,25},{25,17},{2,10},{10... | collective-permute-start | bytes 663560 | tf_op jit(solution)/shard_map/ppermute | solution.py:531
  678.3 13.6 %collective-permute-start.22 = (bf16[16,6912]{1,0:T(8,128)(2,1)S(1)}, bf16[16,6912]{1,0:T(8,128)(2,1)}, u32[]{:S(2)}, u32[]{:S(2)}) collective-permute-start(bf16[16,6912]{1,0:T(8,128)(2,1)S(1)} %get-tuple-element.189), channel_id=1, source_target_pairs={{0,16},{8,24},{16,0},{24,8},{1,17},{9,25},{17,1},{25,9},{2,18},{10... | collective-permute-start | bytes 663560 | tf_op jit(solution)/shard_map/ppermute | solution.py:531
  683.6 22.9 %all-to-all-start.6 = ((bf16[8,64,512]{2,1,0:T(8,128)(2,1)}), bf16[8,64,512]{2,1,0:T(8,128)(2,1)S(1)}, u32[]{:S(2)}, u32[]{:S(2)}) async-start(bf16[8,64,512]{2,1,0:T(8,128)(2,1)} %bitcast.75), calls=%async_computation.6 | async-start | bytes 1048576 | tf_op jit(solution)/shard_map/all_to_all | solution.py:728
  693.1 16.8 %collective-permute-start.24 = (bf16[64,6912]{1,0:T(8,128)(2,1)S(1)}, bf16[64,6912]{1,0:T(8,128)(2,1)}, u32[]{:S(2)}, u32[]{:S(2)}) collective-permute-start(bf16[64,6912]{1,0:T(8,128)(2,1)S(1)} %pad_maximum_fusion.5), channel_id=1, source_target_pairs={{0,4},{4,0},{1,5},{5,1},{2,6},{6,2},{3,7},{7,3},{8,12},{12,8},{9,1... | collective-permute-start | bytes 2654216 | tf_op jit(solution)/shard_map/ppermute | solution.py:682
  (86 other events, 1563.3 us)
Sparse Core Ops, SparseCore 0:
  39.7 41.9 all-gather.5
  86.8 66.6 all-gather.7
  155.4 77.7 all-gather.13
  235.0 82.8 all-gather.11
  320.6 78.6 all-gather.9

commit v5 on v4

--- a/solution.py
+++ b/solution.py
@@ -746,15 +746,9 @@
         dot(packed_grad, in_weights, TURNED) + dot(enter_grad, inward_first)
     )
     input_grad = (branch.astype(F32) + rms_back(inputs, gain_first, normed_grad)).astype(BF)
-    input_grad, back_last, late_grad, late_enter = barrier((input_grad, back_last, packed_grad, enter_grad))
-    third = -(-width // 384) * 128
-    input_first = send_back(input_grad[:, :third])
-    input_next = send_back(after(input_grad[:, third : 2 * third], input_first))
-    input_last = send_back(after(input_grad[:, 2 * third :], input_next))
-    late_grad, late_enter = barrier((late_grad, late_enter, input_first))[:2]
-    grad_inward_up = dot(dot(enter, late_grad, ROWS).astype(BF).reshape(-1, PACK), order, TURNED).astype(BF)
+    grad_inward_up = dot(dot(enter, packed_grad, ROWS).astype(BF).reshape(-1, PACK), order, TURNED).astype(BF)
     grad_inward_up = grad_inward_up.reshape(ranks, -1)
-    grad_inward_down = dot(late_enter, normed, ROWS)
+    grad_inward_down = dot(enter_grad, normed, ROWS)
 
     places = exchange_places(
         lambda j: jnp.concatenate(
@@ -765,12 +759,15 @@
             axis=1,
         )
     )
-    sums = exchange_chips(after(places, input_next))
+    input_grad, places, back_last = barrier((input_grad, places, back_last))
+    input_first = send_back(input_grad[:, : width // 2])
+    input_last = send_back(after(input_grad[:, width // 2 :], input_first))
+    sums = exchange_chips(places)
     at = np.cumsum([0, 2 * hidden_here, hidden_here, out_here, shard, shard, shard, in_width, shard])
     grads = [sums[:, :, at[n] : at[n + 1]] for n in range(8)]
     return (
         jnp.concatenate([back_first, back_last], axis=2).astype(F32),
-        jnp.concatenate([input_first, input_next, input_last], axis=2).astype(F32),
+        jnp.concatenate([input_first, input_last], axis=2).astype(F32),
         grads[7],
         grads[6],
         grads[2],

time: 735 us -> 704 us (0.958)
  waiting for transfers between devices: 155 us -> 125 us
  local copies, waits for them, and re-layouts: 77.8 us -> 88 us
  starting transfers between devices: 85.4 us -> 76.9 us
    ppermute x3, waiting for transfers between devices: 23.7 us -> 0.99 us  [exchange_places(): got.append(lax.ppermute(pieces(j).astype(BF), 'wa', pairs))]
    concatenate x13, local copies, waits for them, and re-layouts: 6.74 us -> 14.6 us  [on_device(): jnp.concatenate(expand_grads[j] + [outer_grads[0][:, j * out_here:(j + 1)...]
    all_to_all x5 -> x4, waiting for transfers between devices: 22.8 us -> 14.9 us  [send_back(): lax.all_to_all(values.reshape(sequences, slot_rows, -1), COLUMN, 0, 0, ti...]
    all_to_all x5 -> x4, starting transfers between devices: 26.9 us -> 20.2 us  [send_back(): lax.all_to_all(values.reshape(sequences, slot_rows, -1), COLUMN, 0, 0, ti...]
  transfers between devices with their start and end apart: 37 -> 36, of which waited for: 15 -> 16; matrix products, arithmetic and copies ran while one was open for 24% -> 26% of each run, Pallas kernels for 25% -> 26%
where the time goes in v5:
time: 704 us; the launch traced here: 693 us
  Pallas kernels  225 us (32%)
  waiting for transfers between devices  125 us (18%)
  matrix products  99.3 us (14%)
  local copies, waits for them, and re-layouts  88 us (12%)
  starting transfers between devices  76.9 us (11%)
  other arithmetic  56.1 us (8%)
  between operations  23.5 us (3%)
    pallas_call x4, Pallas kernels, ffn_part(): pl.pallas_call(later_ffn_kernel if sums else first_ffn_kernel, grid=(step...  121 us
    dot_general x48, matrix products, dot(): lax.dot_general(left, right, (dims, ((), ())), preferred_element_type=F32)  99.3 us
    ppermute x4, waiting for transfers between devices, from_next(): return lax.ppermute(piece, 'wa', next_place)  32.5 us
    ppermute x3, waiting for transfers between devices, on_device(): tables.append(lax.ppermute(prepared[j], 'wa', pairs))  30.9 us
    pallas_call x2, Pallas kernels, back_inside(): pl.pallas_call(back_inside_kernel if old is None else lambda *refs: back_...  30.1 us
    ppermute x10, waiting for transfers between devices, flip(): lax.ppermute(piece, CHIPS, [(i, i ^ bit) for i in range(chips) if keep_pa...  24.6 us
    all_to_all x4, starting transfers between devices, send_back(): lax.all_to_all(values.reshape(sequences, slot_rows, -1), COLUMN, 0, 0, ti...  20.2 us
    ppermute x10, starting transfers between devices, flip(): lax.ppermute(piece, CHIPS, [(i, i ^ bit) for i in range(chips) if keep_pa...  17.6 us
  transfers between devices with their start and end apart: 36, of which 16 were waited for; matrix products, arithmetic and copies ran while one was open for 26% of the time, Pallas kernels for 26%

profile of v5, /device:TPU:0, one launch (start us, length us, event | category | flops | bytes accessed | tf_op | source)
XLA Modules:
  0.0 693.2 jit_solution(9640256687434799991)
XLA Ops:
  16.7 5.1 collective-permute-start
  52.5 25.4 %collective-permute-done.3 = bf16[16,5120]{1,0:T(8,128)(2,1)S(1)} collective-permute-done((bf16[16,5120]{1,0:T(8,128)(2,1)}, bf16[16,5120]{1,0:T(8,128)(2,1)S(1)}, u32[]{:S(2)}, u32[]{:S(2)}) %collective-permute-start.3) | collective-permute-done | bytes 163872 | tf_op jit(solution)/shard_map/ppermute | solution.py:477
  77.9 5.5 collective-permute-done.4
  95.5 29.9 %collective-permute-done.6 = bf16[480,1792]{1,0:T(8,128)(2,1)S(1)} collective-permute-done((bf16[480,1792]{1,0:T(8,128)(2,1)}, bf16[480,1792]{1,0:T(8,128)(2,1)S(1)}, u32[]{:S(2)}, u32[]{:S(2)}) %collective-permute-start.6) | collective-permute-done | bytes 1720352 | tf_op jit(solution)/shard_map/ppermute | solution.py:437
  131.3 5.0 all-to-all-start
  141.4 6.0 copy.83
  147.4 6.1 all-gather.8.cloned.1.call-done
  156.2 6.5 pad_maximum_fusion.1
  165.3 6.2 pad_maximum_fusion
  171.4 7.6 %all-to-all-done = bf16[8,64,1792]{2,1,0:T(8,128)(2,1)S(1)} async-done(((bf16[8,64,1792]{2,1,0:T(8,128)(2,1)}), bf16[8,64,1792]{2,1,0:T(8,128)(2,1)S(1)}, u32[]{:S(2)}, u32[]{:S(2)}) %all-to-all-start) | async-done | bytes 1835040 | tf_op jit(solution)/shard_map/all_to_all | solution.py:446
  180.4 11.1 %fusion.119 = f32[512,4096]{1,0:T(8,128)S(1)} fusion(bf16[1792,4096]{1,0:T(8,128)(2,1)} %pad_maximum_fusion, bf16[512,1792]{1,0:T(8,128)(2,1)S(1)} %bitcast.334, f32[1792]{0:T(1024)S(1)} %copy-done.67, f32[512]{0:T(512)S(1)} %get-tuple-element.277), kind=kOutput, calls=%fused_computation.305 | convolution fusion | flops 7519862784 | bytes 24912896 | tf_op jit(solution)/shard_map/dot_general | solution.py:378
  196.3 12.6 %state.1 = f32[16,160,128]{2,1,0:T(8,128)} custom-call(bf16[512,4096]{1,0:T(8,128)(2,1)} %copy-done.1, f32[1,512]{1,0:T(1,128)} %compare_convert_fusion.keep_ref, bf16[160,128]{1,0:T(8,128)(2,1)} %constant.277.first_ref.back_first_ref.refs_9_, bf16[160,128]{1,0:T(8,128)(2,1)} %constant.278.second_ref.back_second_ref.refs_10_, f32[160,3]{1,0:T(8,128)} %constant.279.ones_ref), custom_call_target="tpu_custom_call" | custom-call | tf_op jit(solution)/shard_map/state/pallas_call | solution.py:562
  240.1 17.3 %collective-permute-done.9 = bf16[16,160,128]{2,1,0:T(8,128)(2,1)S(1)} collective-permute-done((bf16[16,160,128]{2,1,0:T(8,128)(2,1)}, bf16[16,160,128]{2,1,0:T(8,128)(2,1)S(1)}, u32[]{:S(2)}, u32[]{:S(2)}) %collective-permute-start.9) | collective-permute-done | bytes 655392 | tf_op jit(solution)/shard_map/ppermute | solution.py:531
  264.3 14.5 %inside.1.inside_ref = f32[512,2048]{1,0:T(8,128)} custom-call(bf16[512,4096]{1,0:T(8,128)(2,1)} %copy-done.1, f32[512,1]{1,0:T(8,128)} %fusion.48.keep_column_ref.refs_3_), custom_call_target="tpu_custom_call" | custom-call | tf_op jit(solution)/shard_map/inside/pallas_call | solution.py:577
  285.3 15.6 %mixer.1 = (bf16[512,2048]{1,0:T(8,128)(2,1)}, bf16[512,2048]{1,0:T(8,128)(2,1)}) custom-call(bf16[512,4096]{1,0:T(8,128)(2,1)} %copy-done.1, f32[512,2048]{1,0:T(8,128)} %inside.1.inside_ref, bf16[16,160,128]{2,1,0:T(8,128)(2,1)} %fusion.16.state_ref.refs_4_, bf16[8,4096]{1,0:T(8,128)(2,1)} %copy-done.28, f32[8,2048]{1,0:T(8,128)} %pad.36.taps_ref.refs_6_, ...), custom_call_target="tpu_custom_call" | custom-call | tf_op jit(solution)/shard_map/mixer/pallas_call | solution.py:589
  303.1 7.7 %fusion.128 = f32[512,1792]{1,0:T(8,128)S(1)} fusion(bf16[512,2048]{1,0:T(8,128)(2,1)} %get-tuple-element.122, bf16[1792,2048]{1,0:T(8,128)(2,1)} %pad_maximum_fusion.1), kind=kOutput, calls=%fused_computation.312 | convolution fusion | flops 3758096384 | bytes 13107200 | tf_op jit(solution)/shard_map/dot_general | solution.py:378
  327.4 29.5 %ffn_part.4 = (f32[512,1792]{1,0:T(8,128)}, f32[512,1792]{1,0:T(8,128)}, f32[2,512,16]{2,1,0:T(8,128)}, f32[2,16,608]{2,1,0:T(8,128)}, f32[2,16,608]{2,1,0:T(8,128)}, /*index=5*/f32[2,16,608]{2,1,0:T(8,128)}) custom-call(bf16[512,1792]{1,0:T(8,128)(2,1)} %copy-done.8, bf16[512,1792]{1,0:T(8,128)(2,1)} %copy-done.2, bf16[512,16]{1,0:T(8,128)(2,1)} %copy.96.refs_2_, ...), custom_call_target="tpu_custom_call" | custom-call | tf_op jit(solution)/shard_map/ffn_part/pallas_call | solution.py:340
  357.0 31.9 %ffn_part.5 = (f32[512,1792]{1,0:T(8,128)}, f32[512,1792]{1,0:T(8,128)}, f32[2,512,16]{2,1,0:T(8,128)}, f32[2,16,640]{2,1,0:T(8,128)}, f32[2,16,640]{2,1,0:T(8,128)}, /*index=5*/f32[2,16,640]{2,1,0:T(8,128)}) custom-call(bf16[512,1792]{1,0:T(8,128)(2,1)} %copy-done.8, ...), custom_call_target="tpu_custom_call", output_to_operand_aliasing={{0}: (12, {}), {1}: (13, {}), {2}: (14, {})} | custom-call | tf_op jit(solution)/shard_map/ffn_part/pallas_call | solution.py:340
  393.1 30.2 %ffn_part.6 = (f32[512,1792]{1,0:T(8,128)}, f32[512,1792]{1,0:T(8,128)}, f32[2,512,16]{2,1,0:T(8,128)}, f32[2,16,640]{2,1,0:T(8,128)}, f32[2,16,640]{2,1,0:T(8,128)}, /*index=5*/f32[2,16,640]{2,1,0:T(8,128)}) custom-call(bf16[512,1792]{1,0:T(8,128)(2,1)} %copy-done.8, ...), custom_call_target="tpu_custom_call", output_to_operand_aliasing={{0}: (12, {}), {1}: (13, {}), {2}: (14, {})} | custom-call | tf_op jit(solution)/shard_map/ffn_part/pallas_call | solution.py:340
  425.1 29.7 %ffn_part.7 = (f32[512,1792]{1,0:T(8,128)}, f32[512,1792]{1,0:T(8,128)}, f32[2,512,16]{2,1,0:T(8,128)}, f32[2,16,640]{2,1,0:T(8,128)}, f32[2,16,640]{2,1,0:T(8,128)}, /*index=5*/f32[2,16,640]{2,1,0:T(8,128)}) custom-call(bf16[512,1792]{1,0:T(8,128)(2,1)} %copy-done.8, ...), custom_call_target="tpu_custom_call", output_to_operand_aliasing={{0}: (12, {}), {1}: (13, {}), {2}: (14, {})} | custom-call | tf_op jit(solution)/shard_map/ffn_part/pallas_call | solution.py:340
  465.4 8.6 %add_convert_fusion.1.grad_ref.refs_2_ = bf16[512,2048]{1,0:T(8,128)(2,1)} fusion(f32[512,2048]{1,0:T(8,128)S(1)} %fusion.129, bf16[512,1792]{1,0:T(8,128)(2,1)S(1)} %add_convert_fusion.2, bf16[1792,2048]{1,0:T(8,128)(2,1)} %pad_maximum_fusion.1), kind=kOutput, calls=%fused_computation.9 | convolution fusion | flops 3760193536 | bytes 15466496 | tf_op jit(solution)/shard_map/dot_general | solution.py:378
  474.0 13.9 %back_state.1 = (bf16[512,2048]{1,0:T(8,128)(2,1)}, f32[16,160,128]{2,1,0:T(8,128)}, f32[8,2048]{1,0:T(8,128)}) custom-call(bf16[512,4096]{1,0:T(8,128)(2,1)} %copy-done.1, bf16[512,2048]{1,0:T(8,128)(2,1)} %get-tuple-element.121.kept_ref, bf16[512,2048]{1,0:T(8,128)(2,1)} %add_convert_fusion.1.grad_ref.refs_2_, ...), custom_call_target="tpu_custom_call" | custom-call | tf_op jit(solution)/shard_map/back_state/pallas_call | solution.py:646
  494.3 15.0 %back_inside.2.refs_12_ = bf16[512,4096]{1,0:T(8,128)(2,1)} custom-call(bf16[512,4096]{1,0:T(8,128)(2,1)} %copy-done.1, bf16[512,2048]{1,0:T(8,128)(2,1)} %get-tuple-element.150.scaled_ref.refs_1_, bf16[512,2048]{1,0:T(8,128)(2,1)} %add_convert_fusion.1.grad_ref.refs_2_, f32[512,1]{1,0:T(8,128)} %fusion.48.keep_column_ref.refs_3_, ...), custom_call_target="tpu_custom_call" | custom-call | tf_op jit(solution)/shard_map/back_inside/pallas_call | solution.py:696
  518.9 4.8 all-to-all-start.2
  527.1 15.0 %back_inside.3.part_ref = bf16[512,4096]{1,0:T(8,128)(2,1)} custom-call(bf16[512,4096]{1,0:T(8,128)(2,1)} %copy-done.1, bf16[512,2048]{1,0:T(8,128)(2,1)} %get-tuple-element.150.scaled_ref.refs_1_, bf16[512,2048]{1,0:T(8,128)(2,1)} %add_convert_fusion.1.grad_ref.refs_2_, f32[512,1]{1,0:T(8,128)} %fusion.48.keep_column_ref.refs_3_, ...), custom_call_target="tpu_custom_call", output_to_operand_aliasing={{}: (12, {})} | custom-call | tf_op jit(solution)/shard_map/back_inside/pallas_call | solution.py:696
  547.0 16.7 %back_later.1 = bf16[512,4096]{1,0:T(8,128)(2,1)} custom-call(bf16[512,4096]{1,0:T(8,128)(2,1)} %copy-done.1, bf16[512,4096]{1,0:T(8,128)(2,1)} %back_inside.3.part_ref, f32[512,1]{1,0:T(8,128)} %fusion.48.keep_column_ref.refs_3_, bf16[16,160,128]{2,1,0:T(8,128)(2,1)} %fusion.20.later_ref, f32[8,2048]{1,0:T(8,128)} %collective-permute-done.14.edge_ref, ...), custom_call_target="tpu_custom_call" | custom-call | tf_op jit(solution)/shard_map/back_later/pallas_call | solution.py:730
  572.6 5.1 all-to-all-start.3
  592.8 15.9 %fusion.8 = (f32[512]{0:T(512)S(1)}, f32[512,1792]{1,0:T(8,128)}) fusion(bf16[512,1792]{1,0:T(8,128)(2,1)S(1)} %bitcast.338, f32[1792]{0:T(1024)} %param.27, f32[512,1792]{1,0:T(8,128)} %fusion.63, bf16[512,4096]{1,0:T(8,128)(2,1)} %back_later.1, bf16[1792,4096]{1,0:T(8,128)(2,1)} %pad_maximum_fusion), kind=kOutput, calls=%fused_computation.18 | convolution fusion | flops 7520779776 | bytes 28058624 | tf_op jit(solution)/shard_map/dot_general | solution.py:378
  608.8 4.9 fusion.7
  627.4 6.8 all-to-all-start.4
  651.9 5.5 all-to-all-done.4
  674.6 9.4 %all-to-all-done.5 = bf16[8,64,896]{2,1,0:T(8,128)(2,1)S(1)} async-done(((bf16[8,64,896]{2,1,0:T(8,128)(2,1)}), bf16[8,64,896]{2,1,0:T(8,128)(2,1)S(1)}, u32[]{:S(2)}, u32[]{:S(2)}) %all-to-all-start.5) | async-done | bytes 917536 | tf_op jit(solution)/shard_map/all_to_all | solution.py:728
  (428 shorter events, 244.6 us)
Async XLA Ops:
  7.2 140.2 %all-gather.6.cloned.1.call-start = ((), (), s32[]{:S(2)}) async-start(), calls=%async_computation.6 | async-start | bytes 6193152 | tf_op jit(solution)/shard_map/all_gather | solution.py:443
  16.7 21.9 %collective-permute-start = (bf16[224,1536]{1,0:T(8,128)(2,1)}, bf16[224,1536]{1,0:T(8,128)(2,1)S(1)}, u32[]{:S(2)}, u32[]{:S(2)}) collective-permute-start(bf16[224,1536]{1,0:T(8,128)(2,1)} %bitcast_dynamic-update-slice_fusion), channel_id=1, source_target_pairs={{1,0},{2,1},{3,2},{0,3},{5,4},{6,5},{7,6},{4,7},{9,8},{10,9},{11,1... | collective-permute-start | bytes 2064392 | tf_op jit(solution)/shard_map/ppermute | solution.py:437
  39.6 114.0 %all-gather.8.cloned.1.call-start = ((), (), s32[]{:S(2)}) async-start(), calls=%async_computation.7 | async-start | bytes 12386304 | tf_op jit(solution)/shard_map/all_gather | solution.py:443
  39.6 43.8 %collective-permute-start.1 = (bf16[224,1536]{1,0:T(8,128)(2,1)}, bf16[224,1536]{1,0:T(8,128)(2,1)S(1)}, u32[]{:S(2)}, u32[]{:S(2)}) collective-permute-start(bf16[224,1536]{1,0:T(8,128)(2,1)} %copy-done.26), channel_id=1, source_target_pairs={{1,0},{2,1},{3,2},{0,3},{5,4},{6,5},{7,6},{4,7},{9,8},{10,9},{11,1... | collective-permute-start | bytes 2064392 | tf_op jit(solution)/shard_map/ppermute | solution.py:437
  42.0 41.4 %collective-permute-start.2 = (bf16[224,1536]{1,0:T(8,128)(2,1)}, bf16[224,1536]{1,0:T(8,128)(2,1)}, u32[]{:S(2)}, u32[]{:S(2)}) collective-permute-start(bf16[224,1536]{1,0:T(8,128)(2,1)} %bitcast_dynamic-update-slice_fusion), channel_id=1, source_target_pairs={{0,1},{1,2},{2,3},{3,0},{4,5},{5,6},{6,7},{7,4},{8,9},{9,10},{10,1... | collective-permute-start | bytes 2064392 | tf_op jit(solution)/shard_map/ppermute | solution.py:440
  42.0 35.9 %collective-permute-start.3 = (bf16[16,5120]{1,0:T(8,128)(2,1)}, bf16[16,5120]{1,0:T(8,128)(2,1)S(1)}, u32[]{:S(2)}, u32[]{:S(2)}) collective-permute-start(bf16[16,5120]{1,0:T(8,128)(2,1)} %concatenate.119), channel_id=1, source_target_pairs={{0,3},{1,0},{2,1},{3,2},{4,7},{5,4},{6,5},{7,6},{8,11},{9,8},{10,9... | collective-permute-start | bytes 491528 | tf_op jit(solution)/shard_map/ppermute | solution.py:477
  45.8 37.6 %collective-permute-start.4 = (bf16[16,5120]{1,0:T(8,128)(2,1)}, bf16[16,5120]{1,0:T(8,128)(2,1)}, u32[]{:S(2)}, u32[]{:S(2)}) collective-permute-start(bf16[16,5120]{1,0:T(8,128)(2,1)} %concatenate.120), channel_id=1, source_target_pairs={{0,2},{1,3},{2,0},{3,1},{4,6},{5,7},{6,4},{7,5},{8,10},{9,11},{10,... | collective-permute-start | bytes 491528 | tf_op jit(solution)/shard_map/ppermute | solution.py:477
  45.8 37.6 %collective-permute-start.5 = (bf16[16,5120]{1,0:T(8,128)(2,1)}, bf16[16,5120]{1,0:T(8,128)(2,1)}, u32[]{:S(2)}, u32[]{:S(2)}) collective-permute-start(bf16[16,5120]{1,0:T(8,128)(2,1)} %concatenate.121), channel_id=1, source_target_pairs={{0,1},{1,2},{2,3},{3,0},{4,5},{5,6},{6,7},{7,4},{8,9},{9,10},{10,1... | collective-permute-start | bytes 491528 | tf_op jit(solution)/shard_map/ppermute | solution.py:477
  86.7 270.2 %all-gather.14.cloned.1.call-start = ((), (), s32[]{:S(2)}) async-start(), calls=%async_computation.10 | async-start | bytes 15482880 | tf_op jit(solution)/shard_map/all_gather | solution.py:443
  86.8 38.7 %collective-permute-start.6 = (bf16[480,1792]{1,0:T(8,128)(2,1)}, bf16[480,1792]{1,0:T(8,128)(2,1)S(1)}, u32[]{:S(2)}, u32[]{:S(2)}) collective-permute-start(bf16[480,1792]{1,0:T(8,128)(2,1)} %maximum_select_fusion), channel_id=1, source_target_pairs={{1,0},{2,1},{3,2},{0,3},{5,4},{6,5},{7,6},{4,7},{9,8},{10,9},{11,1... | collective-permute-start | bytes 5160968 | tf_op jit(solution)/shard_map/ppermute | solution.py:437
  131.3 47.8 %all-to-all-start = ((bf16[8,64,1792]{2,1,0:T(8,128)(2,1)}), bf16[8,64,1792]{2,1,0:T(8,128)(2,1)S(1)}, u32[]{:S(2)}, u32[]{:S(2)}) async-start(bf16[8,64,1792]{2,1,0:T(8,128)(2,1)} %param.23), calls=%async_computation | async-start | bytes 3670016 | tf_op jit(solution)/shard_map/all_to_all | solution.py:446
  136.2 256.8 %all-gather.12.cloned.1.call-start = ((), (), s32[]{:S(2)}) async-start(), calls=%async_computation.9 | async-start | bytes 15482880 | tf_op jit(solution)/shard_map/all_gather | solution.py:443
  179.1 42.3 %collective-permute-start.7 = (bf16[480,1792]{1,0:T(8,128)(2,1)}, bf16[480,1792]{1,0:T(8,128)(2,1)}, u32[]{:S(2)}, u32[]{:S(2)}) collective-permute-start(bf16[480,1792]{1,0:T(8,128)(2,1)} %maximum_select_fusion), channel_id=1, source_target_pairs={{0,1},{1,2},{2,3},{3,0},{4,5},{5,6},{6,7},{7,4},{8,9},{9,10},{10,1... | collective-permute-start | bytes 5160968 | tf_op jit(solution)/shard_map/ppermute | solution.py:440
  224.7 56.3 %all-to-all-start.1 = ((bf16[8,64,1792]{2,1,0:T(8,128)(2,1)}), bf16[8,64,1792]{2,1,0:T(8,128)(2,1)}, u32[]{:S(2)}, u32[]{:S(2)}) async-start(bf16[8,64,1792]{2,1,0:T(8,128)(2,1)} %param.24), calls=%async_computation.1 | async-start | bytes 3670016 | tf_op jit(solution)/shard_map/all_to_all | solution.py:446
  229.1 196.0 %all-gather.10.cloned.1.call-start = ((), (), s32[]{:S(2)}) async-start(), calls=%async_computation.8 | async-start | bytes 15482880 | tf_op jit(solution)/shard_map/all_gather | solution.py:443
  234.1 23.2 %collective-permute-start.9 = (bf16[16,160,128]{2,1,0:T(8,128)(2,1)}, bf16[16,160,128]{2,1,0:T(8,128)(2,1)S(1)}, u32[]{:S(2)}, u32[]{:S(2)}) collective-permute-start(bf16[16,160,128]{2,1,0:T(8,128)(2,1)} %convert_element_type.296), channel_id=1, source_target_pairs={{0,8},{8,0},{16,24},{24,16},{1,9},{9,1},{17,25},{25,17},{2,10},{10... | collective-permute-start | bytes 1966088 | tf_op jit(solution)/shard_map/ppermute | solution.py:531
  259.6 19.3 %collective-permute-start.10 = (bf16[16,160,128]{2,1,0:T(8,128)(2,1)}, bf16[16,160,128]{2,1,0:T(8,128)(2,1)}, u32[]{:S(2)}, u32[]{:S(2)}) collective-permute-start(bf16[16,160,128]{2,1,0:T(8,128)(2,1)} %fusion.17), channel_id=1, source_target_pairs={{0,16},{8,24},{1,17},{9,25},{2,18},{10,26},{3,19},{11,27},{4,20},{... | collective-permute-start | bytes 1966088 | tf_op jit(solution)/shard_map/ppermute | solution.py:531
  281.1 39.1 %collective-permute-start.11 = (bf16[480,1792]{1,0:T(8,128)(2,1)}, bf16[480,1792]{1,0:T(8,128)(2,1)}, u32[]{:S(2)}, u32[]{:S(2)}) collective-permute-start(bf16[480,1792]{1,0:T(8,128)(2,1)} %copy-done.24), channel_id=1, source_target_pairs={{1,0},{2,1},{3,2},{0,3},{5,4},{6,5},{7,6},{4,7},{9,8},{10,9},{11,1... | collective-permute-start | bytes 5160968 | tf_op jit(solution)/shard_map/ppermute | solution.py:437
  490.1 22.8 %collective-permute-start.12 = (bf16[16,160,128]{2,1,0:T(8,128)(2,1)}, bf16[16,160,128]{2,1,0:T(8,128)(2,1)S(1)}, u32[]{:S(2)}, u32[]{:S(2)}) collective-permute-start(bf16[16,160,128]{2,1,0:T(8,128)(2,1)} %convert_element_type.314), channel_id=1, source_target_pairs={{0,8},{8,0},{16,24},{24,16},{1,9},{9,1},{17,25},{25,17},{2,10},{10... | collective-permute-start | bytes 1966088 | tf_op jit(solution)/shard_map/ppermute | solution.py:531
  518.9 44.9 %all-to-all-start.2 = ((bf16[8,64,896]{2,1,0:T(8,128)(2,1)}), bf16[8,64,896]{2,1,0:T(8,128)(2,1)S(1)}, u32[]{:S(2)}, u32[]{:S(2)}) async-start(bf16[8,64,896]{2,1,0:T(8,128)(2,1)} %bitcast.71), calls=%async_computation.2 | async-start | bytes 1835008 | tf_op jit(solution)/shard_map/all_to_all | solution.py:728
  523.8 23.1 %collective-permute-start.14 = (f32[8,2048]{1,0:T(8,128)}, f32[8,2048]{1,0:T(8,128)}, u32[]{:S(2)}, u32[]{:S(2)}) collective-permute-start(f32[8,2048]{1,0:T(8,128)} %get-tuple-element.153), channel_id=1, source_target_pairs={{8,0},{16,8},{24,16},{9,1},{17,9},{25,17},{10,2},{18,10},{26,18},{... | collective-permute-start | bytes 196616 | tf_op jit(solution)/shard_map/ppermute | solution.py:527
  525.2 20.7 %collective-permute-start.13 = (bf16[16,160,128]{2,1,0:T(8,128)(2,1)S(1)}, bf16[16,160,128]{2,1,0:T(8,128)(2,1)S(1)}, u32[]{:S(2)}, u32[]{:S(2)}) collective-permute-start(bf16[16,160,128]{2,1,0:T(8,128)(2,1)S(1)} %fusion.18), channel_id=1, source_target_pairs={{16,0},{24,8},{17,1},{25,9},{18,2},{26,10},{19,3},{27,11},{20,4},{... | collective-permute-start | bytes 1966088 | tf_op jit(solution)/shard_map/ppermute | solution.py:531
  572.6 46.1 %all-to-all-start.3 = ((bf16[8,64,896]{2,1,0:T(8,128)(2,1)}), bf16[8,64,896]{2,1,0:T(8,128)(2,1)}, u32[]{:S(2)}, u32[]{:S(2)}) async-start(bf16[8,64,896]{2,1,0:T(8,128)(2,1)} %bitcast.106), calls=%async_computation.3 | async-start | bytes 1835008 | tf_op jit(solution)/shard_map/all_to_all | solution.py:728
  583.4 32.0 %collective-permute-start.15 = (bf16[16,6912]{1,0:T(8,128)(2,1)}, bf16[16,6912]{1,0:T(8,128)(2,1)}, u32[]{:S(2)}, u32[]{:S(2)}) collective-permute-start(bf16[16,6912]{1,0:T(8,128)(2,1)} %concatenate.144), channel_id=1, source_target_pairs={{0,1},{1,2},{2,3},{3,0},{4,5},{5,6},{6,7},{7,4},{8,9},{9,10},{10,1... | collective-permute-start | bytes 663560 | tf_op jit(solution)/shard_map/ppermute | solution.py:668
  587.3 29.1 %collective-permute-start.16 = (bf16[16,6912]{1,0:T(8,128)(2,1)}, bf16[16,6912]{1,0:T(8,128)(2,1)}, u32[]{:S(2)}, u32[]{:S(2)}) collective-permute-start(bf16[16,6912]{1,0:T(8,128)(2,1)} %concatenate.146), channel_id=1, source_target_pairs={{0,2},{1,3},{2,0},{3,1},{4,6},{5,7},{6,4},{7,5},{8,10},{9,11},{10,... | collective-permute-start | bytes 663560 | tf_op jit(solution)/shard_map/ppermute | solution.py:668
  591.3 25.0 %collective-permute-start.17 = (bf16[16,6912]{1,0:T(8,128)(2,1)}, bf16[16,6912]{1,0:T(8,128)(2,1)}, u32[]{:S(2)}, u32[]{:S(2)}) collective-permute-start(bf16[16,6912]{1,0:T(8,128)(2,1)} %concatenate.148), channel_id=1, source_target_pairs={{0,3},{1,0},{2,1},{3,2},{4,7},{5,4},{6,5},{7,6},{8,11},{9,8},{10,9... | collective-permute-start | bytes 663560 | tf_op jit(solution)/shard_map/ppermute | solution.py:668
  620.7 13.5 %collective-permute-start.18 = (bf16[16,6912]{1,0:T(8,128)(2,1)}, bf16[16,6912]{1,0:T(8,128)(2,1)}, u32[]{:S(2)}, u32[]{:S(2)}) collective-permute-start(bf16[16,6912]{1,0:T(8,128)(2,1)} %get-tuple-element.189), channel_id=1, source_target_pairs={{0,8},{8,0},{16,24},{24,16},{1,9},{9,1},{17,25},{25,17},{2,10},{10... | collective-permute-start | bytes 663560 | tf_op jit(solution)/shard_map/ppermute | solution.py:531
  623.3 12.0 %collective-permute-start.19 = (bf16[16,6912]{1,0:T(8,128)(2,1)}, bf16[16,6912]{1,0:T(8,128)(2,1)}, u32[]{:S(2)}, u32[]{:S(2)}) collective-permute-start(bf16[16,6912]{1,0:T(8,128)(2,1)} %get-tuple-element.191), channel_id=1, source_target_pairs={{0,16},{8,24},{16,0},{24,8},{1,17},{9,25},{17,1},{25,9},{2,18},{10... | collective-permute-start | bytes 663560 | tf_op jit(solution)/shard_map/ppermute | solution.py:531
  627.4 30.0 %all-to-all-start.4 = ((bf16[8,64,896]{2,1,0:T(8,128)(2,1)}), bf16[8,64,896]{2,1,0:T(8,128)(2,1)S(1)}, u32[]{:S(2)}, u32[]{:S(2)}) async-start(bf16[8,64,896]{2,1,0:T(8,128)(2,1)} %bitcast.107), calls=%async_computation.4 | async-start | bytes 1835008 | tf_op jit(solution)/shard_map/all_to_all | solution.py:728
  638.9 11.5 %collective-permute-start.22 = (bf16[16,6912]{1,0:T(8,128)(2,1)S(1)}, bf16[16,6912]{1,0:T(8,128)(2,1)S(1)}, u32[]{:S(2)}, u32[]{:S(2)}) collective-permute-start(bf16[16,6912]{1,0:T(8,128)(2,1)S(1)} %get-tuple-element.179), channel_id=1, source_target_pairs={{0,16},{8,24},{16,0},{24,8},{1,17},{9,25},{17,1},{25,9},{2,18},{10... | collective-permute-start | bytes 663560 | tf_op jit(solution)/shard_map/ppermute | solution.py:531
  650.4 12.2 %collective-permute-start.24 = (bf16[64,6912]{1,0:T(8,128)(2,1)S(1)}, bf16[64,6912]{1,0:T(8,128)(2,1)}, u32[]{:S(2)}, u32[]{:S(2)}) collective-permute-start(bf16[64,6912]{1,0:T(8,128)(2,1)S(1)} %pad_maximum_fusion.5), channel_id=1, source_target_pairs={{0,4},{4,0},{1,5},{5,1},{2,6},{6,2},{3,7},{7,3},{8,12},{12,8},{9,1... | collective-permute-start | bytes 2654216 | tf_op jit(solution)/shard_map/ppermute | solution.py:682
  657.4 26.7 %all-to-all-start.5 = ((bf16[8,64,896]{2,1,0:T(8,128)(2,1)}), bf16[8,64,896]{2,1,0:T(8,128)(2,1)S(1)}, u32[]{:S(2)}, u32[]{:S(2)}) async-start(bf16[8,64,896]{2,1,0:T(8,128)(2,1)} %bitcast.108), calls=%async_computation.5 | async-start | bytes 1835008 | tf_op jit(solution)/shard_map/all_to_all | solution.py:728
  (79 other events, 1450.1 us)
Sparse Core Ops, SparseCore 0:
  39.7 42.0 all-gather.5
  86.8 66.6 all-gather.7
  155.4 77.7 all-gather.13
  235.0 82.6 all-gather.11
  320.3 78.7 all-gather.9
